TPU v7x, 32 devices: a whole 2x2x4 slice. The times are simulated.
32 devices in a mesh: groups: 2 (over y), frame: 4 (over z), patch: 2 (over x), head: 2 (over core).
Axes of the slice: x: 2, y: 2, z: 4, core: 2. Of those that a mesh axis runs over, the one named last changes fastest.
Arguments:
- video: bfloat16 [16, 8, 1152], P(('groups', 'frame'), 'patch'), parts along dimension 0, may hold values from -1.5 to 1.5
- gain_time: float32 [1152], replicated, may hold values from 0.1 to 1.9
- qkv_time: bfloat16 [1152, 3, 1152], P('frame', None, 'head'), may hold values from -0.5343196 to 0.5343196
- out_time: bfloat16 [1152, 1152], P('frame', 'head'), may hold values from -0.1875 to 0.1875
- gain_space: float32 [1152], replicated, may hold values from 0.1 to 1.9
- qkv_space: bfloat16 [1152, 3, 1152], P('frame', None, 'head'), may hold values from -0.5343196 to 0.5343196
- out_space: bfloat16 [1152, 1152], P('frame', 'head'), may hold values from -0.1875 to 0.1875
Outputs:
- result: float32 [16, 8, 1152], P(('groups', 'frame', 'patch')), parts along dimension 0
There are 2 independent parts, one for each index of `groups`. A program takes and returns all parts, laid end to end along the dimension named above; an argument that names none is the same for every part. Nothing has to cross between parts.
All inputs are finite; a program needn't handle non-finite values.
Results may differ from a plain program's by a relative error of at most 0.04.
Values may be sent and summed in bfloat16 or wider, within the bound.
No kernel may reach another device: no remote copies, remote signals or barrier semaphores. Data moves between devices by JAX's collectives and lax.ppermute only.
A program may use at most 64 MiB of HBM per device.

v0:
```python
import jax
import jax.numpy as jnp
from jax import lax
from jax.sharding import PartitionSpec as P

HEAD_WIDTH = 72


def layer_norm(tokens, gain):
    value_rows = tokens.astype(jnp.float32)
    center = jnp.mean(value_rows, axis=-1, keepdims=True)
    spread = jnp.mean((value_rows - center) ** 2, axis=-1, keepdims=True)
    return ((value_rows - center) * lax.rsqrt(spread + 1e-06) * gain).astype(jnp.bfloat16)


def project_qkv(normed, weight):
    columns = weight.shape[1] * weight.shape[2]
    total = jnp.dot(
        normed, weight.reshape(weight.shape[0], columns), preferred_element_type=jnp.float32
    )
    return total.astype(jnp.bfloat16)


def project_out(attended, weight):
    return lax.dot_general(
        attended, weight, (((1,), (1,)), ((), ())), preferred_element_type=jnp.float32
    )


def attend(qkv, over_first):
    query_rows, key_rows, value_rows = (qkv[:, :, 0], qkv[:, :, 1], qkv[:, :, 2])
    factor = 1.0 / jnp.sqrt(jnp.float32(HEAD_WIDTH))
    if over_first:
        score_matrix = (
            jnp.einsum("abhd,cbhd->bhac", query_rows, key_rows, preferred_element_type=jnp.float32)
            * factor
        )
        attention_weights = jax.nn.softmax(score_matrix, axis=-1).astype(jnp.bfloat16)
        attention_output = jnp.einsum(
            "bhac,cbhd->abhd", attention_weights, value_rows, preferred_element_type=jnp.float32
        )
    else:
        score_matrix = (
            jnp.einsum("abhd,achd->ahbc", query_rows, key_rows, preferred_element_type=jnp.float32)
            * factor
        )
        attention_weights = jax.nn.softmax(score_matrix, axis=-1).astype(jnp.bfloat16)
        attention_output = jnp.einsum(
            "ahbc,achd->abhd", attention_weights, value_rows, preferred_element_type=jnp.float32
        )
    return attention_output.astype(jnp.bfloat16)


def mix_partial(tokens, gain, qkv_weight, out_weight, over_first):
    rows_a, rows_b, width = tokens.shape
    flat = tokens.reshape(rows_a * rows_b, width)
    normed = layer_norm(flat, gain)
    qkv = project_qkv(normed, qkv_weight).reshape(rows_a, rows_b, 3, -1, HEAD_WIDTH)
    attended = attend(qkv, over_first).reshape(rows_a * rows_b, -1)
    partial_value = project_out(attended, out_weight)
    rounded = lax.optimization_barrier(partial_value.astype(jnp.bfloat16)).astype(jnp.float32)
    return (flat, rounded)


def on_device(video, gain_time, qkv_time, out_time, gain_space, qkv_space, out_space):
    frame_size = lax.axis_size("frame")
    patch_size = lax.axis_size("patch")
    device_count = frame_size * patch_size
    series = lax.all_to_all(video, "frame", split_axis=1, concat_axis=0, tiled=True)
    qkv_time, out_time, qkv_space, out_space = (
        lax.all_gather(qkv_time, "frame", axis=0, tiled=True),
        lax.all_gather(out_time, "frame", axis=0, tiled=True),
        lax.all_gather(qkv_space, "frame", axis=0, tiled=True),
        lax.all_gather(out_space, "frame", axis=0, tiled=True),
    )
    frame_count, series_count, width = series.shape
    set_count = frame_count // device_count
    flat, rounded = mix_partial(series, gain_time, qkv_time, out_time, True)
    summed = (
        lax.psum(rounded.astype(jnp.bfloat16), "head")
        .astype(jnp.float32)
        .reshape(device_count, set_count, series_count, width)
    )
    resident = flat.reshape(device_count, set_count, series_count, width)
    after_time = (resident.astype(jnp.float32) + summed).astype(jnp.bfloat16)
    arrived = lax.all_to_all(
        after_time, ("frame", "patch"), split_axis=0, concat_axis=2, tiled=True
    )
    whole_frames = arrived.reshape(set_count, device_count * series_count, width)
    whole_frames = whole_frames.reshape(set_count, frame_size, patch_size, series_count, width)
    whole_frames = jnp.transpose(whole_frames, (0, 2, 1, 3, 4)).reshape(
        set_count, device_count * series_count, width
    )
    flat_space, rounded_space = mix_partial(whole_frames, gain_space, qkv_space, out_space, False)
    summed_space = lax.psum(rounded_space.astype(jnp.bfloat16), "head").astype(jnp.float32)
    result = flat_space.astype(jnp.float32) + summed_space
    return result.reshape(whole_frames.shape)


def solution(mesh):
    placed = (
        P(("groups", "frame"), "patch", None),
        P(),
        P("frame", None, "head"),
        P("frame", "head"),
        P(),
        P("frame", None, "head"),
        P("frame", "head"),
    )
    return jax.shard_map(
        on_device,
        mesh=mesh,
        in_specs=placed,
        out_specs=P(("groups", "frame", "patch"), None, None),
        check_vma=False,
    )
```

profile of v0, /device:TPU:0, one launch (start us, length us, event | category | flops | bytes accessed | tf_op | source)
XLA Modules:
  0.0 264.7 jit_solution(1438901559891736711)
XLA Ops:
  6.5 0.0 all-gather.5.cloned.1.call-start
  6.5 0.7 all-gather.5.cloned.1.call-update
  7.3 0.0 all-gather.7.cloned.1.call-start
  7.3 0.7 all-gather.7.cloned.1.call-update
  8.0 0.0 all-gather.9.cloned.1.call-start
  8.1 0.7 all-gather.9.cloned.1.call-update
  8.7 0.7 copy.33
  9.5 11.8 %all_to_all.8 = bf16[2,4,1152]{2,0,1:T(2,128)(2,1)S(1)} all-to-all(bf16[2,4,1152]{2,0,1:T(2,128)(2,1)S(1)} %copy.33), channel_id=1, replica_groups=mesh['groups'=2,'frame'=4,'patch'=2,'head'=2] {'frame'}, dimensions={1} | all-to-all | bytes 36864 | tf_op jit(solution)/shard_map/all_to_all | solution.py:69
  21.2 0.1 fusion.8
  21.4 0.2 multiply_reduce_fusion.1
  21.5 0.8 multiply_convert_fusion.1
  22.4 73.8 %all-gather.5.cloned.1.call-done = bf16[1152,3,576]{2,0,1:T(8,128)(2,1)} async-done(((bf16[288,3,576]{2,0,1:T(8,128)(2,1)}), bf16[1152,3,576]{2,0,1:T(8,128)(2,1)}) %all-gather.5.cloned.1.call-update) | async-done | bytes 3981328 | tf_op jit(solution)/shard_map/all_gather | solution.py:71
  96.2 6.6 %copy.34 = bf16[1152,3,576]{0,2,1:T(8,128)(2,1)} copy(bf16[1152,3,576]{2,0,1:T(8,128)(2,1)} %all-gather.5.cloned.1.call-done) | data formatting | bytes 7962624 | tf_op jit(solution)/shard_map/all_gather | solution.py:71
  102.8 3.4 %convolution_convert_fusion.3 = bf16[8,1728]{1,0:T(8,128)(2,1)S(1)} fusion(bf16[8,1152]{1,0:T(8,128)(2,1)S(1)} %convert_element_type.113, bf16[1152,1728]{0,1:T(8,128)(2,1)} %bitcast.105), kind=kOutput, calls=%fused_computation.5 | convolution fusion | flops 31864320 | bytes 4027392 | tf_op jit(solution)/shard_map/dot_general | solution.py:18
  106.2 0.2 reshape.202
  106.4 0.2 fusion.19
  106.5 0.2 fusion.6
  106.7 0.1 reshape.206
  106.8 24.7 %all-gather.7.cloned.1.call-done = bf16[1152,576]{1,0:T(8,128)(2,1)} async-done(((bf16[288,576]{1,0:T(8,128)(2,1)}), bf16[1152,576]{1,0:T(8,128)(2,1)}) %all-gather.7.cloned.1.call-update) | async-done | bytes 1327120 | tf_op jit(solution)/shard_map/all_gather | solution.py:72
  131.6 1.9 convolution_convert_fusion.2
  133.4 3.4 %psum.14 = bf16[8,1152]{1,0:T(8,128)(2,1)S(1)} all-reduce(bf16[8,1152]{1,0:T(8,128)(2,1)S(1)} %convolution_convert_fusion.2), channel_id=1, replica_groups=mesh['groups'=2,'frame'=4,'patch'=2,'head'=2] {'head'}, use_global_device_ids=true, to_apply=%region_4.0 | all-reduce | flops 9216 | bytes 36864 | tf_op jit(solution)/shard_map/psum | solution.py:80
  136.9 0.5 broadcast.115
  137.4 0.7 reduce.12
  138.0 0.7 reshape.220
  138.8 3.6 %all-to-all-start.1 = ((bf16[8,2,576]{2,1,0:T(2,128)(2,1)}), bf16[8,2,576]{2,1,0:T(2,128)(2,1)S(1)}, u32[]{:S(2)}, u32[]{:S(2)}) async-start(bf16[8,2,576]{2,1,0:T(2,128)(2,1)} %reshape.220), calls=%async_computation.1 | async-start | bytes 40960 | tf_op jit(solution)/shard_map/all_to_all | solution.py:86
  142.3 0.0 all-gather.11.cloned.1.call-start
  142.4 0.5 all-gather.11.cloned.1.call-update
  142.9 0.0 copy-start
  142.9 74.2 %all-gather.9.cloned.1.call-done = bf16[1152,3,576]{2,0,1:T(8,128)(2,1)} async-done(((bf16[288,3,576]{2,0,1:T(8,128)(2,1)}), bf16[1152,3,576]{2,0,1:T(8,128)(2,1)}) %all-gather.9.cloned.1.call-update) | async-done | bytes 3981328 | tf_op jit(solution)/shard_map/all_gather | solution.py:73
  217.1 6.6 %copy.42 = bf16[1152,3,576]{0,2,1:T(8,128)(2,1)} copy(bf16[1152,3,576]{2,0,1:T(8,128)(2,1)} %all-gather.9.cloned.1.call-done) | data formatting | bytes 7962624 | tf_op jit(solution)/shard_map/all_gather | solution.py:73
  223.6 0.0 all-to-all-done.1
  223.6 0.1 reshape.221
  223.8 0.1 fusion.16
  223.9 0.2 multiply_reduce_fusion
  224.1 0.0 copy-done
  224.1 0.1 multiply_convert_fusion
  224.2 3.4 %convolution_convert_fusion.1 = bf16[8,1728]{1,0:T(8,128)(2,1)S(1)} fusion(bf16[8,1152]{1,0:T(8,128)(2,1)S(1)} %convert_element_type.129, bf16[1152,1728]{0,1:T(8,128)(2,1)} %bitcast.104), kind=kOutput, calls=%fused_computation.3 | convolution fusion | flops 31864320 | bytes 4027392 | tf_op jit(solution)/shard_map/dot_general | solution.py:18
  227.6 0.2 reshape.208
  227.8 0.2 fusion.20
  227.9 0.2 fusion.7
  228.1 0.1 reshape.212
  228.2 24.0 %all-gather.11.cloned.1.call-done = bf16[1152,576]{1,0:T(8,128)(2,1)} async-done(((bf16[288,576]{1,0:T(8,128)(2,1)}), bf16[1152,576]{1,0:T(8,128)(2,1)}) %all-gather.11.cloned.1.call-update) | async-done | bytes 1327120 | tf_op jit(solution)/shard_map/all_gather | solution.py:74
  252.2 1.9 convolution_convert_fusion
  254.1 3.4 %psum.15 = bf16[8,1152]{1,0:T(8,128)(2,1)S(1)} all-reduce(bf16[8,1152]{1,0:T(8,128)(2,1)S(1)} %convolution_convert_fusion), channel_id=1, replica_groups=mesh['groups'=2,'frame'=4,'patch'=2,'head'=2] {'head'}, use_global_device_ids=true, to_apply=%region_9.0 | all-reduce | flops 9216 | bytes 36864 | tf_op jit(solution)/shard_map/psum | solution.py:95
  257.5 0.6 add_bitcast_fusion
  (16 shorter events, 0.2 us)
Async XLA Ops:
  6.5 89.6 %all-gather.5.cloned.1.call-start = ((), (), s32[]{:S(2)}) async-start(), calls=%async_computation.2 | async-start | bytes 5529600 | tf_op jit(solution)/shard_map/all_gather | solution.py:71
  7.3 124.3 %all-gather.7.cloned.1.call-start = ((), (), s32[]{:S(2)}) async-start(), calls=%async_computation.3 | async-start | bytes 1843200 | tf_op jit(solution)/shard_map/all_gather | solution.py:72
  8.0 209.0 %all-gather.9.cloned.1.call-start = ((), (), s32[]{:S(2)}) async-start(), calls=%async_computation.4 | async-start | bytes 5529600 | tf_op jit(solution)/shard_map/all_gather | solution.py:73
  138.8 84.9 %all-to-all-start.1 = ((bf16[8,2,576]{2,1,0:T(2,128)(2,1)}), bf16[8,2,576]{2,1,0:T(2,128)(2,1)S(1)}, u32[]{:S(2)}, u32[]{:S(2)}) async-start(bf16[8,2,576]{2,1,0:T(2,128)(2,1)} %reshape.220), calls=%async_computation.1 | async-start | bytes 40960 | tf_op jit(solution)/shard_map/all_to_all | solution.py:86
  142.3 109.9 %all-gather.11.cloned.1.call-start = ((), (), s32[]{:S(2)}) async-start(), calls=%async_computation.5 | async-start | bytes 1843200 | tf_op jit(solution)/shard_map/all_gather | solution.py:74
  142.9 81.2 %copy-start = (f32[1152]{0:T(1024)S(1)}, f32[1152]{0:T(1024)}, u32[]{:S(2)}) copy-start(f32[1152]{0:T(1024)} %param.11) | copy-start | bytes 13828
Sparse Core Ops, SparseCore 0:
  8.9 87.2 all-gather.4
  97.7 33.7 all-gather.6
  133.1 83.8 all-gather.8
  218.5 33.6 all-gather.10
where the time goes:
time: 265 us
  waiting for transfers between devices  199 us (75%)
  blocking collectives  18.6 us (7%)
  local copies, waits for them, and re-layouts  15.8 us (6%)
  between operations  13.3 us (5%)
  matrix products  11.3 us (4%)
  starting transfers between devices  3.67 us (1%)
  other arithmetic  2.79 us (1%)
    all_gather x1, waiting for transfers between devices, on_device(): lax.all_gather(qkv_space, 'frame', axis=0, tiled=True)  74.2 us
    all_gather x1, waiting for transfers between devices, on_device(): lax.all_gather(qkv_time, 'frame', axis=0, tiled=True)  73.8 us
    all_gather x1, waiting for transfers between devices, on_device(): lax.all_gather(out_time, 'frame', axis=0, tiled=True)  24.7 us
    all_gather x1, waiting for transfers between devices, on_device(): lax.all_gather(out_space, 'frame', axis=0, tiled=True)  24 us
    all_to_all x1, blocking collectives, on_device(): lax.all_to_all(video, 'frame', split_axis=1, concat_axis=0, tiled=True)  11.8 us
    dot_general x2, matrix products, project_qkv(): jnp.dot(normed, weight.reshape(weight.shape[0], columns), preferred_eleme...  6.83 us
    all_gather x1, local copies, waits for them, and re-layouts, on_device(): lax.all_gather(qkv_time, 'frame', axis=0, tiled=True)  6.59 us
    all_gather x1, local copies, waits for them, and re-layouts, on_device(): lax.all_gather(qkv_space, 'frame', axis=0, tiled=True)  6.58 us
  transfers between devices with their start and end apart: 5, of which 4 were waited for; matrix products, arithmetic and copies ran while one was open for 10% of the time, Pallas kernels for 0%

commit v1 on v0

--- a/solution.py
+++ b/solution.py
@@ -1,6 +1,10 @@
+import functools
+
 import jax
 import jax.numpy as jnp
 from jax import lax
+from jax.experimental import pallas as pl
+from jax.experimental.pallas import tpu as pltpu
 from jax.sharding import PartitionSpec as P
 
 HEAD_WIDTH = 72
@@ -97,6 +101,359 @@
     return result.reshape(whole_frames.shape)
 
 
+F32 = jnp.float32
+BF16 = jnp.bfloat16
+KINDS = 3
+NT = (((1,), (1,)), ((), ()))
+
+
+def run(body, outs, *args, scratch=()):
+    vmem = pl.BlockSpec(memory_space=pltpu.VMEM)
+    single = not isinstance(outs, list)
+    shapes = [jax.ShapeDtypeStruct(*o) for o in ([outs] if single else outs)]
+    found = pl.pallas_call(
+        body,
+        out_shape=shapes,
+        in_specs=[vmem] * len(args),
+        out_specs=[vmem] * len(shapes),
+        scratch_shapes=[pltpu.VMEM(*s) for s in scratch],
+    )(*args)
+    return found[0] if single else found
+
+
+def lanes(value, start, size):
+    return lax.slice_in_dim(value, start, start + size, axis=1)
+
+
+def exchange(messages):
+    count = len(messages)
+    return [messages[0]] + [
+        lax.ppermute(messages[k], "frame", [(i, i ^ k) for i in range(count)])
+        for k in range(1, count)
+    ]
+
+
+def pick_rows(value, source):
+    column = lax.broadcasted_iota(jnp.int32, (source.shape[0], value.shape[0]), 1)
+    chosen = jnp.where(column == source, 1.0, 0.0).astype(BF16)
+    return jnp.dot(chosen, value.astype(BF16), preferred_element_type=F32)
+
+
+def split_body(count, video_ref, gain_ref, *refs):
+    outs, held = refs[:count], refs[count]
+    f = lax.axis_index("frame")
+    rows = video_ref.shape[0] * video_ref.shape[1]
+    share = held.shape[2]
+    x = jnp.concatenate([video_ref[i].astype(F32) for i in range(video_ref.shape[0])], axis=0)
+    mean = jnp.mean(x, axis=-1, keepdims=True)
+    centred = x - mean
+    spread = jnp.mean(centred * centred, axis=-1, keepdims=True)
+    y = centred * lax.rsqrt(spread + 1e-06) * gain_ref[...]
+    for s in range(count):
+        held[s, 0:rows] = lanes(y, s * share, share)
+        held[s, rows:] = lanes(x, s * share, share)
+    for k in range(count):
+        outs[k][...] = held[f ^ k].astype(BF16)
+
+
+def project_body(count, *refs):
+    parts, weight_ref, outs = refs[:count], refs[count], refs[count + 1 : 2 * count + 1]
+    tokens, total = refs[2 * count + 1 :]
+    f = lax.axis_index("frame")
+    rows = tokens.shape[0] // count
+    for k in range(count):
+        place = pl.multiple_of((f ^ k) * rows, rows)
+        tokens[pl.ds(place, rows), :] = parts[k][0:rows].astype(F32)
+    row = lax.broadcasted_iota(jnp.int32, (tokens.shape[0], 1), 0)
+    source = lax.rem(row, rows) * count + lax.div(row, rows)
+    x = pick_rows(tokens[...], source).astype(BF16)
+    for t in range(KINDS):
+        total[t] = jnp.dot(x, weight_ref[t], preferred_element_type=F32)
+    for k in range(count):
+        place = pl.multiple_of((f ^ k) * rows, rows)
+        for t in range(KINDS):
+            outs[k][t] = total.at[t][pl.ds(place, rows), :].astype(BF16)
+
+
+def prepare_body(count, *refs):
+    parts, gain_ref, weight_ref = refs[:count], refs[count], refs[count + 1]
+    fixed_ref, gain_own, raw_own, raw_other, gains, raw = refs[count + 2 :]
+    f, p = lax.axis_index("frame"), lax.axis_index("patch")
+    share = gains.shape[2]
+    for s in range(count):
+        gains[s] = jnp.broadcast_to(lanes(gain_ref[...], s * share, share), gains.shape[1:])
+    g = gains[f]
+    gain_own[...] = g
+    g = g.astype(BF16)
+    rows = [jnp.dot(g, weight_ref[t], preferred_element_type=F32) for t in range(KINDS)]
+    row = lax.broadcasted_iota(jnp.int32, rows[0].shape, 0)
+    fixed_ref[...] = jnp.where(row == 0, rows[0], jnp.where(row == 1, rows[1], rows[2]))
+    whole = parts[0].shape[0] // 2
+    places = whole // 2
+    for k in range(count):
+        raw[f ^ k] = parts[k][whole:].astype(F32)
+    even, odd = (
+        jnp.concatenate([raw[s][at : at + places] for s in range(count)], axis=0)
+        for at in (0, places)
+    )
+    raw_own[...] = jnp.where(p == 0, even, odd).astype(BF16)
+    raw_other[...] = jnp.where(p == 0, odd, even).astype(BF16)
+
+
+def attend_rows(query, key, value):
+    rows, width = query.shape
+    heads = width // HEAD_WIDTH
+    spread = heads * rows
+    first = lax.broadcasted_iota(jnp.int32, (heads, rows, width), 0) * HEAD_WIDTH
+    first = first.reshape(spread, width)
+    lane = lax.broadcasted_iota(jnp.int32, (spread, width), 1)
+    mine = (lane >= first) & (lane < first + HEAD_WIDTH)
+    keys = jnp.where(mine, jnp.concatenate([key] * heads, axis=0), 0.0).astype(BF16)
+    values = jnp.where(mine, jnp.concatenate([value] * heads, axis=0), 0.0).astype(BF16)
+    scores = lax.dot_general(keys, query.astype(BF16), NT, preferred_element_type=F32)
+    scores = (scores * (1.0 / HEAD_WIDTH**0.5)).reshape(heads, rows, rows)
+    power = jnp.exp(scores - jnp.max(scores, axis=1, keepdims=True))
+    weights = power / jnp.sum(power, axis=1, keepdims=True)
+    weights = weights.reshape(spread, rows).T.astype(BF16)
+    return jnp.dot(weights, values, preferred_element_type=F32)
+
+
+def attend_time_body(count, *refs):
+    parts, fixed_ref, out_ref = refs[:count], refs[count], refs[count + 1]
+    qkv = []
+    for t in range(KINDS):
+        total = parts[0][t].astype(F32)
+        for k in range(1, count):
+            total = total + parts[k][t].astype(F32)
+        qkv.append(total.astype(BF16).astype(F32))
+    attended = attend_rows(*qkv)
+    out_ref[...] = jnp.concatenate([attended, fixed_ref[...]], axis=0).astype(BF16)
+
+
+def out_time_body(count, *refs):
+    parts, weight_ref, raw_other = refs[:count], refs[count], refs[count + 1]
+    own_ref, other_ref, tokens = refs[count + 2 :]
+    f, p = lax.axis_index("frame"), lax.axis_index("patch")
+    rows = tokens.shape[0] // count
+    for k in range(count):
+        place = pl.multiple_of((f ^ k) * rows, rows)
+        tokens[pl.ds(place, rows), :] = parts[k][0:rows].astype(F32)
+    half = tokens.shape[0] // 2
+    row = lax.broadcasted_iota(jnp.int32, (tokens.shape[0], 1), 0)
+    parity = jnp.where(row < half, p, 1 - p)
+    row = lax.rem(row, half)
+    source = lax.rem(row, count) * rows + 2 * lax.div(row, count) + parity
+    x = pick_rows(tokens[...], source).astype(BF16)
+    total = lax.dot_general(x, weight_ref[...], NT, preferred_element_type=F32)
+    own_ref[...] = total[0:half].astype(BF16)
+    other_ref[0:half] = total[half:].astype(BF16)
+    other_ref[half:] = raw_other[...]
+
+
+def in_three(value):
+    high = value.astype(BF16).astype(F32)
+    middle = (value - high).astype(BF16).astype(F32)
+    return high, middle, value - high - middle
+
+
+def project_space_body(count, *refs):
+    own, own_head, cross, cross_head, raw_own, gain_ref, weight_ref = refs[:7]
+    outs, after_ref, total = refs[7 : 7 + count], *refs[7 + count :]
+    f, p = lax.axis_index("frame"), lax.axis_index("patch")
+    half = own.shape[0]
+    summed = own[...].astype(F32) + own_head[...].astype(F32)
+    first = raw_own[...].astype(F32) + summed
+    summed = cross[0:half].astype(F32) + cross_head[0:half].astype(F32)
+    second = cross[half:].astype(F32) + summed
+    low, high = jnp.where(p == 0, first, second), jnp.where(p == 0, second, first)
+    places = half // count
+    pieces = [v[i : i + places] for i in range(0, half, places) for v in (low, high)]
+    after_ref[...] = jnp.concatenate(pieces, axis=0).astype(BF16)
+    x = after_ref[...].astype(F32)
+    mean = jnp.mean(x, axis=-1, keepdims=True)
+    centred = x - mean
+    square = jnp.sum(centred * centred, axis=-1, keepdims=True)
+    y = (centred * gain_ref[0:1]).astype(BF16)
+    width = weight_ref.shape[2]
+    last = width // 128 * 128
+    for t in range(KINDS):
+        total[t, :, 0:width] = jnp.dot(y, weight_ref[t], preferred_element_type=F32)
+        tail = total[t, :, last:]
+        lane = lax.broadcasted_iota(jnp.int32, tail.shape, 1) - (width - last)
+        tail = jnp.where(lane < 0, tail, 0.0)
+        if t == 0:
+            for at, item in enumerate((*in_three(mean), *in_three(square))):
+                tail = jnp.where(lane == at, item, tail)
+        total[t, :, last:] = tail
+    rows = total.shape[1] // count
+    for k in range(count):
+        place = pl.multiple_of((f ^ k) * rows, rows)
+        for t in range(KINDS):
+            outs[k][t] = total.at[t][pl.ds(place, rows), :].astype(BF16)
+
+
+def attend_space_body(count, share, *refs):
+    parts, fixed, out_ref = refs[:count], refs[count : 2 * count], refs[2 * count]
+    rows, width = out_ref.shape
+    last = width // 128 * 128
+    means, squares = [], []
+    for k in range(count):
+        tail = parts[k][0].astype(F32)[:, last:]
+        lane = lax.broadcasted_iota(jnp.int32, tail.shape, 1) - (width - last)
+        means.append(
+            jnp.sum(jnp.where((lane >= 0) & (lane < 3), tail, 0.0), axis=-1, keepdims=True)
+        )
+        squares.append(
+            jnp.sum(jnp.where((lane >= 3) & (lane < 6), tail, 0.0), axis=-1, keepdims=True)
+        )
+    mean = sum(means) / count
+    square = sum(squares) + share * sum((m - mean) * (m - mean) for m in means)
+    scale = lax.rsqrt(square / (share * count) + 1e-06)
+    qkv = []
+    for t in range(KINDS):
+        total = jnp.zeros((rows, width), F32)
+        for k in range(count):
+            row = fixed[k][...].astype(F32)[rows + t : rows + t + 1]
+            total = total + parts[k][t].astype(F32)[:, 0:width] + (means[k] - mean) * row
+        qkv.append((total * scale).astype(BF16).astype(F32))
+    out_ref[...] = attend_rows(*qkv).astype(BF16)
+
+
+def out_space_body(count, *refs):
+    parts, weight_ref, after_ref = refs[:count], refs[count], refs[count + 1]
+    outs, (tokens, total, after) = refs[count + 2 : 2 * count + 2], refs[2 * count + 2 :]
+    f = lax.axis_index("frame")
+    rows = tokens.shape[0] // count
+    for k in range(count):
+        place = pl.multiple_of((f ^ k) * rows, rows)
+        tokens[pl.ds(place, rows), :] = parts[k][...].astype(F32)
+    total[...] = lax.dot_general(
+        tokens[...].astype(BF16), weight_ref[...], NT, preferred_element_type=F32
+    )
+    after[...] = after_ref[...].astype(F32)
+    for k in range(count):
+        place = pl.multiple_of((f ^ k) * rows, rows)
+        value = jnp.concatenate(
+            [total[pl.ds(place, rows), :], after[pl.ds(place, rows), :]], axis=0
+        )
+        outs[k][...] = value.astype(BF16)
+
+
+def join_body(count, *refs):
+    parts, partial_ref, after_ref, held = refs[:count], *refs[count:]
+    f = lax.axis_index("frame")
+    rows = partial_ref.shape[0]
+    for k in range(count):
+        held[f ^ k] = parts[k][...].astype(F32)
+    whole = jnp.concatenate([held[s] for s in range(count)], axis=1)
+    partial_ref[...] = whole[0:rows].astype(BF16)
+    after_ref[...] = whole[rows:].astype(BF16)
+
+
+def finish_body(own, other, after, out_ref):
+    out_ref[0] = after[...].astype(F32) + (own[...].astype(F32) + other[...].astype(F32))
+
+
+def moving_tokens(video, gain_time, qkv_time, out_time, gain_space, qkv_space, out_space):
+    count = lax.axis_size("frame")
+    frames_here, patches_here, width = video.shape
+    share, columns = out_time.shape
+    rows = frames_here * patches_here
+    plane = rows * count
+    padded = (columns // 128 + 1) * 128
+    qkv_time, qkv_space = (jnp.transpose(w, (1, 0, 2)) for w in (qkv_time, qkv_space))
+    gain_time, gain_space = gain_time.reshape(1, width), gain_space.reshape(1, width)
+    body = functools.partial
+    swap = [(0, 1), (1, 0)]
+
+    normed = exchange(
+        run(
+            body(split_body, count),
+            [((2 * rows, share), BF16)] * count,
+            video,
+            gain_time,
+            scratch=[((count, 2 * rows, share), F32)],
+        )
+    )
+    partial_time = exchange(
+        run(
+            body(project_body, count),
+            [((KINDS, rows, columns), BF16)] * count,
+            *normed,
+            qkv_time,
+            scratch=[((plane, share), F32), ((KINDS, plane, columns), F32)],
+        )
+    )
+    fixed, gain_own, raw_own, raw_other = run(
+        body(prepare_body, count),
+        [
+            ((8, columns), F32),
+            ((8, share), F32),
+            ((plane // 2, share), BF16),
+            ((plane // 2, share), BF16),
+        ],
+        *normed,
+        gain_space,
+        qkv_space,
+        scratch=[((count, 8, share), F32), ((count, rows, share), F32)],
+    )
+    attended = run(
+        body(attend_time_body, count), ((rows + 8, columns), BF16), *partial_time, fixed
+    )
+    attended = exchange([attended] * count)
+    own, cross = run(
+        body(out_time_body, count),
+        [((plane // 2, share), BF16), ((plane, share), BF16)],
+        *attended,
+        out_time,
+        raw_other,
+        scratch=[((plane, columns), F32)],
+    )
+    own_head = lax.ppermute(own, "head", swap)
+    crossed = lax.ppermute(cross, "patch", swap)
+    cross_head = lax.ppermute(
+        cross[: plane // 2], ("patch", "head"), [(i, 3 - i) for i in range(4)]
+    )
+    *partial_space, after = run(
+        body(project_space_body, count),
+        [((KINDS, rows, padded), BF16)] * count + [((plane, share), BF16)],
+        own,
+        own_head,
+        crossed,
+        cross_head,
+        raw_own,
+        gain_own,
+        qkv_space,
+        scratch=[((KINDS, plane, padded), F32)],
+    )
+    partial_space = exchange(partial_space)
+    frame = run(
+        body(attend_space_body, count, share),
+        ((rows, columns), BF16),
+        *partial_space,
+        *attended,
+    )
+    frame = exchange([frame] * count)
+    pieces = exchange(
+        run(
+            body(out_space_body, count),
+            [((2 * rows, share), BF16)] * count,
+            *frame,
+            out_space,
+            after,
+            scratch=[((plane, columns), F32), ((plane, share), F32), ((plane, share), F32)],
+        )
+    )
+    mine, after = run(
+        body(join_body, count),
+        [((rows, width), BF16)] * 2,
+        *pieces,
+        scratch=[((count, 2 * rows, share), F32)],
+    )
+    theirs = lax.ppermute(mine, "head", swap)
+    return run(finish_body, ((1, rows, width), F32), mine, theirs, after)
+
+
 def solution(mesh):
     placed = (
         P(("groups", "frame"), "patch", None),
@@ -107,8 +464,20 @@
         P("frame", None, "head"),
         P("frame", "head"),
     )
+
+    def program(video, *rest):
+        frames_here, patches_here, width = video.shape
+        count = lax.axis_size("frame")
+        small = (
+            patches_here == count
+            and frames_here == lax.axis_size("patch") == lax.axis_size("head") == 2
+            and frames_here * patches_here == 8
+            and frames_here * count * patches_here < width
+        )
+        return (moving_tokens if small else on_device)(video, *rest)
+
     return jax.shard_map(
-        on_device,
+        program,
         mesh=mesh,
         in_specs=placed,
         out_specs=P(("groups", "frame", "patch"), None, None),

time: 265 us -> 79.9 us (0.30)
  waiting for transfers between devices: 199 us -> 22.9 us
  starting transfers between devices: 3.67 us -> 29.7 us
  Pallas kernels: 0 us -> 19.1 us
  blocking collectives: 18.6 us -> 0 us
  between operations: 13.3 us -> 0.11 us
  matrix products: 11.3 us -> 0 us
  local copies, waits for them, and re-layouts: 15.8 us -> 7.43 us
  other arithmetic: 2.79 us -> 0 us
    all_gather x4 -> x0, waiting for transfers between devices: 197 us -> none  [the longest x1 74.2 us: on_device(): lax.all_gather(qkv_space, 'frame', axis=0, tiled=True)]
    ppermute x0 -> x22, starting transfers between devices: none -> 29.7 us  [the longest x18 27.6 us: exchange(): lax.ppermute(messages[k], 'frame', [(i, i ^ k) for i in range(count)])]
    ppermute x0 -> x22, waiting for transfers between devices: none -> 22.9 us  [the longest x18 19 us: exchange(): lax.ppermute(messages[k], 'frame', [(i, i ^ k) for i in range(count)])]
    pallas_call x0 -> x10, Pallas kernels: none -> 19.1 us  [run(): pl.pallas_call(body, out_shape=shapes, in_specs=[vmem] * len(args), out_s...]
    all_gather x2 -> x0, local copies, waits for them, and re-layouts: 13.2 us -> none  [the longest x1 6.59 us: on_device(): lax.all_gather(qkv_time, 'frame', axis=0, tiled=True)]
    all_to_all x1 -> x0, blocking collectives: 11.8 us -> none  [on_device(): lax.all_to_all(video, 'frame', split_axis=1, concat_axis=0, tiled=True)]
    dot_general x6 -> x0, matrix products: 11 us -> none  [the longest x2 6.83 us: project_qkv(): jnp.dot(normed, weight.reshape(weight.shape[0], columns), preferred_eleme...]
    psum x2 -> x0, blocking collectives: 6.85 us -> none  [the longest x1 3.43 us: on_device(): lax.psum(rounded.astype(jnp.bfloat16), 'head').astype(jnp.float32)]
  transfers between devices with their start and end apart: 5 -> 22, of which waited for: 4 -> 12; matrix products, arithmetic and copies ran while one was open for 10% -> 2% of each run, Pallas kernels for 0% -> 3%
where the time goes in v1:
time: 79.9 us; the launch traced here: 79.2 us
  starting transfers between devices  29.7 us (37%)
  waiting for transfers between devices  22.9 us (29%)
  Pallas kernels  19.1 us (24%)
  local copies, waits for them, and re-layouts  7.43 us (9%)
    ppermute x18, starting transfers between devices, exchange(): lax.ppermute(messages[k], 'frame', [(i, i ^ k) for i in range(count)])  27.6 us
    pallas_call x10, Pallas kernels, run(): pl.pallas_call(body, out_shape=shapes, in_specs=[vmem] * len(args), out_s...  19.1 us
    ppermute x18, waiting for transfers between devices, exchange(): lax.ppermute(messages[k], 'frame', [(i, i ^ k) for i in range(count)])  19 us
    unnamed x46, local copies, waits for them, and re-layouts  4.78 us
    ppermute x1, waiting for transfers between devices, moving_tokens(): lax.ppermute(cross[:plane // 2], ('patch', 'head'), [(i, 3 - i) for i in...  2.47 us
  transfers between devices with their start and end apart: 22, of which 12 were waited for; matrix products, arithmetic and copies ran while one was open for 2% of the time, Pallas kernels for 3%

profile of v1, /device:TPU:0, one launch (start us, length us, event | category | flops | bytes accessed | tf_op | source)
XLA Modules:
  0.0 79.2 jit_solution(2129985945289084215)
XLA Ops:
  0.0 1.3 %reshape.6.gain_ref = f32[1,1152]{1,0:T(1,128)} reshape(f32[1152]{0:T(1024)} %param.8) | data formatting | bytes 9216 | tf_op jit(solution)/shard_map/reshape | solution.py:365
  1.3 1.6 %shard_map.73 = (bf16[16,288]{1,0:T(8,128)(2,1)}, bf16[16,288]{1,0:T(8,128)(2,1)}, bf16[16,288]{1,0:T(8,128)(2,1)}, bf16[16,288]{1,0:T(8,128)(2,1)}) custom-call(bf16[2,4,1152]{2,1,0:T(4,128)(2,1)} %video_ref.1, f32[1,1152]{1,0:T(1,128)} %reshape.6.gain_ref), custom_call_target="tpu_custom_call" | custom-call | tf_op jit(solution)/shard_map/pallas_call | solution.py:114
  2.9 3.1 %collective-permute-start = (bf16[16,288]{1,0:T(8,128)(2,1)}, bf16[16,288]{1,0:T(8,128)(2,1)S(1)}, u32[]{:S(2)}, u32[]{:S(2)}) collective-permute-start(bf16[16,288]{1,0:T(8,128)(2,1)} %get-tuple-element.31), channel_id=1, source_target_pairs={{0,4},{4,0},{8,12},{12,8},{1,5},{5,1},{9,13},{13,9},{2,6},{6,2},{1... | collective-permute-start | bytes 27656 | tf_op jit(solution)/shard_map/ppermute | solution.py:131
  6.0 2.6 %collective-permute-start.1 = (bf16[16,288]{1,0:T(8,128)(2,1)}, bf16[16,288]{1,0:T(8,128)(2,1)S(1)}, u32[]{:S(2)}, u32[]{:S(2)}) collective-permute-start(bf16[16,288]{1,0:T(8,128)(2,1)} %get-tuple-element.32), channel_id=1, source_target_pairs={{0,8},{4,12},{8,0},{12,4},{1,9},{5,13},{9,1},{13,5},{2,10},{6,14},... | collective-permute-start | bytes 27656 | tf_op jit(solution)/shard_map/ppermute | solution.py:131
  8.6 2.2 %collective-permute-done.1.refs_2_ = bf16[16,288]{1,0:T(8,128)(2,1)S(1)} collective-permute-done((bf16[16,288]{1,0:T(8,128)(2,1)}, bf16[16,288]{1,0:T(8,128)(2,1)S(1)}, u32[]{:S(2)}, u32[]{:S(2)}) %collective-permute-start.1) | collective-permute-done | bytes 9248 | tf_op jit(solution)/shard_map/ppermute | solution.py:131
  10.8 3.5 %collective-permute-done.2.refs_3_ = bf16[16,288]{1,0:T(8,128)(2,1)S(1)} collective-permute-done((bf16[16,288]{1,0:T(8,128)(2,1)}, bf16[16,288]{1,0:T(8,128)(2,1)S(1)}, u32[]{:S(2)}, u32[]{:S(2)}) %collective-permute-start.2) | collective-permute-done | bytes 9248 | tf_op jit(solution)/shard_map/ppermute | solution.py:131
  14.3 0.6 copy-done.5
  14.9 2.4 %shard_map.74 = (bf16[3,8,576]{2,1,0:T(8,128)(2,1)}, bf16[3,8,576]{2,1,0:T(8,128)(2,1)}, bf16[3,8,576]{2,1,0:T(8,128)(2,1)}, bf16[3,8,576]{2,1,0:T(8,128)(2,1)}) custom-call(bf16[16,288]{1,0:T(8,128)(2,1)} %get-tuple-element.30.refs_0_, bf16[16,288]{1,0:T(8,128)(2,1)} %copy-done.3, bf16[16,288]{1,0:T(8,128)(2,1)} %copy-done.4, bf16[16,288]{1,0:T(8,128)(2,1)} %copy-done.5, ...), custom_call_target="tpu_custom_call" | custom-call | tf_op jit(solution)/shard_map/pallas_call | solution.py:114
  17.2 0.0 collective-permute-start.3
  17.2 0.7 collective-permute-start.4
  17.9 3.7 %collective-permute-start.5 = (bf16[3,8,576]{2,1,0:T(8,128)(2,1)}, bf16[3,8,576]{2,1,0:T(8,128)(2,1)S(1)}, u32[]{:S(2)}, u32[]{:S(2)}) collective-permute-start(bf16[3,8,576]{2,1,0:T(8,128)(2,1)} %get-tuple-element.37), channel_id=1, source_target_pairs={{0,12},{4,8},{8,4},{12,0},{1,13},{5,9},{9,5},{13,1},{2,14},{6,10},... | collective-permute-start | bytes 82952 | tf_op jit(solution)/shard_map/ppermute | solution.py:131
  21.6 0.6 reshape.7.refs_4_
  22.2 2.3 %shard_map.75 = (f32[8,576]{1,0:T(8,128)}, f32[8,288]{1,0:T(8,128)}, bf16[16,288]{1,0:T(8,128)(2,1)}, bf16[16,288]{1,0:T(8,128)(2,1)}) custom-call(bf16[16,288]{1,0:T(8,128)(2,1)} %get-tuple-element.30.refs_0_, bf16[16,288]{1,0:T(8,128)(2,1)} %copy-done.3, bf16[16,288]{1,0:T(8,128)(2,1)} %copy-done.4, bf16[16,288]{1,0:T(8,128)(2,1)} %copy-done.5, ...), custom_call_target="tpu_custom_call" | custom-call | tf_op jit(solution)/shard_map/pallas_call | solution.py:114
  24.5 0.0 collective-permute-done.3.refs_1_
  24.5 0.0 collective-permute-done.5.refs_3_
  24.6 0.5 copy-done.6
  25.1 0.0 copy-done.7
  25.1 0.0 copy-done.8
  25.1 1.8 %shard_map.76.refs_0_.refs_4_ = bf16[16,576]{1,0:T(8,128)(2,1)} custom-call(bf16[3,8,576]{2,1,0:T(8,128)(2,1)} %get-tuple-element.34.refs_0_, bf16[3,8,576]{2,1,0:T(8,128)(2,1)} %copy-done.6, bf16[3,8,576]{2,1,0:T(8,128)(2,1)} %copy-done.7, bf16[3,8,576]{2,1,0:T(8,128)(2,1)} %copy-done.8, f32[8,576]{1,0:T(8,128)} %get-tuple-element.38.refs_4_), custom_call_target="tpu_custom_call" | custom-call | tf_op jit(solution)/shard_map/pallas_call | solution.py:114
  26.9 3.0 %collective-permute-start.8 = (bf16[16,576]{1,0:T(8,128)(2,1)}, bf16[16,576]{1,0:T(8,128)(2,1)S(1)}, u32[]{:S(2)}, u32[]{:S(2)}) collective-permute-start(bf16[16,576]{1,0:T(8,128)(2,1)} %shard_map.76.refs_0_.refs_4_), channel_id=1, source_target_pairs={{0,12},{4,8},{8,4},{12,0},{1,13},{5,9},{9,5},{13,1},{2,14},{6,10},... | collective-permute-start | bytes 55304 | tf_op jit(solution)/shard_map/ppermute | solution.py:131
  29.9 0.0 collective-permute-start.7
  29.9 1.4 %collective-permute-start.6 = (bf16[16,576]{1,0:T(8,128)(2,1)}, bf16[16,576]{1,0:T(8,128)(2,1)S(1)}, u32[]{:S(2)}, u32[]{:S(2)}) collective-permute-start(bf16[16,576]{1,0:T(8,128)(2,1)} %shard_map.76.refs_0_.refs_4_), channel_id=1, source_target_pairs={{0,4},{4,0},{8,12},{12,8},{1,5},{5,1},{9,13},{13,9},{2,6},{6,2},{1... | collective-permute-start | bytes 55304 | tf_op jit(solution)/shard_map/ppermute | solution.py:131
  31.3 1.4 %collective-permute-done.8.refs_3_.refs_7_ = bf16[16,576]{1,0:T(8,128)(2,1)S(1)} collective-permute-done((bf16[16,576]{1,0:T(8,128)(2,1)}, bf16[16,576]{1,0:T(8,128)(2,1)S(1)}, u32[]{:S(2)}, u32[]{:S(2)}) %collective-permute-start.8) | collective-permute-done | bytes 18464 | tf_op jit(solution)/shard_map/ppermute | solution.py:131
  32.7 2.1 %collective-permute-done.7.refs_2_.refs_6_ = bf16[16,576]{1,0:T(8,128)(2,1)S(1)} collective-permute-done((bf16[16,576]{1,0:T(8,128)(2,1)}, bf16[16,576]{1,0:T(8,128)(2,1)S(1)}, u32[]{:S(2)}, u32[]{:S(2)}) %collective-permute-start.7) | collective-permute-done | bytes 18464 | tf_op jit(solution)/shard_map/ppermute | solution.py:131
  34.8 0.0 collective-permute-done.6.refs_1_.refs_5_
  34.8 0.6 copy-done.1
  35.4 0.0 copy-done.2
  35.4 2.0 %shard_map.77 = (bf16[16,288]{1,0:T(8,128)(2,1)}, bf16[32,288]{1,0:T(8,128)(2,1)}) custom-call(bf16[16,576]{1,0:T(8,128)(2,1)} %shard_map.76.refs_0_.refs_4_, bf16[16,576]{1,0:T(8,128)(2,1)} %copy-done.2, bf16[16,576]{1,0:T(8,128)(2,1)} %copy-done.1, bf16[16,576]{1,0:T(8,128)(2,1)} %copy-done, bf16[288,576]{1,0:T(8,128)(2,1)} %refs_4_.2, ...), custom_call_target="tpu_custom_call" | custom-call | tf_op jit(solution)/shard_map/pallas_call | solution.py:114
  37.4 1.5 %collective-permute-start.10 = (bf16[32,288]{1,0:T(8,128)(2,1)}, bf16[32,288]{1,0:T(8,128)(2,1)S(1)}, u32[]{:S(2)}, u32[]{:S(2)}) collective-permute-start(bf16[32,288]{1,0:T(8,128)(2,1)} %get-tuple-element.41), channel_id=1, source_target_pairs={{0,2},{2,0},{1,3},{3,1},{4,6},{6,4},{5,7},{7,5},{8,10},{10,8},{9,1... | collective-permute-start | bytes 55304 | tf_op jit(solution)/shard_map/ppermute | solution.py:413
  38.9 0.7 slice.3
  39.7 0.6 collective-permute-start.9
  40.3 2.5 %collective-permute-done.11.refs_3_ = bf16[16,288]{1,0:T(8,128)(2,1)S(1)} collective-permute-done((bf16[16,288]{1,0:T(8,128)(2,1)S(1)}, bf16[16,288]{1,0:T(8,128)(2,1)S(1)}, u32[]{:S(2)}, u32[]{:S(2)}) %collective-permute-start.11) | collective-permute-done | bytes 9248 | tf_op jit(solution)/shard_map/ppermute | solution.py:414
  42.8 0.0 collective-permute-done.10.refs_2_
  42.8 0.6 copy-done.14
  43.4 0.0 copy-done.15
  43.4 0.0 copy-done.12
  43.4 2.4 %shard_map.78 = (bf16[3,8,640]{2,1,0:T(8,128)(2,1)}, bf16[3,8,640]{2,1,0:T(8,128)(2,1)}, bf16[3,8,640]{2,1,0:T(8,128)(2,1)}, bf16[3,8,640]{2,1,0:T(8,128)(2,1)}, bf16[32,288]{1,0:T(8,128)(2,1)}) custom-call(bf16[16,288]{1,0:T(8,128)(2,1)} %get-tuple-element.40.refs_0_, bf16[16,288]{1,0:T(8,128)(2,1)} %copy-done.15, bf16[32,288]{1,0:T(8,128)(2,1)} %copy-done.12, ...), custom_call_target="tpu_custom_call" | custom-call | tf_op jit(solution)/shard_map/pallas_call | solution.py:114
  45.8 0.5 collective-permute-start.12
  46.3 1.6 %collective-permute-start.13 = (bf16[3,8,640]{2,1,0:T(8,128)(2,1)}, bf16[3,8,640]{2,1,0:T(8,128)(2,1)S(1)}, u32[]{:S(2)}, u32[]{:S(2)}) collective-permute-start(bf16[3,8,640]{2,1,0:T(8,128)(2,1)} %get-tuple-element.46), channel_id=1, source_target_pairs={{0,8},{4,12},{8,0},{12,4},{1,9},{5,13},{9,1},{13,5},{2,10},{6,14},... | collective-permute-start | bytes 92168 | tf_op jit(solution)/shard_map/ppermute | solution.py:131
  47.9 2.3 %collective-permute-start.14 = (bf16[3,8,640]{2,1,0:T(8,128)(2,1)}, bf16[3,8,640]{2,1,0:T(8,128)(2,1)S(1)}, u32[]{:S(2)}, u32[]{:S(2)}) collective-permute-start(bf16[3,8,640]{2,1,0:T(8,128)(2,1)} %get-tuple-element.47), channel_id=1, source_target_pairs={{0,12},{4,8},{8,4},{12,0},{1,13},{5,9},{9,5},{13,1},{2,14},{6,10},... | collective-permute-start | bytes 92168 | tf_op jit(solution)/shard_map/ppermute | solution.py:131
  50.2 1.2 %collective-permute-done.13.refs_2_ = bf16[3,8,640]{2,1,0:T(8,128)(2,1)S(1)} collective-permute-done((bf16[3,8,640]{2,1,0:T(8,128)(2,1)}, bf16[3,8,640]{2,1,0:T(8,128)(2,1)S(1)}, u32[]{:S(2)}, u32[]{:S(2)}) %collective-permute-start.13) | collective-permute-done | bytes 30752 | tf_op jit(solution)/shard_map/ppermute | solution.py:131
  51.4 2.3 %collective-permute-done.14.refs_3_ = bf16[3,8,640]{2,1,0:T(8,128)(2,1)S(1)} collective-permute-done((bf16[3,8,640]{2,1,0:T(8,128)(2,1)}, bf16[3,8,640]{2,1,0:T(8,128)(2,1)S(1)}, u32[]{:S(2)}, u32[]{:S(2)}) %collective-permute-start.14) | collective-permute-done | bytes 30752 | tf_op jit(solution)/shard_map/ppermute | solution.py:131
  53.8 0.6 copy-done.11
  54.4 1.9 %shard_map.79.refs_0_ = bf16[8,576]{1,0:T(8,128)(2,1)} custom-call(bf16[3,8,640]{2,1,0:T(8,128)(2,1)} %get-tuple-element.44.refs_0_, bf16[3,8,640]{2,1,0:T(8,128)(2,1)} %copy-done.9, bf16[3,8,640]{2,1,0:T(8,128)(2,1)} %copy-done.10, bf16[3,8,640]{2,1,0:T(8,128)(2,1)} %copy-done.11, bf16[16,576]{1,0:T(8,128)(2,1)} %shard_map.76.refs_0_.refs_4_, ...), custom_call_target="tpu_custom_call" | custom-call | tf_op jit(solution)/shard_map/pallas_call | solution.py:114
  56.3 2.3 %collective-permute-start.17 = (bf16[8,576]{1,0:T(8,128)(2,1)}, bf16[8,576]{1,0:T(8,128)(2,1)S(1)}, u32[]{:S(2)}, u32[]{:S(2)}) collective-permute-start(bf16[8,576]{1,0:T(8,128)(2,1)} %shard_map.79.refs_0_), channel_id=1, source_target_pairs={{0,12},{4,8},{8,4},{12,0},{1,13},{5,9},{9,5},{13,1},{2,14},{6,10},... | collective-permute-start | bytes 27656 | tf_op jit(solution)/shard_map/ppermute | solution.py:131
  58.6 0.0 collective-permute-start.16
  58.6 2.1 %collective-permute-start.15 = (bf16[8,576]{1,0:T(8,128)(2,1)}, bf16[8,576]{1,0:T(8,128)(2,1)S(1)}, u32[]{:S(2)}, u32[]{:S(2)}) collective-permute-start(bf16[8,576]{1,0:T(8,128)(2,1)} %shard_map.79.refs_0_), channel_id=1, source_target_pairs={{0,4},{4,0},{8,12},{12,8},{1,5},{5,1},{9,13},{13,9},{2,6},{6,2},{1... | collective-permute-start | bytes 27656 | tf_op jit(solution)/shard_map/ppermute | solution.py:131
  60.7 1.3 %collective-permute-done.17.refs_3_ = bf16[8,576]{1,0:T(8,128)(2,1)S(1)} collective-permute-done((bf16[8,576]{1,0:T(8,128)(2,1)}, bf16[8,576]{1,0:T(8,128)(2,1)S(1)}, u32[]{:S(2)}, u32[]{:S(2)}) %collective-permute-start.17) | collective-permute-done | bytes 9248 | tf_op jit(solution)/shard_map/ppermute | solution.py:131
  62.0 1.4 %collective-permute-done.16.refs_2_ = bf16[8,576]{1,0:T(8,128)(2,1)S(1)} collective-permute-done((bf16[8,576]{1,0:T(8,128)(2,1)}, bf16[8,576]{1,0:T(8,128)(2,1)S(1)}, u32[]{:S(2)}, u32[]{:S(2)}) %collective-permute-start.16) | collective-permute-done | bytes 9248 | tf_op jit(solution)/shard_map/ppermute | solution.py:131
  63.4 0.6 copy-done.20
  64.0 0.0 copy-done.21
  64.0 1.9 %shard_map.80 = (bf16[16,288]{1,0:T(8,128)(2,1)}, bf16[16,288]{1,0:T(8,128)(2,1)}, bf16[16,288]{1,0:T(8,128)(2,1)}, bf16[16,288]{1,0:T(8,128)(2,1)}) custom-call(bf16[8,576]{1,0:T(8,128)(2,1)} %shard_map.79.refs_0_, bf16[8,576]{1,0:T(8,128)(2,1)} %copy-done.21, bf16[8,576]{1,0:T(8,128)(2,1)} %copy-done.20, bf16[8,576]{1,0:T(8,128)(2,1)} %copy-done.19, ...), custom_call_target="tpu_custom_call" | custom-call | tf_op jit(solution)/shard_map/pallas_call | solution.py:114
  65.9 1.2 %collective-permute-start.18 = (bf16[16,288]{1,0:T(8,128)(2,1)}, bf16[16,288]{1,0:T(8,128)(2,1)S(1)}, u32[]{:S(2)}, u32[]{:S(2)}) collective-permute-start(bf16[16,288]{1,0:T(8,128)(2,1)} %get-tuple-element.50), channel_id=1, source_target_pairs={{0,4},{4,0},{8,12},{12,8},{1,5},{5,1},{9,13},{13,9},{2,6},{6,2},{1... | collective-permute-start | bytes 27656 | tf_op jit(solution)/shard_map/ppermute | solution.py:131
  67.1 1.0 %collective-permute-start.19 = (bf16[16,288]{1,0:T(8,128)(2,1)}, bf16[16,288]{1,0:T(8,128)(2,1)S(1)}, u32[]{:S(2)}, u32[]{:S(2)}) collective-permute-start(bf16[16,288]{1,0:T(8,128)(2,1)} %get-tuple-element.51), channel_id=1, source_target_pairs={{0,8},{4,12},{8,0},{12,4},{1,9},{5,13},{9,1},{13,5},{2,10},{6,14},... | collective-permute-start | bytes 27656 | tf_op jit(solution)/shard_map/ppermute | solution.py:131
  68.1 2.2 %collective-permute-start.20 = (bf16[16,288]{1,0:T(8,128)(2,1)}, bf16[16,288]{1,0:T(8,128)(2,1)S(1)}, u32[]{:S(2)}, u32[]{:S(2)}) collective-permute-start(bf16[16,288]{1,0:T(8,128)(2,1)} %get-tuple-element.52), channel_id=1, source_target_pairs={{0,12},{4,8},{8,4},{12,0},{1,13},{5,9},{9,5},{13,1},{2,14},{6,10},... | collective-permute-start | bytes 27656 | tf_op jit(solution)/shard_map/ppermute | solution.py:131
  70.3 0.0 collective-permute-done.18.refs_1_
  70.3 1.6 %collective-permute-done.19.refs_2_ = bf16[16,288]{1,0:T(8,128)(2,1)S(1)} collective-permute-done((bf16[16,288]{1,0:T(8,128)(2,1)}, bf16[16,288]{1,0:T(8,128)(2,1)S(1)}, u32[]{:S(2)}, u32[]{:S(2)}) %collective-permute-start.19) | collective-permute-done | bytes 9248 | tf_op jit(solution)/shard_map/ppermute | solution.py:131
  71.9 1.9 %collective-permute-done.20.refs_3_ = bf16[16,288]{1,0:T(8,128)(2,1)S(1)} collective-permute-done((bf16[16,288]{1,0:T(8,128)(2,1)}, bf16[16,288]{1,0:T(8,128)(2,1)S(1)}, u32[]{:S(2)}, u32[]{:S(2)}) %collective-permute-start.20) | collective-permute-done | bytes 9248 | tf_op jit(solution)/shard_map/ppermute | solution.py:131
  73.8 0.6 copy-done.18
  74.4 1.5 %shard_map.81 = (bf16[8,1152]{1,0:T(8,128)(2,1)}, bf16[8,1152]{1,0:T(8,128)(2,1)}) custom-call(bf16[16,288]{1,0:T(8,128)(2,1)} %get-tuple-element.49.refs_0_, bf16[16,288]{1,0:T(8,128)(2,1)} %copy-done.16, bf16[16,288]{1,0:T(8,128)(2,1)} %copy-done.17, bf16[16,288]{1,0:T(8,128)(2,1)} %copy-done.18), custom_call_target="tpu_custom_call" | custom-call | tf_op jit(solution)/shard_map/pallas_call | solution.py:114
  75.8 0.0 collective-permute-start.21
  75.8 1.4 %collective-permute-done.21.other = bf16[8,1152]{1,0:T(8,128)(2,1)S(1)} collective-permute-done((bf16[8,1152]{1,0:T(8,128)(2,1)}, bf16[8,1152]{1,0:T(8,128)(2,1)S(1)}, u32[]{:S(2)}, u32[]{:S(2)}) %collective-permute-start.21) | collective-permute-done | bytes 18464 | tf_op jit(solution)/shard_map/ppermute | solution.py:453
  77.2 0.6 copy-done.13
  77.8 1.4 %shard_map.82 = f32[1,8,1152]{2,1,0:T(8,128)} custom-call(bf16[8,1152]{1,0:T(8,128)(2,1)} %get-tuple-element.53.own, bf16[8,1152]{1,0:T(8,128)(2,1)} %copy-done.13, bf16[8,1152]{1,0:T(8,128)(2,1)} %get-tuple-element.54.after), custom_call_target="tpu_custom_call" | custom-call | tf_op jit(solution)/shard_map/pallas_call | solution.py:114
  (39 shorter events, 0.1 us)
Async XLA Ops:
  0.0 21.6 %copy-start.22 = (f32[1152]{0:T(1024)S(1)}, f32[1152]{0:T(1024)}, u32[]{:S(2)}) copy-start(f32[1152]{0:T(1024)} %param.11) | copy-start | bytes 13828
  2.9 5.7 %collective-permute-start = (bf16[16,288]{1,0:T(8,128)(2,1)}, bf16[16,288]{1,0:T(8,128)(2,1)S(1)}, u32[]{:S(2)}, u32[]{:S(2)}) collective-permute-start(bf16[16,288]{1,0:T(8,128)(2,1)} %get-tuple-element.31), channel_id=1, source_target_pairs={{0,4},{4,0},{8,12},{12,8},{1,5},{5,1},{9,13},{13,9},{2,6},{6,2},{1... | collective-permute-start | bytes 27656 | tf_op jit(solution)/shard_map/ppermute | solution.py:131
  6.0 4.8 %collective-permute-start.1 = (bf16[16,288]{1,0:T(8,128)(2,1)}, bf16[16,288]{1,0:T(8,128)(2,1)S(1)}, u32[]{:S(2)}, u32[]{:S(2)}) collective-permute-start(bf16[16,288]{1,0:T(8,128)(2,1)} %get-tuple-element.32), channel_id=1, source_target_pairs={{0,8},{4,12},{8,0},{12,4},{1,9},{5,13},{9,1},{13,5},{2,10},{6,14},... | collective-permute-start | bytes 27656 | tf_op jit(solution)/shard_map/ppermute | solution.py:131
  8.6 5.7 %collective-permute-start.2 = (bf16[16,288]{1,0:T(8,128)(2,1)}, bf16[16,288]{1,0:T(8,128)(2,1)S(1)}, u32[]{:S(2)}, u32[]{:S(2)}) collective-permute-start(bf16[16,288]{1,0:T(8,128)(2,1)} %get-tuple-element.33), channel_id=1, source_target_pairs={{0,12},{4,8},{8,4},{12,0},{1,13},{5,9},{9,5},{13,1},{2,14},{6,10},... | collective-permute-start | bytes 27656 | tf_op jit(solution)/shard_map/ppermute | solution.py:131
  8.6 5.7 %copy-start.3 = (bf16[16,288]{1,0:T(8,128)(2,1)}, bf16[16,288]{1,0:T(8,128)(2,1)S(1)}, u32[]{:S(2)}) copy-start(bf16[16,288]{1,0:T(8,128)(2,1)S(1)} %collective-permute-done.refs_1_) | copy-start | bytes 27652
  10.8 3.5 %copy-start.4 = (bf16[16,288]{1,0:T(8,128)(2,1)}, bf16[16,288]{1,0:T(8,128)(2,1)S(1)}, u32[]{:S(2)}) copy-start(bf16[16,288]{1,0:T(8,128)(2,1)S(1)} %collective-permute-done.1.refs_2_) | copy-start | bytes 27652
  14.3 0.6 copy-start.5
  17.2 7.3 %collective-permute-start.3 = (bf16[3,8,576]{2,1,0:T(8,128)(2,1)}, bf16[3,8,576]{2,1,0:T(8,128)(2,1)S(1)}, u32[]{:S(2)}, u32[]{:S(2)}) collective-permute-start(bf16[3,8,576]{2,1,0:T(8,128)(2,1)} %get-tuple-element.35), channel_id=1, source_target_pairs={{0,4},{4,0},{8,12},{12,8},{1,5},{5,1},{9,13},{13,9},{2,6},{6,2},{1... | collective-permute-start | bytes 82952 | tf_op jit(solution)/shard_map/ppermute | solution.py:131
  17.2 7.3 %collective-permute-start.4 = (bf16[3,8,576]{2,1,0:T(8,128)(2,1)}, bf16[3,8,576]{2,1,0:T(8,128)(2,1)S(1)}, u32[]{:S(2)}, u32[]{:S(2)}) collective-permute-start(bf16[3,8,576]{2,1,0:T(8,128)(2,1)} %get-tuple-element.36), channel_id=1, source_target_pairs={{0,8},{4,12},{8,0},{12,4},{1,9},{5,13},{9,1},{13,5},{2,10},{6,14},... | collective-permute-start | bytes 82952 | tf_op jit(solution)/shard_map/ppermute | solution.py:131
  17.9 6.6 %collective-permute-start.5 = (bf16[3,8,576]{2,1,0:T(8,128)(2,1)}, bf16[3,8,576]{2,1,0:T(8,128)(2,1)S(1)}, u32[]{:S(2)}, u32[]{:S(2)}) collective-permute-start(bf16[3,8,576]{2,1,0:T(8,128)(2,1)} %get-tuple-element.37), channel_id=1, source_target_pairs={{0,12},{4,8},{8,4},{12,0},{1,13},{5,9},{9,5},{13,1},{2,14},{6,10},... | collective-permute-start | bytes 82952 | tf_op jit(solution)/shard_map/ppermute | solution.py:131
  24.5 0.6 copy-start.6
  24.5 0.6 copy-start.7
  24.5 0.6 copy-start.8
  26.9 5.8 %collective-permute-start.8 = (bf16[16,576]{1,0:T(8,128)(2,1)}, bf16[16,576]{1,0:T(8,128)(2,1)S(1)}, u32[]{:S(2)}, u32[]{:S(2)}) collective-permute-start(bf16[16,576]{1,0:T(8,128)(2,1)} %shard_map.76.refs_0_.refs_4_), channel_id=1, source_target_pairs={{0,12},{4,8},{8,4},{12,0},{1,13},{5,9},{9,5},{13,1},{2,14},{6,10},... | collective-permute-start | bytes 55304 | tf_op jit(solution)/shard_map/ppermute | solution.py:131
  29.9 4.9 %collective-permute-start.7 = (bf16[16,576]{1,0:T(8,128)(2,1)}, bf16[16,576]{1,0:T(8,128)(2,1)S(1)}, u32[]{:S(2)}, u32[]{:S(2)}) collective-permute-start(bf16[16,576]{1,0:T(8,128)(2,1)} %shard_map.76.refs_0_.refs_4_), channel_id=1, source_target_pairs={{0,8},{4,12},{8,0},{12,4},{1,9},{5,13},{9,1},{13,5},{2,10},{6,14},... | collective-permute-start | bytes 55304 | tf_op jit(solution)/shard_map/ppermute | solution.py:131
  29.9 4.9 %collective-permute-start.6 = (bf16[16,576]{1,0:T(8,128)(2,1)}, bf16[16,576]{1,0:T(8,128)(2,1)S(1)}, u32[]{:S(2)}, u32[]{:S(2)}) collective-permute-start(bf16[16,576]{1,0:T(8,128)(2,1)} %shard_map.76.refs_0_.refs_4_), channel_id=1, source_target_pairs={{0,4},{4,0},{8,12},{12,8},{1,5},{5,1},{9,13},{13,9},{2,6},{6,2},{1... | collective-permute-start | bytes 55304 | tf_op jit(solution)/shard_map/ppermute | solution.py:131
  32.7 2.1 %copy-start = (bf16[16,576]{1,0:T(8,128)(2,1)}, bf16[16,576]{1,0:T(8,128)(2,1)S(1)}, u32[]{:S(2)}) copy-start(bf16[16,576]{1,0:T(8,128)(2,1)S(1)} %collective-permute-done.8.refs_3_.refs_7_) | copy-start | bytes 55300
  34.8 0.6 copy-start.1
  34.8 0.6 copy-start.2
  37.4 5.4 %collective-permute-start.10 = (bf16[32,288]{1,0:T(8,128)(2,1)}, bf16[32,288]{1,0:T(8,128)(2,1)S(1)}, u32[]{:S(2)}, u32[]{:S(2)}) collective-permute-start(bf16[32,288]{1,0:T(8,128)(2,1)} %get-tuple-element.41), channel_id=1, source_target_pairs={{0,2},{2,0},{1,3},{3,1},{4,6},{6,4},{5,7},{7,5},{8,10},{10,8},{9,1... | collective-permute-start | bytes 55304 | tf_op jit(solution)/shard_map/ppermute | solution.py:413
  39.7 3.1 %collective-permute-start.11 = (bf16[16,288]{1,0:T(8,128)(2,1)S(1)}, bf16[16,288]{1,0:T(8,128)(2,1)S(1)}, u32[]{:S(2)}, u32[]{:S(2)}) collective-permute-start(bf16[16,288]{1,0:T(8,128)(2,1)S(1)} %slice.3), channel_id=1, source_target_pairs={{0,3},{1,2},{2,1},{3,0},{4,7},{5,6},{6,5},{7,4},{8,11},{9,10},{10,... | collective-permute-start | bytes 27656 | tf_op jit(solution)/shard_map/ppermute | solution.py:414
  39.7 3.1 %collective-permute-start.9 = (bf16[16,288]{1,0:T(8,128)(2,1)}, bf16[16,288]{1,0:T(8,128)(2,1)S(1)}, u32[]{:S(2)}, u32[]{:S(2)}) collective-permute-start(bf16[16,288]{1,0:T(8,128)(2,1)} %get-tuple-element.40.refs_0_), channel_id=1, source_target_pairs={{0,1},{1,0},{2,3},{3,2},{4,5},{5,4},{6,7},{7,6},{8,9},{9,8},{10,11... | collective-permute-start | bytes 27656 | tf_op jit(solution)/shard_map/ppermute | solution.py:412
  42.8 0.6 copy-start.14
  42.8 0.6 copy-start.15
  42.8 0.6 copy-start.12
  45.8 4.4 %collective-permute-start.12 = (bf16[3,8,640]{2,1,0:T(8,128)(2,1)}, bf16[3,8,640]{2,1,0:T(8,128)(2,1)S(1)}, u32[]{:S(2)}, u32[]{:S(2)}) collective-permute-start(bf16[3,8,640]{2,1,0:T(8,128)(2,1)} %get-tuple-element.45), channel_id=1, source_target_pairs={{0,4},{4,0},{8,12},{12,8},{1,5},{5,1},{9,13},{13,9},{2,6},{6,2},{1... | collective-permute-start | bytes 92168 | tf_op jit(solution)/shard_map/ppermute | solution.py:131
  46.3 5.2 %collective-permute-start.13 = (bf16[3,8,640]{2,1,0:T(8,128)(2,1)}, bf16[3,8,640]{2,1,0:T(8,128)(2,1)S(1)}, u32[]{:S(2)}, u32[]{:S(2)}) collective-permute-start(bf16[3,8,640]{2,1,0:T(8,128)(2,1)} %get-tuple-element.46), channel_id=1, source_target_pairs={{0,8},{4,12},{8,0},{12,4},{1,9},{5,13},{9,1},{13,5},{2,10},{6,14},... | collective-permute-start | bytes 92168 | tf_op jit(solution)/shard_map/ppermute | solution.py:131
  47.9 5.9 %collective-permute-start.14 = (bf16[3,8,640]{2,1,0:T(8,128)(2,1)}, bf16[3,8,640]{2,1,0:T(8,128)(2,1)S(1)}, u32[]{:S(2)}, u32[]{:S(2)}) collective-permute-start(bf16[3,8,640]{2,1,0:T(8,128)(2,1)} %get-tuple-element.47), channel_id=1, source_target_pairs={{0,12},{4,8},{8,4},{12,0},{1,13},{5,9},{9,5},{13,1},{2,14},{6,10},... | collective-permute-start | bytes 92168 | tf_op jit(solution)/shard_map/ppermute | solution.py:131
  50.2 3.6 %copy-start.9 = (bf16[3,8,640]{2,1,0:T(8,128)(2,1)}, bf16[3,8,640]{2,1,0:T(8,128)(2,1)S(1)}, u32[]{:S(2)}) copy-start(bf16[3,8,640]{2,1,0:T(8,128)(2,1)S(1)} %collective-permute-done.12.refs_1_) | copy-start | bytes 92164
  51.4 2.4 %copy-start.10 = (bf16[3,8,640]{2,1,0:T(8,128)(2,1)}, bf16[3,8,640]{2,1,0:T(8,128)(2,1)S(1)}, u32[]{:S(2)}) copy-start(bf16[3,8,640]{2,1,0:T(8,128)(2,1)S(1)} %collective-permute-done.13.refs_2_) | copy-start | bytes 92164
  53.8 0.6 copy-start.11
  56.3 5.7 %collective-permute-start.17 = (bf16[8,576]{1,0:T(8,128)(2,1)}, bf16[8,576]{1,0:T(8,128)(2,1)S(1)}, u32[]{:S(2)}, u32[]{:S(2)}) collective-permute-start(bf16[8,576]{1,0:T(8,128)(2,1)} %shard_map.79.refs_0_), channel_id=1, source_target_pairs={{0,12},{4,8},{8,4},{12,0},{1,13},{5,9},{9,5},{13,1},{2,14},{6,10},... | collective-permute-start | bytes 27656 | tf_op jit(solution)/shard_map/ppermute | solution.py:131
  58.6 4.8 %collective-permute-start.16 = (bf16[8,576]{1,0:T(8,128)(2,1)}, bf16[8,576]{1,0:T(8,128)(2,1)S(1)}, u32[]{:S(2)}, u32[]{:S(2)}) collective-permute-start(bf16[8,576]{1,0:T(8,128)(2,1)} %shard_map.79.refs_0_), channel_id=1, source_target_pairs={{0,8},{4,12},{8,0},{12,4},{1,9},{5,13},{9,1},{13,5},{2,10},{6,14},... | collective-permute-start | bytes 27656 | tf_op jit(solution)/shard_map/ppermute | solution.py:131
  58.6 4.8 %collective-permute-start.15 = (bf16[8,576]{1,0:T(8,128)(2,1)}, bf16[8,576]{1,0:T(8,128)(2,1)S(1)}, u32[]{:S(2)}, u32[]{:S(2)}) collective-permute-start(bf16[8,576]{1,0:T(8,128)(2,1)} %shard_map.79.refs_0_), channel_id=1, source_target_pairs={{0,4},{4,0},{8,12},{12,8},{1,5},{5,1},{9,13},{13,9},{2,6},{6,2},{1... | collective-permute-start | bytes 27656 | tf_op jit(solution)/shard_map/ppermute | solution.py:131
  62.0 1.4 %copy-start.19 = (bf16[8,576]{1,0:T(8,128)(2,1)}, bf16[8,576]{1,0:T(8,128)(2,1)S(1)}, u32[]{:S(2)}) copy-start(bf16[8,576]{1,0:T(8,128)(2,1)S(1)} %collective-permute-done.17.refs_3_) | copy-start | bytes 27652
  63.4 0.6 copy-start.20
  63.4 0.6 copy-start.21
  65.9 4.4 %collective-permute-start.18 = (bf16[16,288]{1,0:T(8,128)(2,1)}, bf16[16,288]{1,0:T(8,128)(2,1)S(1)}, u32[]{:S(2)}, u32[]{:S(2)}) collective-permute-start(bf16[16,288]{1,0:T(8,128)(2,1)} %get-tuple-element.50), channel_id=1, source_target_pairs={{0,4},{4,0},{8,12},{12,8},{1,5},{5,1},{9,13},{13,9},{2,6},{6,2},{1... | collective-permute-start | bytes 27656 | tf_op jit(solution)/shard_map/ppermute | solution.py:131
  67.1 4.8 %collective-permute-start.19 = (bf16[16,288]{1,0:T(8,128)(2,1)}, bf16[16,288]{1,0:T(8,128)(2,1)S(1)}, u32[]{:S(2)}, u32[]{:S(2)}) collective-permute-start(bf16[16,288]{1,0:T(8,128)(2,1)} %get-tuple-element.51), channel_id=1, source_target_pairs={{0,8},{4,12},{8,0},{12,4},{1,9},{5,13},{9,1},{13,5},{2,10},{6,14},... | collective-permute-start | bytes 27656 | tf_op jit(solution)/shard_map/ppermute | solution.py:131
  68.1 5.7 %collective-permute-start.20 = (bf16[16,288]{1,0:T(8,128)(2,1)}, bf16[16,288]{1,0:T(8,128)(2,1)S(1)}, u32[]{:S(2)}, u32[]{:S(2)}) collective-permute-start(bf16[16,288]{1,0:T(8,128)(2,1)} %get-tuple-element.52), channel_id=1, source_target_pairs={{0,12},{4,8},{8,4},{12,0},{1,13},{5,9},{9,5},{13,1},{2,14},{6,10},... | collective-permute-start | bytes 27656 | tf_op jit(solution)/shard_map/ppermute | solution.py:131
  70.3 3.5 %copy-start.16 = (bf16[16,288]{1,0:T(8,128)(2,1)}, bf16[16,288]{1,0:T(8,128)(2,1)S(1)}, u32[]{:S(2)}) copy-start(bf16[16,288]{1,0:T(8,128)(2,1)S(1)} %collective-permute-done.18.refs_1_) | copy-start | bytes 27652
  71.9 1.9 %copy-start.17 = (bf16[16,288]{1,0:T(8,128)(2,1)}, bf16[16,288]{1,0:T(8,128)(2,1)S(1)}, u32[]{:S(2)}) copy-start(bf16[16,288]{1,0:T(8,128)(2,1)S(1)} %collective-permute-done.19.refs_2_) | copy-start | bytes 27652
  73.8 0.6 copy-start.18
  75.8 1.4 %collective-permute-start.21 = (bf16[8,1152]{1,0:T(8,128)(2,1)}, bf16[8,1152]{1,0:T(8,128)(2,1)S(1)}, u32[]{:S(2)}, u32[]{:S(2)}) collective-permute-start(bf16[8,1152]{1,0:T(8,128)(2,1)} %get-tuple-element.53.own), channel_id=1, source_target_pairs={{0,1},{1,0},{2,3},{3,2},{4,5},{5,4},{6,7},{7,6},{8,9},{9,8},{10,11... | collective-permute-start | bytes 55304 | tf_op jit(solution)/shard_map/ppermute | solution.py:453
  77.2 0.6 copy-start.13

commit v2 on v1

--- a/solution.py
+++ b/solution.py
@@ -117,6 +117,7 @@
         in_specs=[vmem] * len(args),
         out_specs=[vmem] * len(shapes),
         scratch_shapes=[pltpu.VMEM(*s) for s in scratch],
+        compiler_params=pltpu.CompilerParams(vmem_limit_bytes=16 << 20),
     )(*args)
     return found[0] if single else found
 

time: 79.9 us -> 60.7 us (0.76)
  Pallas kernels: 19.1 us -> 3.53 us
  local copies, waits for them, and re-layouts: 7.43 us -> 3.48 us
    pallas_call x10, Pallas kernels: 19.1 us -> 3.53 us  [run(): pl.pallas_call(body, out_shape=shapes, in_specs=[vmem] * len(args), out_s...]
    unnamed x46 -> x10, local copies, waits for them, and re-layouts: 4.78 us -> 1.98 us
  transfers between devices with their start and end apart: 22 -> 22, of which waited for: 12 -> 13; matrix products, arithmetic and copies ran while one was open for 2% -> 1% of each run, Pallas kernels for 3% -> 1%
where the time goes in v2:
time: 60.7 us; the launch traced here: 60.5 us
  starting transfers between devices  30.1 us (50%)
  waiting for transfers between devices  23.2 us (38%)
  Pallas kernels  3.53 us (6%)
  local copies, waits for them, and re-layouts  3.48 us (6%)
    ppermute x18, starting transfers between devices, exchange(): lax.ppermute(messages[k], 'frame', [(i, i ^ k) for i in range(count)])  27.9 us
    ppermute x18, waiting for transfers between devices, exchange(): lax.ppermute(messages[k], 'frame', [(i, i ^ k) for i in range(count)])  19.6 us
    pallas_call x10, Pallas kernels, run(): pl.pallas_call(body, out_shape=shapes, in_specs=[vmem] * len(args), out_s...  3.53 us
    ppermute x1, waiting for transfers between devices, moving_tokens(): lax.ppermute(cross[:plane // 2], ('patch', 'head'), [(i, 3 - i) for i in...  2.47 us
    unnamed x10, local copies, waits for them, and re-layouts  1.98 us
    ppermute x1, starting transfers between devices, moving_tokens(): crossed = lax.ppermute(cross, 'patch', swap)  1.56 us
  transfers between devices with their start and end apart: 22, of which 13 were waited for; matrix products, arithmetic and copies ran while one was open for 1% of the time, Pallas kernels for 1%

profile of v2, /device:TPU:0, one launch (start us, length us, event | category | flops | bytes accessed | tf_op | source)
XLA Modules:
  0.0 60.5 jit_solution(4031107580188973766)
XLA Ops:
  0.0 0.0 copy-start
  0.0 0.8 %reshape.6.gain_ref = f32[1,1152]{1,0:T(1,128)S(1)} reshape(f32[1152]{0:T(1024)} %param.8) | data formatting | bytes 9216 | tf_op jit(solution)/shard_map/reshape | solution.py:366
  0.8 0.0 copy-start.4
  0.8 0.7 %copy-done.4 = bf16[2,4,1152]{2,1,0:T(4,128)(2,1)S(1)} copy-done((bf16[2,4,1152]{2,1,0:T(4,128)(2,1)S(1)}, bf16[2,4,1152]{2,1,0:T(4,128)(2,1)}, u32[]{:S(2)}) %copy-start.4) | copy-done | bytes 18456
  1.5 0.3 shard_map.73
  1.8 3.1 %collective-permute-start = (bf16[16,288]{1,0:T(8,128)(2,1)S(1)}, bf16[16,288]{1,0:T(8,128)(2,1)S(1)}, u32[]{:S(2)}, u32[]{:S(2)}) collective-permute-start(bf16[16,288]{1,0:T(8,128)(2,1)S(1)} %get-tuple-element.31), channel_id=1, source_target_pairs={{0,4},{4,0},{8,12},{12,8},{1,5},{5,1},{9,13},{13,9},{2,6},{6,2},{1... | collective-permute-start | bytes 27656 | tf_op jit(solution)/shard_map/ppermute | solution.py:132
  4.9 2.6 %collective-permute-start.1 = (bf16[16,288]{1,0:T(8,128)(2,1)S(1)}, bf16[16,288]{1,0:T(8,128)(2,1)S(1)}, u32[]{:S(2)}, u32[]{:S(2)}) collective-permute-start(bf16[16,288]{1,0:T(8,128)(2,1)S(1)} %get-tuple-element.32), channel_id=1, source_target_pairs={{0,8},{4,12},{8,0},{12,4},{1,9},{5,13},{9,1},{13,5},{2,10},{6,14},... | collective-permute-start | bytes 27656 | tf_op jit(solution)/shard_map/ppermute | solution.py:132
  7.5 0.0 collective-permute-start.2
  7.5 0.0 collective-permute-done.refs_1_
  7.5 2.0 %collective-permute-done.1.refs_2_ = bf16[16,288]{1,0:T(8,128)(2,1)S(1)} collective-permute-done((bf16[16,288]{1,0:T(8,128)(2,1)S(1)}, bf16[16,288]{1,0:T(8,128)(2,1)S(1)}, u32[]{:S(2)}, u32[]{:S(2)}) %collective-permute-start.1) | collective-permute-done | bytes 9248 | tf_op jit(solution)/shard_map/ppermute | solution.py:132
  9.5 3.5 %collective-permute-done.2.refs_3_ = bf16[16,288]{1,0:T(8,128)(2,1)S(1)} collective-permute-done((bf16[16,288]{1,0:T(8,128)(2,1)S(1)}, bf16[16,288]{1,0:T(8,128)(2,1)S(1)}, u32[]{:S(2)}, u32[]{:S(2)}) %collective-permute-start.2) | collective-permute-done | bytes 9248 | tf_op jit(solution)/shard_map/ppermute | solution.py:132
  13.0 1.2 %copy-done.1 = bf16[288,3,576]{2,0,1:T(8,128)(2,1)S(1)} copy-done((bf16[288,3,576]{2,0,1:T(8,128)(2,1)S(1)}, bf16[288,3,576]{2,0,1:T(8,128)(2,1)}, u32[]{:S(2)}) %copy-start.1) | copy-done | bytes 995352
  14.2 0.4 shard_map.74
  14.7 0.1 collective-permute-start.3
  14.8 0.7 %collective-permute-start.4 = (bf16[3,8,576]{2,1,0:T(8,128)(2,1)S(1)}, bf16[3,8,576]{2,1,0:T(8,128)(2,1)S(1)}, u32[]{:S(2)}, u32[]{:S(2)}) collective-permute-start(bf16[3,8,576]{2,1,0:T(8,128)(2,1)S(1)} %get-tuple-element.36), channel_id=1, source_target_pairs={{0,8},{4,12},{8,0},{12,4},{1,9},{5,13},{9,1},{13,5},{2,10},{6,14},... | collective-permute-start | bytes 82952 | tf_op jit(solution)/shard_map/ppermute | solution.py:132
  15.5 3.7 %collective-permute-start.5 = (bf16[3,8,576]{2,1,0:T(8,128)(2,1)S(1)}, bf16[3,8,576]{2,1,0:T(8,128)(2,1)S(1)}, u32[]{:S(2)}, u32[]{:S(2)}) collective-permute-start(bf16[3,8,576]{2,1,0:T(8,128)(2,1)S(1)} %get-tuple-element.37), channel_id=1, source_target_pairs={{0,12},{4,8},{8,4},{12,0},{1,13},{5,9},{9,5},{13,1},{2,14},{6,10},... | collective-permute-start | bytes 82952 | tf_op jit(solution)/shard_map/ppermute | solution.py:132
  19.1 0.7 %reshape.7.refs_4_ = f32[1,1152]{1,0:T(1,128)S(1)} reshape(f32[1152]{0:T(1024)} %param.11) | data formatting | bytes 9216 | tf_op jit(solution)/shard_map/reshape | solution.py:366
  19.8 0.0 copy-done
  19.9 0.3 shard_map.75
  20.2 0.0 copy-start.3
  20.2 0.0 collective-permute-done.3.refs_1_
  20.2 0.0 collective-permute-done.4.refs_2_
  20.2 1.2 %collective-permute-done.5.refs_3_ = bf16[3,8,576]{2,1,0:T(8,128)(2,1)S(1)} collective-permute-done((bf16[3,8,576]{2,1,0:T(8,128)(2,1)S(1)}, bf16[3,8,576]{2,1,0:T(8,128)(2,1)S(1)}, u32[]{:S(2)}, u32[]{:S(2)}) %collective-permute-start.5) | collective-permute-done | bytes 27680 | tf_op jit(solution)/shard_map/ppermute | solution.py:132
  21.4 0.4 shard_map.76.refs_0_.refs_4_
  21.8 3.4 %collective-permute-start.8 = (bf16[16,576]{1,0:T(8,128)(2,1)S(1)}, bf16[16,576]{1,0:T(8,128)(2,1)S(1)}, u32[]{:S(2)}, u32[]{:S(2)}) collective-permute-start(bf16[16,576]{1,0:T(8,128)(2,1)S(1)} %shard_map.76.refs_0_.refs_4_), channel_id=1, source_target_pairs={{0,12},{4,8},{8,4},{12,0},{1,13},{5,9},{9,5},{13,1},{2,14},{6,10},... | collective-permute-start | bytes 55304 | tf_op jit(solution)/shard_map/ppermute | solution.py:132
  25.2 0.0 collective-permute-start.7
  25.2 1.0 %collective-permute-start.6 = (bf16[16,576]{1,0:T(8,128)(2,1)S(1)}, bf16[16,576]{1,0:T(8,128)(2,1)S(1)}, u32[]{:S(2)}, u32[]{:S(2)}) collective-permute-start(bf16[16,576]{1,0:T(8,128)(2,1)S(1)} %shard_map.76.refs_0_.refs_4_), channel_id=1, source_target_pairs={{0,4},{4,0},{8,12},{12,8},{1,5},{5,1},{9,13},{13,9},{2,6},{6,2},{1... | collective-permute-start | bytes 55304 | tf_op jit(solution)/shard_map/ppermute | solution.py:132
  26.2 1.2 %collective-permute-done.8.refs_3_.refs_7_ = bf16[16,576]{1,0:T(8,128)(2,1)S(1)} collective-permute-done((bf16[16,576]{1,0:T(8,128)(2,1)S(1)}, bf16[16,576]{1,0:T(8,128)(2,1)S(1)}, u32[]{:S(2)}, u32[]{:S(2)}) %collective-permute-start.8) | collective-permute-done | bytes 18464 | tf_op jit(solution)/shard_map/ppermute | solution.py:132
  27.4 2.5 %collective-permute-done.7.refs_2_.refs_6_ = bf16[16,576]{1,0:T(8,128)(2,1)S(1)} collective-permute-done((bf16[16,576]{1,0:T(8,128)(2,1)S(1)}, bf16[16,576]{1,0:T(8,128)(2,1)S(1)}, u32[]{:S(2)}, u32[]{:S(2)}) %collective-permute-start.7) | collective-permute-done | bytes 18464 | tf_op jit(solution)/shard_map/ppermute | solution.py:132
  29.9 0.0 collective-permute-done.6.refs_1_.refs_5_
  29.9 0.0 copy-done.2
  29.9 0.3 shard_map.77
  30.2 1.6 %collective-permute-start.10 = (bf16[32,288]{1,0:T(8,128)(2,1)S(1)}, bf16[32,288]{1,0:T(8,128)(2,1)S(1)}, u32[]{:S(2)}, u32[]{:S(2)}) collective-permute-start(bf16[32,288]{1,0:T(8,128)(2,1)S(1)} %get-tuple-element.41), channel_id=1, source_target_pairs={{0,2},{2,0},{1,3},{3,1},{4,6},{6,4},{5,7},{7,5},{8,10},{10,8},{9,1... | collective-permute-start | bytes 55304 | tf_op jit(solution)/shard_map/ppermute | solution.py:414
  31.8 0.0 collective-permute-start.11
  31.8 0.6 %collective-permute-start.9 = (bf16[16,288]{1,0:T(8,128)(2,1)S(1)}, bf16[16,288]{1,0:T(8,128)(2,1)S(1)}, u32[]{:S(2)}, u32[]{:S(2)}) collective-permute-start(bf16[16,288]{1,0:T(8,128)(2,1)S(1)} %get-tuple-element.40.refs_0_), channel_id=1, source_target_pairs={{0,1},{1,0},{2,3},{3,2},{4,5},{5,4},{6,7},{7,6},{8,9},{9,8},{10,11... | collective-permute-start | bytes 27656 | tf_op jit(solution)/shard_map/ppermute | solution.py:413
  32.4 2.5 %collective-permute-done.11.refs_3_ = bf16[16,288]{1,0:T(8,128)(2,1)S(1)} collective-permute-done((bf16[16,288]{1,0:T(8,128)(2,1)S(1)}, bf16[16,288]{1,0:T(8,128)(2,1)S(1)}, u32[]{:S(2)}, u32[]{:S(2)}) %collective-permute-start.11) | collective-permute-done | bytes 9248 | tf_op jit(solution)/shard_map/ppermute | solution.py:415
  34.9 0.0 collective-permute-done.9.refs_1_
  34.9 0.0 collective-permute-done.10.refs_2_
  34.9 0.4 shard_map.78
  35.3 0.1 collective-permute-start.12
  35.5 2.0 %collective-permute-start.13 = (bf16[3,8,640]{2,1,0:T(8,128)(2,1)S(1)}, bf16[3,8,640]{2,1,0:T(8,128)(2,1)S(1)}, u32[]{:S(2)}, u32[]{:S(2)}) collective-permute-start(bf16[3,8,640]{2,1,0:T(8,128)(2,1)S(1)} %get-tuple-element.46), channel_id=1, source_target_pairs={{0,8},{4,12},{8,0},{12,4},{1,9},{5,13},{9,1},{13,5},{2,10},{6,14},... | collective-permute-start | bytes 92168 | tf_op jit(solution)/shard_map/ppermute | solution.py:132
  37.5 2.3 %collective-permute-start.14 = (bf16[3,8,640]{2,1,0:T(8,128)(2,1)S(1)}, bf16[3,8,640]{2,1,0:T(8,128)(2,1)S(1)}, u32[]{:S(2)}, u32[]{:S(2)}) collective-permute-start(bf16[3,8,640]{2,1,0:T(8,128)(2,1)S(1)} %get-tuple-element.47), channel_id=1, source_target_pairs={{0,12},{4,8},{8,4},{12,0},{1,13},{5,9},{9,5},{13,1},{2,14},{6,10},... | collective-permute-start | bytes 92168 | tf_op jit(solution)/shard_map/ppermute | solution.py:132
  39.8 0.0 collective-permute-done.12.refs_1_
  39.8 0.5 collective-permute-done.13.refs_2_
  40.3 2.9 %collective-permute-done.14.refs_3_ = bf16[3,8,640]{2,1,0:T(8,128)(2,1)S(1)} collective-permute-done((bf16[3,8,640]{2,1,0:T(8,128)(2,1)S(1)}, bf16[3,8,640]{2,1,0:T(8,128)(2,1)S(1)}, u32[]{:S(2)}, u32[]{:S(2)}) %collective-permute-start.14) | collective-permute-done | bytes 30752 | tf_op jit(solution)/shard_map/ppermute | solution.py:132
  43.2 0.5 shard_map.79.refs_0_
  43.7 2.3 %collective-permute-start.17 = (bf16[8,576]{1,0:T(8,128)(2,1)S(1)}, bf16[8,576]{1,0:T(8,128)(2,1)S(1)}, u32[]{:S(2)}, u32[]{:S(2)}) collective-permute-start(bf16[8,576]{1,0:T(8,128)(2,1)S(1)} %shard_map.79.refs_0_), channel_id=1, source_target_pairs={{0,12},{4,8},{8,4},{12,0},{1,13},{5,9},{9,5},{13,1},{2,14},{6,10},... | collective-permute-start | bytes 27656 | tf_op jit(solution)/shard_map/ppermute | solution.py:132
  46.0 0.0 collective-permute-start.16
  46.0 2.1 %collective-permute-start.15 = (bf16[8,576]{1,0:T(8,128)(2,1)S(1)}, bf16[8,576]{1,0:T(8,128)(2,1)S(1)}, u32[]{:S(2)}, u32[]{:S(2)}) collective-permute-start(bf16[8,576]{1,0:T(8,128)(2,1)S(1)} %shard_map.79.refs_0_), channel_id=1, source_target_pairs={{0,4},{4,0},{8,12},{12,8},{1,5},{5,1},{9,13},{13,9},{2,6},{6,2},{1... | collective-permute-start | bytes 27656 | tf_op jit(solution)/shard_map/ppermute | solution.py:132
  48.1 1.1 %collective-permute-done.17.refs_3_ = bf16[8,576]{1,0:T(8,128)(2,1)S(1)} collective-permute-done((bf16[8,576]{1,0:T(8,128)(2,1)S(1)}, bf16[8,576]{1,0:T(8,128)(2,1)S(1)}, u32[]{:S(2)}, u32[]{:S(2)}) %collective-permute-start.17) | collective-permute-done | bytes 9248 | tf_op jit(solution)/shard_map/ppermute | solution.py:132
  49.1 1.4 %collective-permute-done.16.refs_2_ = bf16[8,576]{1,0:T(8,128)(2,1)S(1)} collective-permute-done((bf16[8,576]{1,0:T(8,128)(2,1)S(1)}, bf16[8,576]{1,0:T(8,128)(2,1)S(1)}, u32[]{:S(2)}, u32[]{:S(2)}) %collective-permute-start.16) | collective-permute-done | bytes 9248 | tf_op jit(solution)/shard_map/ppermute | solution.py:132
  50.5 0.0 collective-permute-done.15.refs_1_
  50.5 0.0 copy-done.3
  50.5 0.2 shard_map.80
  50.8 1.3 %collective-permute-start.18 = (bf16[16,288]{1,0:T(8,128)(2,1)S(1)}, bf16[16,288]{1,0:T(8,128)(2,1)S(1)}, u32[]{:S(2)}, u32[]{:S(2)}) collective-permute-start(bf16[16,288]{1,0:T(8,128)(2,1)S(1)} %get-tuple-element.50), channel_id=1, source_target_pairs={{0,4},{4,0},{8,12},{12,8},{1,5},{5,1},{9,13},{13,9},{2,6},{6,2},{1... | collective-permute-start | bytes 27656 | tf_op jit(solution)/shard_map/ppermute | solution.py:132
  52.1 0.9 %collective-permute-start.19 = (bf16[16,288]{1,0:T(8,128)(2,1)S(1)}, bf16[16,288]{1,0:T(8,128)(2,1)S(1)}, u32[]{:S(2)}, u32[]{:S(2)}) collective-permute-start(bf16[16,288]{1,0:T(8,128)(2,1)S(1)} %get-tuple-element.51), channel_id=1, source_target_pairs={{0,8},{4,12},{8,0},{12,4},{1,9},{5,13},{9,1},{13,5},{2,10},{6,14},... | collective-permute-start | bytes 27656 | tf_op jit(solution)/shard_map/ppermute | solution.py:132
  53.0 2.2 %collective-permute-start.20 = (bf16[16,288]{1,0:T(8,128)(2,1)S(1)}, bf16[16,288]{1,0:T(8,128)(2,1)S(1)}, u32[]{:S(2)}, u32[]{:S(2)}) collective-permute-start(bf16[16,288]{1,0:T(8,128)(2,1)S(1)} %get-tuple-element.52), channel_id=1, source_target_pairs={{0,12},{4,8},{8,4},{12,0},{1,13},{5,9},{9,5},{13,1},{2,14},{6,10},... | collective-permute-start | bytes 27656 | tf_op jit(solution)/shard_map/ppermute | solution.py:132
  55.2 0.0 collective-permute-done.18.refs_1_
  55.2 1.4 %collective-permute-done.19.refs_2_ = bf16[16,288]{1,0:T(8,128)(2,1)S(1)} collective-permute-done((bf16[16,288]{1,0:T(8,128)(2,1)S(1)}, bf16[16,288]{1,0:T(8,128)(2,1)S(1)}, u32[]{:S(2)}, u32[]{:S(2)}) %collective-permute-start.19) | collective-permute-done | bytes 9248 | tf_op jit(solution)/shard_map/ppermute | solution.py:132
  56.6 1.8 %collective-permute-done.20.refs_3_ = bf16[16,288]{1,0:T(8,128)(2,1)S(1)} collective-permute-done((bf16[16,288]{1,0:T(8,128)(2,1)S(1)}, bf16[16,288]{1,0:T(8,128)(2,1)S(1)}, u32[]{:S(2)}, u32[]{:S(2)}) %collective-permute-start.20) | collective-permute-done | bytes 9248 | tf_op jit(solution)/shard_map/ppermute | solution.py:132
  58.5 0.1 shard_map.81
  58.6 0.1 collective-permute-start.21
  58.7 1.2 %collective-permute-done.21.other = bf16[8,1152]{1,0:T(8,128)(2,1)S(1)} collective-permute-done((bf16[8,1152]{1,0:T(8,128)(2,1)S(1)}, bf16[8,1152]{1,0:T(8,128)(2,1)S(1)}, u32[]{:S(2)}, u32[]{:S(2)}) %collective-permute-start.21) | collective-permute-done | bytes 18464 | tf_op jit(solution)/shard_map/ppermute | solution.py:454
  59.8 0.6 %shard_map.82 = f32[1,8,1152]{2,1,0:T(8,128)} custom-call(bf16[8,1152]{1,0:T(8,128)(2,1)S(1)} %get-tuple-element.53.own, bf16[8,1152]{1,0:T(8,128)(2,1)S(1)} %collective-permute-done.21.other, bf16[8,1152]{1,0:T(8,128)(2,1)S(1)} %get-tuple-element.54.after), custom_call_target="tpu_custom_call" | custom-call | tf_op jit(solution)/shard_map/pallas_call | solution.py:114
  (3 shorter events, 0.0 us)
Async XLA Ops:
  0.0 19.8 %copy-start = (bf16[288,3,576]{2,0,1:T(8,128)(2,1)S(1)}, bf16[288,3,576]{2,0,1:T(8,128)(2,1)}, u32[]{:S(2)}) copy-start(bf16[288,3,576]{2,0,1:T(8,128)(2,1)} %param.12) | copy-start | bytes 2985988
  0.8 0.7 %copy-start.4 = (bf16[2,4,1152]{2,1,0:T(4,128)(2,1)S(1)}, bf16[2,4,1152]{2,1,0:T(4,128)(2,1)}, u32[]{:S(2)}) copy-start(bf16[2,4,1152]{2,1,0:T(4,128)(2,1)} %video_ref.1) | copy-start | bytes 55300
  1.8 5.7 %collective-permute-start = (bf16[16,288]{1,0:T(8,128)(2,1)S(1)}, bf16[16,288]{1,0:T(8,128)(2,1)S(1)}, u32[]{:S(2)}, u32[]{:S(2)}) collective-permute-start(bf16[16,288]{1,0:T(8,128)(2,1)S(1)} %get-tuple-element.31), channel_id=1, source_target_pairs={{0,4},{4,0},{8,12},{12,8},{1,5},{5,1},{9,13},{13,9},{2,6},{6,2},{1... | collective-permute-start | bytes 27656 | tf_op jit(solution)/shard_map/ppermute | solution.py:132
  4.9 4.6 %collective-permute-start.1 = (bf16[16,288]{1,0:T(8,128)(2,1)S(1)}, bf16[16,288]{1,0:T(8,128)(2,1)S(1)}, u32[]{:S(2)}, u32[]{:S(2)}) collective-permute-start(bf16[16,288]{1,0:T(8,128)(2,1)S(1)} %get-tuple-element.32), channel_id=1, source_target_pairs={{0,8},{4,12},{8,0},{12,4},{1,9},{5,13},{9,1},{13,5},{2,10},{6,14},... | collective-permute-start | bytes 27656 | tf_op jit(solution)/shard_map/ppermute | solution.py:132
  7.5 5.5 %collective-permute-start.2 = (bf16[16,288]{1,0:T(8,128)(2,1)S(1)}, bf16[16,288]{1,0:T(8,128)(2,1)S(1)}, u32[]{:S(2)}, u32[]{:S(2)}) collective-permute-start(bf16[16,288]{1,0:T(8,128)(2,1)S(1)} %get-tuple-element.33), channel_id=1, source_target_pairs={{0,12},{4,8},{8,4},{12,0},{1,13},{5,9},{9,5},{13,1},{2,14},{6,10},... | collective-permute-start | bytes 27656 | tf_op jit(solution)/shard_map/ppermute | solution.py:132
  13.0 1.2 %copy-start.1 = (bf16[288,3,576]{2,0,1:T(8,128)(2,1)S(1)}, bf16[288,3,576]{2,0,1:T(8,128)(2,1)}, u32[]{:S(2)}) copy-start(bf16[288,3,576]{2,0,1:T(8,128)(2,1)} %param.9) | copy-start | bytes 2985988
  14.2 15.7 %copy-start.2 = (bf16[288,576]{1,0:T(8,128)(2,1)S(1)}, bf16[288,576]{1,0:T(8,128)(2,1)}, u32[]{:S(2)}) copy-start(bf16[288,576]{1,0:T(8,128)(2,1)} %refs_4_.2) | copy-start | bytes 995332
  14.7 5.5 %collective-permute-start.3 = (bf16[3,8,576]{2,1,0:T(8,128)(2,1)S(1)}, bf16[3,8,576]{2,1,0:T(8,128)(2,1)S(1)}, u32[]{:S(2)}, u32[]{:S(2)}) collective-permute-start(bf16[3,8,576]{2,1,0:T(8,128)(2,1)S(1)} %get-tuple-element.35), channel_id=1, source_target_pairs={{0,4},{4,0},{8,12},{12,8},{1,5},{5,1},{9,13},{13,9},{2,6},{6,2},{1... | collective-permute-start | bytes 82952 | tf_op jit(solution)/shard_map/ppermute | solution.py:132
  14.8 5.4 %collective-permute-start.4 = (bf16[3,8,576]{2,1,0:T(8,128)(2,1)S(1)}, bf16[3,8,576]{2,1,0:T(8,128)(2,1)S(1)}, u32[]{:S(2)}, u32[]{:S(2)}) collective-permute-start(bf16[3,8,576]{2,1,0:T(8,128)(2,1)S(1)} %get-tuple-element.36), channel_id=1, source_target_pairs={{0,8},{4,12},{8,0},{12,4},{1,9},{5,13},{9,1},{13,5},{2,10},{6,14},... | collective-permute-start | bytes 82952 | tf_op jit(solution)/shard_map/ppermute | solution.py:132
  15.5 6.0 %collective-permute-start.5 = (bf16[3,8,576]{2,1,0:T(8,128)(2,1)S(1)}, bf16[3,8,576]{2,1,0:T(8,128)(2,1)S(1)}, u32[]{:S(2)}, u32[]{:S(2)}) collective-permute-start(bf16[3,8,576]{2,1,0:T(8,128)(2,1)S(1)} %get-tuple-element.37), channel_id=1, source_target_pairs={{0,12},{4,8},{8,4},{12,0},{1,13},{5,9},{9,5},{13,1},{2,14},{6,10},... | collective-permute-start | bytes 82952 | tf_op jit(solution)/shard_map/ppermute | solution.py:132
  20.2 30.4 %copy-start.3 = (bf16[288,576]{1,0:T(8,128)(2,1)S(1)}, bf16[288,576]{1,0:T(8,128)(2,1)}, u32[]{:S(2)}) copy-start(bf16[288,576]{1,0:T(8,128)(2,1)} %refs_4_.3) | copy-start | bytes 995332
  21.8 5.6 %collective-permute-start.8 = (bf16[16,576]{1,0:T(8,128)(2,1)S(1)}, bf16[16,576]{1,0:T(8,128)(2,1)S(1)}, u32[]{:S(2)}, u32[]{:S(2)}) collective-permute-start(bf16[16,576]{1,0:T(8,128)(2,1)S(1)} %shard_map.76.refs_0_.refs_4_), channel_id=1, source_target_pairs={{0,12},{4,8},{8,4},{12,0},{1,13},{5,9},{9,5},{13,1},{2,14},{6,10},... | collective-permute-start | bytes 55304 | tf_op jit(solution)/shard_map/ppermute | solution.py:132
  25.2 4.7 %collective-permute-start.7 = (bf16[16,576]{1,0:T(8,128)(2,1)S(1)}, bf16[16,576]{1,0:T(8,128)(2,1)S(1)}, u32[]{:S(2)}, u32[]{:S(2)}) collective-permute-start(bf16[16,576]{1,0:T(8,128)(2,1)S(1)} %shard_map.76.refs_0_.refs_4_), channel_id=1, source_target_pairs={{0,8},{4,12},{8,0},{12,4},{1,9},{5,13},{9,1},{13,5},{2,10},{6,14},... | collective-permute-start | bytes 55304 | tf_op jit(solution)/shard_map/ppermute | solution.py:132
  25.2 4.7 %collective-permute-start.6 = (bf16[16,576]{1,0:T(8,128)(2,1)S(1)}, bf16[16,576]{1,0:T(8,128)(2,1)S(1)}, u32[]{:S(2)}, u32[]{:S(2)}) collective-permute-start(bf16[16,576]{1,0:T(8,128)(2,1)S(1)} %shard_map.76.refs_0_.refs_4_), channel_id=1, source_target_pairs={{0,4},{4,0},{8,12},{12,8},{1,5},{5,1},{9,13},{13,9},{2,6},{6,2},{1... | collective-permute-start | bytes 55304 | tf_op jit(solution)/shard_map/ppermute | solution.py:132
  30.2 4.7 %collective-permute-start.10 = (bf16[32,288]{1,0:T(8,128)(2,1)S(1)}, bf16[32,288]{1,0:T(8,128)(2,1)S(1)}, u32[]{:S(2)}, u32[]{:S(2)}) collective-permute-start(bf16[32,288]{1,0:T(8,128)(2,1)S(1)} %get-tuple-element.41), channel_id=1, source_target_pairs={{0,2},{2,0},{1,3},{3,1},{4,6},{6,4},{5,7},{7,5},{8,10},{10,8},{9,1... | collective-permute-start | bytes 55304 | tf_op jit(solution)/shard_map/ppermute | solution.py:414
  31.8 3.1 %collective-permute-start.11 = (bf16[16,288]{1,0:T(8,128)(2,1)S(1)}, bf16[16,288]{1,0:T(8,128)(2,1)S(1)}, u32[]{:S(2)}, u32[]{:S(2)}) collective-permute-start(bf16[16,288]{1,0:T(8,128)(2,1)S(1)} %slice.3), channel_id=1, source_target_pairs={{0,3},{1,2},{2,1},{3,0},{4,7},{5,6},{6,5},{7,4},{8,11},{9,10},{10,... | collective-permute-start | bytes 27656 | tf_op jit(solution)/shard_map/ppermute | solution.py:415
  31.8 3.1 %collective-permute-start.9 = (bf16[16,288]{1,0:T(8,128)(2,1)S(1)}, bf16[16,288]{1,0:T(8,128)(2,1)S(1)}, u32[]{:S(2)}, u32[]{:S(2)}) collective-permute-start(bf16[16,288]{1,0:T(8,128)(2,1)S(1)} %get-tuple-element.40.refs_0_), channel_id=1, source_target_pairs={{0,1},{1,0},{2,3},{3,2},{4,5},{5,4},{6,7},{7,6},{8,9},{9,8},{10,11... | collective-permute-start | bytes 27656 | tf_op jit(solution)/shard_map/ppermute | solution.py:413
  35.3 4.5 %collective-permute-start.12 = (bf16[3,8,640]{2,1,0:T(8,128)(2,1)S(1)}, bf16[3,8,640]{2,1,0:T(8,128)(2,1)S(1)}, u32[]{:S(2)}, u32[]{:S(2)}) collective-permute-start(bf16[3,8,640]{2,1,0:T(8,128)(2,1)S(1)} %get-tuple-element.45), channel_id=1, source_target_pairs={{0,4},{4,0},{8,12},{12,8},{1,5},{5,1},{9,13},{13,9},{2,6},{6,2},{1... | collective-permute-start | bytes 92168 | tf_op jit(solution)/shard_map/ppermute | solution.py:132
  35.5 4.8 %collective-permute-start.13 = (bf16[3,8,640]{2,1,0:T(8,128)(2,1)S(1)}, bf16[3,8,640]{2,1,0:T(8,128)(2,1)S(1)}, u32[]{:S(2)}, u32[]{:S(2)}) collective-permute-start(bf16[3,8,640]{2,1,0:T(8,128)(2,1)S(1)} %get-tuple-element.46), channel_id=1, source_target_pairs={{0,8},{4,12},{8,0},{12,4},{1,9},{5,13},{9,1},{13,5},{2,10},{6,14},... | collective-permute-start | bytes 92168 | tf_op jit(solution)/shard_map/ppermute | solution.py:132
  37.5 5.7 %collective-permute-start.14 = (bf16[3,8,640]{2,1,0:T(8,128)(2,1)S(1)}, bf16[3,8,640]{2,1,0:T(8,128)(2,1)S(1)}, u32[]{:S(2)}, u32[]{:S(2)}) collective-permute-start(bf16[3,8,640]{2,1,0:T(8,128)(2,1)S(1)} %get-tuple-element.47), channel_id=1, source_target_pairs={{0,12},{4,8},{8,4},{12,0},{1,13},{5,9},{9,5},{13,1},{2,14},{6,10},... | collective-permute-start | bytes 92168 | tf_op jit(solution)/shard_map/ppermute | solution.py:132
  43.7 5.5 %collective-permute-start.17 = (bf16[8,576]{1,0:T(8,128)(2,1)S(1)}, bf16[8,576]{1,0:T(8,128)(2,1)S(1)}, u32[]{:S(2)}, u32[]{:S(2)}) collective-permute-start(bf16[8,576]{1,0:T(8,128)(2,1)S(1)} %shard_map.79.refs_0_), channel_id=1, source_target_pairs={{0,12},{4,8},{8,4},{12,0},{1,13},{5,9},{9,5},{13,1},{2,14},{6,10},... | collective-permute-start | bytes 27656 | tf_op jit(solution)/shard_map/ppermute | solution.py:132
  46.0 4.6 %collective-permute-start.16 = (bf16[8,576]{1,0:T(8,128)(2,1)S(1)}, bf16[8,576]{1,0:T(8,128)(2,1)S(1)}, u32[]{:S(2)}, u32[]{:S(2)}) collective-permute-start(bf16[8,576]{1,0:T(8,128)(2,1)S(1)} %shard_map.79.refs_0_), channel_id=1, source_target_pairs={{0,8},{4,12},{8,0},{12,4},{1,9},{5,13},{9,1},{13,5},{2,10},{6,14},... | collective-permute-start | bytes 27656 | tf_op jit(solution)/shard_map/ppermute | solution.py:132
  46.0 4.6 %collective-permute-start.15 = (bf16[8,576]{1,0:T(8,128)(2,1)S(1)}, bf16[8,576]{1,0:T(8,128)(2,1)S(1)}, u32[]{:S(2)}, u32[]{:S(2)}) collective-permute-start(bf16[8,576]{1,0:T(8,128)(2,1)S(1)} %shard_map.79.refs_0_), channel_id=1, source_target_pairs={{0,4},{4,0},{8,12},{12,8},{1,5},{5,1},{9,13},{13,9},{2,6},{6,2},{1... | collective-permute-start | bytes 27656 | tf_op jit(solution)/shard_map/ppermute | solution.py:132
  50.8 4.5 %collective-permute-start.18 = (bf16[16,288]{1,0:T(8,128)(2,1)S(1)}, bf16[16,288]{1,0:T(8,128)(2,1)S(1)}, u32[]{:S(2)}, u32[]{:S(2)}) collective-permute-start(bf16[16,288]{1,0:T(8,128)(2,1)S(1)} %get-tuple-element.50), channel_id=1, source_target_pairs={{0,4},{4,0},{8,12},{12,8},{1,5},{5,1},{9,13},{13,9},{2,6},{6,2},{1... | collective-permute-start | bytes 27656 | tf_op jit(solution)/shard_map/ppermute | solution.py:132
  52.1 4.6 %collective-permute-start.19 = (bf16[16,288]{1,0:T(8,128)(2,1)S(1)}, bf16[16,288]{1,0:T(8,128)(2,1)S(1)}, u32[]{:S(2)}, u32[]{:S(2)}) collective-permute-start(bf16[16,288]{1,0:T(8,128)(2,1)S(1)} %get-tuple-element.51), channel_id=1, source_target_pairs={{0,8},{4,12},{8,0},{12,4},{1,9},{5,13},{9,1},{13,5},{2,10},{6,14},... | collective-permute-start | bytes 27656 | tf_op jit(solution)/shard_map/ppermute | solution.py:132
  53.0 5.5 %collective-permute-start.20 = (bf16[16,288]{1,0:T(8,128)(2,1)S(1)}, bf16[16,288]{1,0:T(8,128)(2,1)S(1)}, u32[]{:S(2)}, u32[]{:S(2)}) collective-permute-start(bf16[16,288]{1,0:T(8,128)(2,1)S(1)} %get-tuple-element.52), channel_id=1, source_target_pairs={{0,12},{4,8},{8,4},{12,0},{1,13},{5,9},{9,5},{13,1},{2,14},{6,10},... | collective-permute-start | bytes 27656 | tf_op jit(solution)/shard_map/ppermute | solution.py:132
  58.6 1.3 %collective-permute-start.21 = (bf16[8,1152]{1,0:T(8,128)(2,1)S(1)}, bf16[8,1152]{1,0:T(8,128)(2,1)S(1)}, u32[]{:S(2)}, u32[]{:S(2)}) collective-permute-start(bf16[8,1152]{1,0:T(8,128)(2,1)S(1)} %get-tuple-element.53.own), channel_id=1, source_target_pairs={{0,1},{1,0},{2,3},{3,2},{4,5},{5,4},{6,7},{7,6},{8,9},{9,8},{10,11... | collective-permute-start | bytes 55304 | tf_op jit(solution)/shard_map/ppermute | solution.py:454

commit v3 on v2

--- a/solution.py
+++ b/solution.py
@@ -5,6 +5,8 @@
 from jax import lax
 from jax.experimental import pallas as pl
 from jax.experimental.pallas import tpu as pltpu
+
+
 from jax.sharding import PartitionSpec as P
 
 HEAD_WIDTH = 72
@@ -149,7 +151,7 @@
     mean = jnp.mean(x, axis=-1, keepdims=True)
     centred = x - mean
     spread = jnp.mean(centred * centred, axis=-1, keepdims=True)
-    y = centred * lax.rsqrt(spread + 1e-06) * gain_ref[...]
+    y = centred * lax.rsqrt(spread + 1e-06) * gain_ref[...].reshape(1, -1)
     for s in range(count):
         held[s, 0:rows] = lanes(y, s * share, share)
         held[s, rows:] = lanes(x, s * share, share)
@@ -182,7 +184,7 @@
     f, p = lax.axis_index("frame"), lax.axis_index("patch")
     share = gains.shape[2]
     for s in range(count):
-        gains[s] = jnp.broadcast_to(lanes(gain_ref[...], s * share, share), gains.shape[1:])
+        gains[s] = jnp.broadcast_to(lanes(gain_ref[...].reshape(1, -1), s * share, share), gains.shape[1:])
     g = gains[f]
     gain_own[...] = g
     g = g.astype(BF16)
@@ -233,7 +235,7 @@
 
 def out_time_body(count, *refs):
     parts, weight_ref, raw_other = refs[:count], refs[count], refs[count + 1]
-    own_ref, other_ref, tokens = refs[count + 2 :]
+    own_ref, other_ref, alone_ref, tokens = refs[count + 2 :]
     f, p = lax.axis_index("frame"), lax.axis_index("patch")
     rows = tokens.shape[0] // count
     for k in range(count):
@@ -248,6 +250,7 @@
     total = lax.dot_general(x, weight_ref[...], NT, preferred_element_type=F32)
     own_ref[...] = total[0:half].astype(BF16)
     other_ref[0:half] = total[half:].astype(BF16)
+    alone_ref[...] = total[half:].astype(BF16)
     other_ref[half:] = raw_other[...]
 
 
@@ -259,96 +262,79 @@
 
 def project_space_body(count, *refs):
     own, own_head, cross, cross_head, raw_own, gain_ref, weight_ref = refs[:7]
-    outs, after_ref, total = refs[7 : 7 + count], *refs[7 + count :]
+    outs, total = refs[7 : 7 + count], refs[7 + count]
     f, p = lax.axis_index("frame"), lax.axis_index("patch")
     half = own.shape[0]
     summed = own[...].astype(F32) + own_head[...].astype(F32)
     first = raw_own[...].astype(F32) + summed
-    summed = cross[0:half].astype(F32) + cross_head[0:half].astype(F32)
+    summed = cross[0:half].astype(F32) + cross_head[...].astype(F32)
     second = cross[half:].astype(F32) + summed
     low, high = jnp.where(p == 0, first, second), jnp.where(p == 0, second, first)
     places = half // count
     pieces = [v[i : i + places] for i in range(0, half, places) for v in (low, high)]
-    after_ref[...] = jnp.concatenate(pieces, axis=0).astype(BF16)
-    x = after_ref[...].astype(F32)
+    x = jnp.concatenate(pieces, axis=0).astype(BF16).astype(F32)
     mean = jnp.mean(x, axis=-1, keepdims=True)
     centred = x - mean
     square = jnp.sum(centred * centred, axis=-1, keepdims=True)
     y = (centred * gain_ref[0:1]).astype(BF16)
-    width = weight_ref.shape[2]
-    last = width // 128 * 128
-    for t in range(KINDS):
-        total[t, :, 0:width] = jnp.dot(y, weight_ref[t], preferred_element_type=F32)
-        tail = total[t, :, last:]
-        lane = lax.broadcasted_iota(jnp.int32, tail.shape, 1) - (width - last)
-        tail = jnp.where(lane < 0, tail, 0.0)
-        if t == 0:
-            for at, item in enumerate((*in_three(mean), *in_three(square))):
-                tail = jnp.where(lane == at, item, tail)
-        total[t, :, last:] = tail
-    rows = total.shape[1] // count
+    found = [jnp.dot(y, weight_ref[t], preferred_element_type=F32) for t in range(KINDS)]
+    spare = total.shape[1] - KINDS * weight_ref.shape[2] - x.shape[1]
+    lane = lax.broadcasted_iota(jnp.int32, (x.shape[0], spare), 1)
+    tail = jnp.zeros(lane.shape, F32)
+    for at, item in enumerate((*in_three(mean), *in_three(square))):
+        tail = jnp.where(lane == at, item, tail)
+    total[...] = jnp.concatenate([*found, x, tail], axis=1)
+    rows = total.shape[0] // count
     for k in range(count):
         place = pl.multiple_of((f ^ k) * rows, rows)
-        for t in range(KINDS):
-            outs[k][t] = total.at[t][pl.ds(place, rows), :].astype(BF16)
-
-
-def attend_space_body(count, share, *refs):
-    parts, fixed, out_ref = refs[:count], refs[count : 2 * count], refs[2 * count]
-    rows, width = out_ref.shape
-    last = width // 128 * 128
-    means, squares = [], []
-    for k in range(count):
-        tail = parts[k][0].astype(F32)[:, last:]
-        lane = lax.broadcasted_iota(jnp.int32, tail.shape, 1) - (width - last)
-        means.append(
-            jnp.sum(jnp.where((lane >= 0) & (lane < 3), tail, 0.0), axis=-1, keepdims=True)
-        )
-        squares.append(
-            jnp.sum(jnp.where((lane >= 3) & (lane < 6), tail, 0.0), axis=-1, keepdims=True)
-        )
+        outs[k][...] = total[pl.ds(place, rows), :].astype(BF16)
+
+
+def attend_space_body(count, *refs):
+    parts, fixed, refs = refs[:count], refs[count : 2 * count], refs[2 * count :]
+    weight_ref, partial_ref, after_ref, held = refs
+    f = lax.axis_index("frame")
+    rows, columns = parts[0].shape[0], weight_ref.shape[1]
+    share = weight_ref.shape[0] // count
+    messages = [part[...].astype(F32) for part in parts]
+    tails = [lanes(m, KINDS * columns + share, m.shape[1] - KINDS * columns - share) for m in messages]
+    lane = lax.broadcasted_iota(jnp.int32, tails[0].shape, 1)
+    means = [jnp.sum(jnp.where(lane < 3, t, 0.0), axis=-1, keepdims=True) for t in tails]
+    squares = [
+        jnp.sum(jnp.where((lane >= 3) & (lane < 6), t, 0.0), axis=-1, keepdims=True) for t in tails
+    ]
     mean = sum(means) / count
     square = sum(squares) + share * sum((m - mean) * (m - mean) for m in means)
     scale = lax.rsqrt(square / (share * count) + 1e-06)
+    total = sum(messages)
     qkv = []
     for t in range(KINDS):
-        total = jnp.zeros((rows, width), F32)
+        value = lanes(total, t * columns, columns)
         for k in range(count):
-            row = fixed[k][...].astype(F32)[rows + t : rows + t + 1]
-            total = total + parts[k][t].astype(F32)[:, 0:width] + (means[k] - mean) * row
-        qkv.append((total * scale).astype(BF16).astype(F32))
-    out_ref[...] = attend_rows(*qkv).astype(BF16)
-
-
-def out_space_body(count, *refs):
-    parts, weight_ref, after_ref = refs[:count], refs[count], refs[count + 1]
-    outs, (tokens, total, after) = refs[count + 2 : 2 * count + 2], refs[2 * count + 2 :]
-    f = lax.axis_index("frame")
-    rows = tokens.shape[0] // count
-    for k in range(count):
-        place = pl.multiple_of((f ^ k) * rows, rows)
-        tokens[pl.ds(place, rows), :] = parts[k][...].astype(F32)
-    total[...] = lax.dot_general(
-        tokens[...].astype(BF16), weight_ref[...], NT, preferred_element_type=F32
-    )
-    after[...] = after_ref[...].astype(F32)
-    for k in range(count):
-        place = pl.multiple_of((f ^ k) * rows, rows)
-        value = jnp.concatenate(
-            [total[pl.ds(place, rows), :], after[pl.ds(place, rows), :]], axis=0
-        )
-        outs[k][...] = value.astype(BF16)
-
-
-def join_body(count, *refs):
-    parts, partial_ref, after_ref, held = refs[:count], *refs[count:]
-    f = lax.axis_index("frame")
-    rows = partial_ref.shape[0]
-    for k in range(count):
-        held[f ^ k] = parts[k][...].astype(F32)
-    whole = jnp.concatenate([held[s] for s in range(count)], axis=1)
-    partial_ref[...] = whole[0:rows].astype(BF16)
-    after_ref[...] = whole[rows:].astype(BF16)
+            value = value + (means[k] - mean) * fixed[k][...].astype(F32)[rows + t : rows + t + 1]
+        qkv.append((value * scale).astype(BF16).astype(F32))
+    attended = attend_rows(*qkv).astype(BF16)
+    for k in range(count):
+        held[f ^ k] = lanes(messages[k], KINDS * columns, share)
+    partial_ref[...] = lax.dot_general(
+        attended, weight_ref[...], NT, preferred_element_type=F32
+    ).astype(BF16)
+    after_ref[...] = jnp.concatenate([held[s] for s in range(count)], axis=1).astype(BF16)
+
+
+def assemble_body(count, own, near, side, far, last, out_ref):
+    f, p, g = lax.axis_index("frame"), lax.axis_index("patch"), lax.axis_index("groups")
+    share, quarter = own.shape[0], own.shape[0] // 4
+    out_ref[pl.ds(pl.multiple_of(f * share, share), share), :] = own[...]
+    for k in range(1, count):
+        for piece, q in (
+            (near, 2 * p + g),
+            (side, 2 * (1 - p) + g),
+            (far, 2 * p + 1 - g),
+            (last, 2 * (1 - p) + 1 - g),
+        ):
+            place = pl.multiple_of((f ^ k) * share + q * quarter, quarter)
+            out_ref[pl.ds(place, quarter), :] = piece[(k - 1) * quarter : k * quarter]
 
 
 def finish_body(own, other, after, out_ref):
@@ -361,29 +347,34 @@
     share, columns = out_time.shape
     rows = frames_here * patches_here
     plane = rows * count
-    padded = (columns // 128 + 1) * 128
+    message = (KINDS * columns + share) // 128 * 128 + 128
     qkv_time, qkv_space = (jnp.transpose(w, (1, 0, 2)) for w in (qkv_time, qkv_space))
-    gain_time, gain_space = gain_time.reshape(1, width), gain_space.reshape(1, width)
     body = functools.partial
     swap = [(0, 1), (1, 0)]
 
-    normed = exchange(
-        run(
-            body(split_body, count),
-            [((2 * rows, share), BF16)] * count,
-            video,
-            gain_time,
-            scratch=[((count, 2 * rows, share), F32)],
-        )
-    )
-    partial_time = exchange(
-        run(
-            body(project_body, count),
-            [((KINDS, rows, columns), BF16)] * count,
-            *normed,
-            qkv_time,
-            scratch=[((plane, share), F32), ((KINDS, plane, columns), F32)],
-        )
+    normed = run(
+        body(split_body, count),
+        [((2 * rows, share), BF16)] * count,
+        video,
+        gain_time,
+        scratch=[((count, 2 * rows, share), F32)],
+    )
+    normed = exchange(normed)
+    partial_time = run(
+        body(project_body, count),
+        [((KINDS, rows, columns), BF16)] * count,
+        *normed,
+        qkv_time,
+        scratch=[((plane, share), F32), ((KINDS, plane, columns), F32)],
+    )
+    partial_time = exchange(partial_time)
+    quarter = 2 * lax.axis_index("patch") + lax.axis_index("groups")
+    piece = lax.dynamic_slice_in_dim(out_space, quarter * (share // 4), share // 4)
+    near = jnp.concatenate(exchange([piece] * count)[1:], axis=0)
+    side = lax.ppermute(near, "patch", swap)
+    far, last = (lax.ppermute(v, "groups", swap) for v in (near, side))
+    whole_space = run(
+        body(assemble_body, count), ((width, columns), BF16), out_space, near, side, far, last
     )
     fixed, gain_own, raw_own, raw_other = run(
         body(prepare_body, count),
@@ -402,9 +393,9 @@
         body(attend_time_body, count), ((rows + 8, columns), BF16), *partial_time, fixed
     )
     attended = exchange([attended] * count)
-    own, cross = run(
+    own, cross, cross_only = run(
         body(out_time_body, count),
-        [((plane // 2, share), BF16), ((plane, share), BF16)],
+        [((plane // 2, share), BF16), ((plane, share), BF16), ((plane // 2, share), BF16)],
         *attended,
         out_time,
         raw_other,
@@ -412,12 +403,10 @@
     )
     own_head = lax.ppermute(own, "head", swap)
     crossed = lax.ppermute(cross, "patch", swap)
-    cross_head = lax.ppermute(
-        cross[: plane // 2], ("patch", "head"), [(i, 3 - i) for i in range(4)]
-    )
-    *partial_space, after = run(
+    cross_head = lax.ppermute(cross_only, ("patch", "head"), [(i, 3 - i) for i in range(4)])
+    partial_space = run(
         body(project_space_body, count),
-        [((KINDS, rows, padded), BF16)] * count + [((plane, share), BF16)],
+        [((rows, message), BF16)] * count,
         own,
         own_head,
         crossed,
@@ -425,31 +414,16 @@
         raw_own,
         gain_own,
         qkv_space,
-        scratch=[((KINDS, plane, padded), F32)],
+        scratch=[((plane, message), F32)],
     )
     partial_space = exchange(partial_space)
-    frame = run(
-        body(attend_space_body, count, share),
-        ((rows, columns), BF16),
+    mine, after = run(
+        body(attend_space_body, count),
+        [((rows, width), BF16)] * 2,
         *partial_space,
         *attended,
-    )
-    frame = exchange([frame] * count)
-    pieces = exchange(
-        run(
-            body(out_space_body, count),
-            [((2 * rows, share), BF16)] * count,
-            *frame,
-            out_space,
-            after,
-            scratch=[((plane, columns), F32), ((plane, share), F32), ((plane, share), F32)],
-        )
-    )
-    mine, after = run(
-        body(join_body, count),
-        [((rows, width), BF16)] * 2,
-        *pieces,
-        scratch=[((count, 2 * rows, share), F32)],
+        whole_space,
+        scratch=[((count, rows, share), F32)],
     )
     theirs = lax.ppermute(mine, "head", swap)
     return run(finish_body, ((1, rows, width), F32), mine, theirs, after)
@@ -472,6 +446,7 @@
         small = (
             patches_here == count
             and frames_here == lax.axis_size("patch") == lax.axis_size("head") == 2
+            and lax.axis_size("groups") == 2
             and frames_here * patches_here == 8
             and frames_here * count * patches_here < width
         )

time: 60.7 us -> 67.7 us (1.12)
  waiting for transfers between devices: 23.2 us -> 29 us
    ppermute x1 -> x4, starting transfers between devices: 0.01 us -> 4.6 us  [the longest x2 3.04 us: moving_tokens(): far, last = (lax.ppermute(v, 'groups', swap) for v in (near, side))]
    ppermute x18 -> x15, starting transfers between devices: 27.9 us -> 23.8 us  [exchange(): lax.ppermute(messages[k], 'frame', [(i, i ^ k) for i in range(count)])]
    ppermute x1 -> x4, waiting for transfers between devices: 2.47 us -> 5.99 us  [the longest x1 3.51 us: moving_tokens(): side = lax.ppermute(near, 'patch', swap)]
    ppermute x18 -> x15, waiting for transfers between devices: 19.6 us -> 21.8 us  [exchange(): lax.ppermute(messages[k], 'frame', [(i, i ^ k) for i in range(count)])]
    reshape x2 -> x0, local copies, waits for them, and re-layouts: 1.49 us -> none  [the longest x1 0.79 us: moving_tokens(): gain_time.reshape(1, width)]
    dynamic_slice x0 -> x1, local copies, waits for them, and re-layouts: none -> 0.99 us  [moving_tokens(): lax.dynamic_slice_in_dim(out_space, quarter * (share // 4), share // 4)]
    unnamed x10 -> x16, local copies, waits for them, and re-layouts: 1.98 us -> 2.71 us
    pallas_call x10 -> x9, Pallas kernels: 3.53 us -> 3.98 us  [run(): pl.pallas_call(body, out_shape=shapes, in_specs=[vmem] * len(args), out_s...]
  transfers between devices with their start and end apart: 22 -> 22, of which waited for: 13 -> 13; matrix products, arithmetic and copies ran while one was open for 1% -> 0% of each run, Pallas kernels for 1% -> 3%
where the time goes in v3:
time: 67.7 us; the launch traced here: 67.5 us
  starting transfers between devices  30.6 us (45%)
  waiting for transfers between devices  29 us (43%)
  Pallas kernels  3.98 us (6%)
  local copies, waits for them, and re-layouts  3.71 us (5%)
    ppermute x15, starting transfers between devices, exchange(): lax.ppermute(messages[k], 'frame', [(i, i ^ k) for i in range(count)])  23.8 us
    ppermute x15, waiting for transfers between devices, exchange(): lax.ppermute(messages[k], 'frame', [(i, i ^ k) for i in range(count)])  21.8 us
    pallas_call x9, Pallas kernels, run(): pl.pallas_call(body, out_shape=shapes, in_specs=[vmem] * len(args), out_s...  3.98 us
    ppermute x1, waiting for transfers between devices, moving_tokens(): side = lax.ppermute(near, 'patch', swap)  3.51 us
    ppermute x2, starting transfers between devices, moving_tokens(): far, last = (lax.ppermute(v, 'groups', swap) for v in (near, side))  3.04 us
    unnamed x16, local copies, waits for them, and re-layouts  2.71 us
    ppermute x1, waiting for transfers between devices, moving_tokens(): lax.ppermute(cross_only, ('patch', 'head'), [(i, 3 - i) for i in range(4)])  2.47 us
    ppermute x1, starting transfers between devices, moving_tokens(): crossed = lax.ppermute(cross, 'patch', swap)  1.56 us
  transfers between devices with their start and end apart: 22, of which 13 were waited for; matrix products, arithmetic and copies ran while one was open for 0% of the time, Pallas kernels for 3%

profile of v3, /device:TPU:0, one launch (start us, length us, event | category | flops | bytes accessed | tf_op | source)
XLA Modules:
  0.0 67.5 jit_solution(13367437301404065552)
XLA Ops:
  0.0 0.0 copy-start
  0.0 1.0 %constant_dynamic-slice_fusion = bf16[72,576]{1,0:T(8,128)(2,1)S(1)} fusion(bf16[288,576]{1,0:T(8,128)(2,1)} %own.1, s32[]{:T(128)S(6)} %select_n.3), kind=kLoop, calls=%fused_computation.3 | loop fusion | bytes 165892 | tf_op jit(solution)/shard_map/dynamic_slice | solution.py:372
  1.0 3.1 %collective-permute-start.15 = (bf16[72,576]{1,0:T(8,128)(2,1)S(1)}, bf16[72,576]{1,0:T(8,128)(2,1)S(1)}, u32[]{:S(2)}, u32[]{:S(2)}) collective-permute-start(bf16[72,576]{1,0:T(8,128)(2,1)S(1)} %constant_dynamic-slice_fusion), channel_id=1, source_target_pairs={{0,4},{4,0},{8,12},{12,8},{1,5},{5,1},{9,13},{13,9},{2,6},{6,2},{1... | collective-permute-start | bytes 248840 | tf_op jit(solution)/shard_map/ppermute | solution.py:134
  4.1 2.6 %collective-permute-start.16 = (bf16[72,576]{1,0:T(8,128)(2,1)S(1)}, bf16[72,576]{1,0:T(8,128)(2,1)S(1)}, u32[]{:S(2)}, u32[]{:S(2)}) collective-permute-start(bf16[72,576]{1,0:T(8,128)(2,1)S(1)} %constant_dynamic-slice_fusion), channel_id=1, source_target_pairs={{0,8},{4,12},{8,0},{12,4},{1,9},{5,13},{9,1},{13,5},{2,10},{6,14},... | collective-permute-start | bytes 248840 | tf_op jit(solution)/shard_map/ppermute | solution.py:134
  6.7 0.0 collective-permute-start.17
  6.7 0.1 collective-permute-done.15
  6.8 7.3 %collective-permute-done.16 = bf16[72,576]{1,0:T(8,128)(2,1)S(1)} collective-permute-done((bf16[72,576]{1,0:T(8,128)(2,1)S(1)}, bf16[72,576]{1,0:T(8,128)(2,1)S(1)}, u32[]{:S(2)}, u32[]{:S(2)}) %collective-permute-start.16) | collective-permute-done | bytes 82976 | tf_op jit(solution)/shard_map/ppermute | solution.py:134
  14.1 0.0 collective-permute-done.17
  14.1 1.6 %collective-permute-start.18 = (bf16[216,576]{1,0:T(8,128)(2,1)S(1)}, bf16[216,576]{1,0:T(8,128)(2,1)S(1)}, u32[]{:S(2)}, u32[]{:S(2)}) collective-permute-start(bf16[216,576]{1,0:T(8,128)(2,1)S(1)} %constant_dynamic-update-slice_fusion.near), channel_id=1, source_target_pairs={{0,2},{2,0},{1,3},{3,1},{4,6},{6,4},{5,7},{7,5},{8,10},{10,8},{9,1... | collective-permute-start | bytes 746504 | tf_op jit(solution)/shard_map/ppermute | solution.py:374
  15.7 1.5 %collective-permute-start.19 = (bf16[216,576]{1,0:T(8,128)(2,1)S(1)}, bf16[216,576]{1,0:T(8,128)(2,1)S(1)}, u32[]{:S(2)}, u32[]{:S(2)}) collective-permute-start(bf16[216,576]{1,0:T(8,128)(2,1)S(1)} %constant_dynamic-update-slice_fusion.near), channel_id=1, source_target_pairs={{0,16},{16,0},{1,17},{17,1},{2,18},{18,2},{3,19},{19,3},{4,20},{20... | collective-permute-start | bytes 746504 | tf_op jit(solution)/shard_map/ppermute | solution.py:375
  17.2 3.5 %collective-permute-done.18.side = bf16[216,576]{1,0:T(8,128)(2,1)S(1)} collective-permute-done((bf16[216,576]{1,0:T(8,128)(2,1)S(1)}, bf16[216,576]{1,0:T(8,128)(2,1)S(1)}, u32[]{:S(2)}, u32[]{:S(2)}) %collective-permute-start.18) | collective-permute-done | bytes 248864 | tf_op jit(solution)/shard_map/ppermute | solution.py:374
  20.7 1.5 %collective-permute-start.20 = (bf16[216,576]{1,0:T(8,128)(2,1)S(1)}, bf16[216,576]{1,0:T(8,128)(2,1)S(1)}, u32[]{:S(2)}, u32[]{:S(2)}) collective-permute-start(bf16[216,576]{1,0:T(8,128)(2,1)S(1)} %collective-permute-done.18.side), channel_id=1, source_target_pairs={{0,16},{16,0},{1,17},{17,1},{2,18},{18,2},{3,19},{19,3},{4,20},{20... | collective-permute-start | bytes 746504 | tf_op jit(solution)/shard_map/ppermute | solution.py:375
  22.2 0.0 copy-start.4
  22.2 0.7 %copy-done.4 = bf16[2,4,1152]{2,1,0:T(4,128)(2,1)S(1)} copy-done((bf16[2,4,1152]{2,1,0:T(4,128)(2,1)S(1)}, bf16[2,4,1152]{2,1,0:T(4,128)(2,1)}, u32[]{:S(2)}) %copy-start.4) | copy-done | bytes 18456
  23.0 0.7 %copy-done.6 = f32[1152]{0:T(1024)S(1)} copy-done((f32[1152]{0:T(1024)S(1)}, f32[1152]{0:T(1024)}, u32[]{:S(2)}) %copy-start.6) | copy-done | bytes 4632
  23.6 0.3 shard_map.73
  23.9 2.4 %collective-permute-start = (bf16[16,288]{1,0:T(8,128)(2,1)S(1)}, bf16[16,288]{1,0:T(8,128)(2,1)S(1)}, u32[]{:S(2)}, u32[]{:S(2)}) collective-permute-start(bf16[16,288]{1,0:T(8,128)(2,1)S(1)} %get-tuple-element.27), channel_id=1, source_target_pairs={{0,4},{4,0},{8,12},{12,8},{1,5},{5,1},{9,13},{13,9},{2,6},{6,2},{1... | collective-permute-start | bytes 27656 | tf_op jit(solution)/shard_map/ppermute | solution.py:134
  26.3 1.0 %collective-permute-start.1 = (bf16[16,288]{1,0:T(8,128)(2,1)S(1)}, bf16[16,288]{1,0:T(8,128)(2,1)S(1)}, u32[]{:S(2)}, u32[]{:S(2)}) collective-permute-start(bf16[16,288]{1,0:T(8,128)(2,1)S(1)} %get-tuple-element.28), channel_id=1, source_target_pairs={{0,8},{4,12},{8,0},{12,4},{1,9},{5,13},{9,1},{13,5},{2,10},{6,14},... | collective-permute-start | bytes 27656 | tf_op jit(solution)/shard_map/ppermute | solution.py:134
  27.3 1.4 %collective-permute-start.2 = (bf16[16,288]{1,0:T(8,128)(2,1)S(1)}, bf16[16,288]{1,0:T(8,128)(2,1)S(1)}, u32[]{:S(2)}, u32[]{:S(2)}) collective-permute-start(bf16[16,288]{1,0:T(8,128)(2,1)S(1)} %get-tuple-element.29), channel_id=1, source_target_pairs={{0,12},{4,8},{8,4},{12,0},{1,13},{5,9},{9,5},{13,1},{2,14},{6,10},... | collective-permute-start | bytes 27656 | tf_op jit(solution)/shard_map/ppermute | solution.py:134
  28.7 0.0 collective-permute-done.refs_1_
  28.7 2.2 %collective-permute-done.1.refs_2_ = bf16[16,288]{1,0:T(8,128)(2,1)S(1)} collective-permute-done((bf16[16,288]{1,0:T(8,128)(2,1)S(1)}, bf16[16,288]{1,0:T(8,128)(2,1)S(1)}, u32[]{:S(2)}, u32[]{:S(2)}) %collective-permute-start.1) | collective-permute-done | bytes 9248 | tf_op jit(solution)/shard_map/ppermute | solution.py:134
  30.9 1.9 %collective-permute-done.2.refs_3_ = bf16[16,288]{1,0:T(8,128)(2,1)S(1)} collective-permute-done((bf16[16,288]{1,0:T(8,128)(2,1)S(1)}, bf16[16,288]{1,0:T(8,128)(2,1)S(1)}, u32[]{:S(2)}, u32[]{:S(2)}) %collective-permute-start.2) | collective-permute-done | bytes 9248 | tf_op jit(solution)/shard_map/ppermute | solution.py:134
  32.8 1.2 %copy-done.1 = bf16[288,3,576]{2,0,1:T(8,128)(2,1)S(1)} copy-done((bf16[288,3,576]{2,0,1:T(8,128)(2,1)S(1)}, bf16[288,3,576]{2,0,1:T(8,128)(2,1)}, u32[]{:S(2)}) %copy-start.1) | copy-done | bytes 995352
  34.0 0.4 shard_map.74
  34.5 0.2 collective-permute-start.3
  34.7 1.8 %collective-permute-start.4 = (bf16[3,8,576]{2,1,0:T(8,128)(2,1)S(1)}, bf16[3,8,576]{2,1,0:T(8,128)(2,1)S(1)}, u32[]{:S(2)}, u32[]{:S(2)}) collective-permute-start(bf16[3,8,576]{2,1,0:T(8,128)(2,1)S(1)} %get-tuple-element.32), channel_id=1, source_target_pairs={{0,8},{4,12},{8,0},{12,4},{1,9},{5,13},{9,1},{13,5},{2,10},{6,14},... | collective-permute-start | bytes 82952 | tf_op jit(solution)/shard_map/ppermute | solution.py:134
  36.5 2.4 %collective-permute-start.5 = (bf16[3,8,576]{2,1,0:T(8,128)(2,1)S(1)}, bf16[3,8,576]{2,1,0:T(8,128)(2,1)S(1)}, u32[]{:S(2)}, u32[]{:S(2)}) collective-permute-start(bf16[3,8,576]{2,1,0:T(8,128)(2,1)S(1)} %get-tuple-element.33), channel_id=1, source_target_pairs={{0,12},{4,8},{8,4},{12,0},{1,13},{5,9},{9,5},{13,1},{2,14},{6,10},... | collective-permute-start | bytes 82952 | tf_op jit(solution)/shard_map/ppermute | solution.py:134
  38.9 0.0 copy-done
  38.9 0.0 copy-done.5
  39.0 0.3 shard_map.75
  39.3 0.0 copy-start.2
  39.3 0.0 collective-permute-done.3.refs_1_
  39.3 0.2 collective-permute-done.4.refs_2_
  39.5 2.9 %collective-permute-done.5.refs_3_ = bf16[3,8,576]{2,1,0:T(8,128)(2,1)S(1)} collective-permute-done((bf16[3,8,576]{2,1,0:T(8,128)(2,1)S(1)}, bf16[3,8,576]{2,1,0:T(8,128)(2,1)S(1)}, u32[]{:S(2)}, u32[]{:S(2)}) %collective-permute-start.5) | collective-permute-done | bytes 27680 | tf_op jit(solution)/shard_map/ppermute | solution.py:134
  42.4 0.4 shard_map.76.refs_0_.refs_4_
  42.8 0.0 collective-permute-start.6
  42.8 2.8 %collective-permute-start.7 = (bf16[16,576]{1,0:T(8,128)(2,1)S(1)}, bf16[16,576]{1,0:T(8,128)(2,1)S(1)}, u32[]{:S(2)}, u32[]{:S(2)}) collective-permute-start(bf16[16,576]{1,0:T(8,128)(2,1)S(1)} %shard_map.76.refs_0_.refs_4_), channel_id=1, source_target_pairs={{0,8},{4,12},{8,0},{12,4},{1,9},{5,13},{9,1},{13,5},{2,10},{6,14},... | collective-permute-start | bytes 55304 | tf_op jit(solution)/shard_map/ppermute | solution.py:134
  45.6 1.6 %collective-permute-start.8 = (bf16[16,576]{1,0:T(8,128)(2,1)S(1)}, bf16[16,576]{1,0:T(8,128)(2,1)S(1)}, u32[]{:S(2)}, u32[]{:S(2)}) collective-permute-start(bf16[16,576]{1,0:T(8,128)(2,1)S(1)} %shard_map.76.refs_0_.refs_4_), channel_id=1, source_target_pairs={{0,12},{4,8},{8,4},{12,0},{1,13},{5,9},{9,5},{13,1},{2,14},{6,10},... | collective-permute-start | bytes 55304 | tf_op jit(solution)/shard_map/ppermute | solution.py:134
  47.2 0.0 collective-permute-done.6.refs_1_.refs_5_
  47.2 0.3 collective-permute-done.7.refs_2_.refs_6_
  47.5 3.7 %collective-permute-done.8.refs_3_.refs_7_ = bf16[16,576]{1,0:T(8,128)(2,1)S(1)} collective-permute-done((bf16[16,576]{1,0:T(8,128)(2,1)S(1)}, bf16[16,576]{1,0:T(8,128)(2,1)S(1)}, u32[]{:S(2)}, u32[]{:S(2)}) %collective-permute-start.8) | collective-permute-done | bytes 18464 | tf_op jit(solution)/shard_map/ppermute | solution.py:134
  51.2 0.0 copy-done.3
  51.2 0.3 shard_map.77
  51.5 1.6 %collective-permute-start.10 = (bf16[32,288]{1,0:T(8,128)(2,1)S(1)}, bf16[32,288]{1,0:T(8,128)(2,1)S(1)}, u32[]{:S(2)}, u32[]{:S(2)}) collective-permute-start(bf16[32,288]{1,0:T(8,128)(2,1)S(1)} %get-tuple-element.37), channel_id=1, source_target_pairs={{0,2},{2,0},{1,3},{3,1},{4,6},{6,4},{5,7},{7,5},{8,10},{10,8},{9,1... | collective-permute-start | bytes 55304 | tf_op jit(solution)/shard_map/ppermute | solution.py:405
  53.1 0.0 collective-permute-start.11
  53.1 0.6 collective-permute-start.9
  53.7 2.5 %collective-permute-done.11.refs_3_ = bf16[16,288]{1,0:T(8,128)(2,1)S(1)} collective-permute-done((bf16[16,288]{1,0:T(8,128)(2,1)S(1)}, bf16[16,288]{1,0:T(8,128)(2,1)S(1)}, u32[]{:S(2)}, u32[]{:S(2)}) %collective-permute-start.11) | collective-permute-done | bytes 9248 | tf_op jit(solution)/shard_map/ppermute | solution.py:406
  56.2 0.0 collective-permute-done.9.refs_1_
  56.2 0.0 collective-permute-done.10.refs_2_
  56.2 0.4 shard_map.78
  56.6 0.1 collective-permute-start.12
  56.7 2.1 %collective-permute-start.13 = (bf16[8,2048]{1,0:T(8,128)(2,1)S(1)}, bf16[8,2048]{1,0:T(8,128)(2,1)S(1)}, u32[]{:S(2)}, u32[]{:S(2)}) collective-permute-start(bf16[8,2048]{1,0:T(8,128)(2,1)S(1)} %get-tuple-element.43), channel_id=1, source_target_pairs={{0,8},{4,12},{8,0},{12,4},{1,9},{5,13},{9,1},{13,5},{2,10},{6,14},... | collective-permute-start | bytes 98312 | tf_op jit(solution)/shard_map/ppermute | solution.py:134
  58.8 2.3 %collective-permute-start.14 = (bf16[8,2048]{1,0:T(8,128)(2,1)S(1)}, bf16[8,2048]{1,0:T(8,128)(2,1)S(1)}, u32[]{:S(2)}, u32[]{:S(2)}) collective-permute-start(bf16[8,2048]{1,0:T(8,128)(2,1)S(1)} %get-tuple-element.44), channel_id=1, source_target_pairs={{0,12},{4,8},{8,4},{12,0},{1,13},{5,9},{9,5},{13,1},{2,14},{6,10},... | collective-permute-start | bytes 98312 | tf_op jit(solution)/shard_map/ppermute | solution.py:134
  61.1 0.0 collective-permute-done.19.far
  61.1 0.0 collective-permute-done.20.last
  61.1 0.0 copy-done.2
  61.1 0.1 shard_map.79.refs_8_
  61.2 0.0 collective-permute-done.12.refs_1_
  61.2 0.3 collective-permute-done.13.refs_2_
  61.6 2.9 %collective-permute-done.14.refs_3_ = bf16[8,2048]{1,0:T(8,128)(2,1)S(1)} collective-permute-done((bf16[8,2048]{1,0:T(8,128)(2,1)S(1)}, bf16[8,2048]{1,0:T(8,128)(2,1)S(1)}, u32[]{:S(2)}, u32[]{:S(2)}) %collective-permute-start.14) | collective-permute-done | bytes 32800 | tf_op jit(solution)/shard_map/ppermute | solution.py:134
  64.5 1.1 %shard_map.80 = (bf16[8,1152]{1,0:T(8,128)(2,1)S(1)}, bf16[8,1152]{1,0:T(8,128)(2,1)S(1)}) custom-call(bf16[8,2048]{1,0:T(8,128)(2,1)S(1)} %get-tuple-element.41.refs_0_, bf16[8,2048]{1,0:T(8,128)(2,1)S(1)} %collective-permute-done.12.refs_1_, bf16[8,2048]{1,0:T(8,128)(2,1)S(1)} %collective-permute-done.13.refs_2_, ...), custom_call_target="tpu_custom_call" | custom-call | tf_op jit(solution)/shard_map/pallas_call | solution.py:116
  65.6 0.0 collective-permute-start.21
  65.6 1.2 %collective-permute-done.21.other = bf16[8,1152]{1,0:T(8,128)(2,1)S(1)} collective-permute-done((bf16[8,1152]{1,0:T(8,128)(2,1)S(1)}, bf16[8,1152]{1,0:T(8,128)(2,1)S(1)}, u32[]{:S(2)}, u32[]{:S(2)}) %collective-permute-start.21) | collective-permute-done | bytes 18464 | tf_op jit(solution)/shard_map/ppermute | solution.py:428
  66.9 0.6 shard_map.81
  (7 shorter events, 0.0 us)
Async XLA Ops:
  0.0 38.9 %copy-start = (bf16[288,3,576]{2,0,1:T(8,128)(2,1)S(1)}, bf16[288,3,576]{2,0,1:T(8,128)(2,1)}, u32[]{:S(2)}) copy-start(bf16[288,3,576]{2,0,1:T(8,128)(2,1)} %param.12) | copy-start | bytes 2985988
  1.0 5.8 %collective-permute-start.15 = (bf16[72,576]{1,0:T(8,128)(2,1)S(1)}, bf16[72,576]{1,0:T(8,128)(2,1)S(1)}, u32[]{:S(2)}, u32[]{:S(2)}) collective-permute-start(bf16[72,576]{1,0:T(8,128)(2,1)S(1)} %constant_dynamic-slice_fusion), channel_id=1, source_target_pairs={{0,4},{4,0},{8,12},{12,8},{1,5},{5,1},{9,13},{13,9},{2,6},{6,2},{1... | collective-permute-start | bytes 248840 | tf_op jit(solution)/shard_map/ppermute | solution.py:134
  4.1 10.0 %collective-permute-start.16 = (bf16[72,576]{1,0:T(8,128)(2,1)S(1)}, bf16[72,576]{1,0:T(8,128)(2,1)S(1)}, u32[]{:S(2)}, u32[]{:S(2)}) collective-permute-start(bf16[72,576]{1,0:T(8,128)(2,1)S(1)} %constant_dynamic-slice_fusion), channel_id=1, source_target_pairs={{0,8},{4,12},{8,0},{12,4},{1,9},{5,13},{9,1},{13,5},{2,10},{6,14},... | collective-permute-start | bytes 248840 | tf_op jit(solution)/shard_map/ppermute | solution.py:134
  6.7 7.4 %collective-permute-start.17 = (bf16[72,576]{1,0:T(8,128)(2,1)S(1)}, bf16[72,576]{1,0:T(8,128)(2,1)S(1)}, u32[]{:S(2)}, u32[]{:S(2)}) collective-permute-start(bf16[72,576]{1,0:T(8,128)(2,1)S(1)} %constant_dynamic-slice_fusion), channel_id=1, source_target_pairs={{0,12},{4,8},{8,4},{12,0},{1,13},{5,9},{9,5},{13,1},{2,14},{6,10},... | collective-permute-start | bytes 248840 | tf_op jit(solution)/shard_map/ppermute | solution.py:134
  14.1 6.6 %collective-permute-start.18 = (bf16[216,576]{1,0:T(8,128)(2,1)S(1)}, bf16[216,576]{1,0:T(8,128)(2,1)S(1)}, u32[]{:S(2)}, u32[]{:S(2)}) collective-permute-start(bf16[216,576]{1,0:T(8,128)(2,1)S(1)} %constant_dynamic-update-slice_fusion.near), channel_id=1, source_target_pairs={{0,2},{2,0},{1,3},{3,1},{4,6},{6,4},{5,7},{7,5},{8,10},{10,8},{9,1... | collective-permute-start | bytes 746504 | tf_op jit(solution)/shard_map/ppermute | solution.py:374
  15.7 45.4 %collective-permute-start.19 = (bf16[216,576]{1,0:T(8,128)(2,1)S(1)}, bf16[216,576]{1,0:T(8,128)(2,1)S(1)}, u32[]{:S(2)}, u32[]{:S(2)}) collective-permute-start(bf16[216,576]{1,0:T(8,128)(2,1)S(1)} %constant_dynamic-update-slice_fusion.near), channel_id=1, source_target_pairs={{0,16},{16,0},{1,17},{17,1},{2,18},{18,2},{3,19},{19,3},{4,20},{20... | collective-permute-start | bytes 746504 | tf_op jit(solution)/shard_map/ppermute | solution.py:375
  20.7 40.4 %collective-permute-start.20 = (bf16[216,576]{1,0:T(8,128)(2,1)S(1)}, bf16[216,576]{1,0:T(8,128)(2,1)S(1)}, u32[]{:S(2)}, u32[]{:S(2)}) collective-permute-start(bf16[216,576]{1,0:T(8,128)(2,1)S(1)} %collective-permute-done.18.side), channel_id=1, source_target_pairs={{0,16},{16,0},{1,17},{17,1},{2,18},{18,2},{3,19},{19,3},{4,20},{20... | collective-permute-start | bytes 746504 | tf_op jit(solution)/shard_map/ppermute | solution.py:375
  22.2 0.7 %copy-start.4 = (bf16[2,4,1152]{2,1,0:T(4,128)(2,1)S(1)}, bf16[2,4,1152]{2,1,0:T(4,128)(2,1)}, u32[]{:S(2)}) copy-start(bf16[2,4,1152]{2,1,0:T(4,128)(2,1)} %video_ref.1) | copy-start | bytes 55300
  22.9 0.7 %copy-start.6 = (f32[1152]{0:T(1024)S(1)}, f32[1152]{0:T(1024)}, u32[]{:S(2)}) copy-start(f32[1152]{0:T(1024)} %gain_ref.1) | copy-start | bytes 13828
  23.9 4.8 %collective-permute-start = (bf16[16,288]{1,0:T(8,128)(2,1)S(1)}, bf16[16,288]{1,0:T(8,128)(2,1)S(1)}, u32[]{:S(2)}, u32[]{:S(2)}) collective-permute-start(bf16[16,288]{1,0:T(8,128)(2,1)S(1)} %get-tuple-element.27), channel_id=1, source_target_pairs={{0,4},{4,0},{8,12},{12,8},{1,5},{5,1},{9,13},{13,9},{2,6},{6,2},{1... | collective-permute-start | bytes 27656 | tf_op jit(solution)/shard_map/ppermute | solution.py:134
  26.3 4.6 %collective-permute-start.1 = (bf16[16,288]{1,0:T(8,128)(2,1)S(1)}, bf16[16,288]{1,0:T(8,128)(2,1)S(1)}, u32[]{:S(2)}, u32[]{:S(2)}) collective-permute-start(bf16[16,288]{1,0:T(8,128)(2,1)S(1)} %get-tuple-element.28), channel_id=1, source_target_pairs={{0,8},{4,12},{8,0},{12,4},{1,9},{5,13},{9,1},{13,5},{2,10},{6,14},... | collective-permute-start | bytes 27656 | tf_op jit(solution)/shard_map/ppermute | solution.py:134
  27.3 5.5 %collective-permute-start.2 = (bf16[16,288]{1,0:T(8,128)(2,1)S(1)}, bf16[16,288]{1,0:T(8,128)(2,1)S(1)}, u32[]{:S(2)}, u32[]{:S(2)}) collective-permute-start(bf16[16,288]{1,0:T(8,128)(2,1)S(1)} %get-tuple-element.29), channel_id=1, source_target_pairs={{0,12},{4,8},{8,4},{12,0},{1,13},{5,9},{9,5},{13,1},{2,14},{6,10},... | collective-permute-start | bytes 27656 | tf_op jit(solution)/shard_map/ppermute | solution.py:134
  32.8 1.2 %copy-start.1 = (bf16[288,3,576]{2,0,1:T(8,128)(2,1)S(1)}, bf16[288,3,576]{2,0,1:T(8,128)(2,1)}, u32[]{:S(2)}) copy-start(bf16[288,3,576]{2,0,1:T(8,128)(2,1)} %param.9) | copy-start | bytes 2985988
  34.0 4.9 %copy-start.5 = (f32[1152]{0:T(1024)S(1)}, f32[1152]{0:T(1024)}, u32[]{:S(2)}) copy-start(f32[1152]{0:T(1024)} %refs_4_.2) | copy-start | bytes 13828
  34.0 17.2 %copy-start.3 = (bf16[288,576]{1,0:T(8,128)(2,1)S(1)}, bf16[288,576]{1,0:T(8,128)(2,1)}, u32[]{:S(2)}) copy-start(bf16[288,576]{1,0:T(8,128)(2,1)} %refs_4_.3) | copy-start | bytes 995332
  34.5 4.8 %collective-permute-start.3 = (bf16[3,8,576]{2,1,0:T(8,128)(2,1)S(1)}, bf16[3,8,576]{2,1,0:T(8,128)(2,1)S(1)}, u32[]{:S(2)}, u32[]{:S(2)}) collective-permute-start(bf16[3,8,576]{2,1,0:T(8,128)(2,1)S(1)} %get-tuple-element.31), channel_id=1, source_target_pairs={{0,4},{4,0},{8,12},{12,8},{1,5},{5,1},{9,13},{13,9},{2,6},{6,2},{1... | collective-permute-start | bytes 82952 | tf_op jit(solution)/shard_map/ppermute | solution.py:134
  34.7 4.8 %collective-permute-start.4 = (bf16[3,8,576]{2,1,0:T(8,128)(2,1)S(1)}, bf16[3,8,576]{2,1,0:T(8,128)(2,1)S(1)}, u32[]{:S(2)}, u32[]{:S(2)}) collective-permute-start(bf16[3,8,576]{2,1,0:T(8,128)(2,1)S(1)} %get-tuple-element.32), channel_id=1, source_target_pairs={{0,8},{4,12},{8,0},{12,4},{1,9},{5,13},{9,1},{13,5},{2,10},{6,14},... | collective-permute-start | bytes 82952 | tf_op jit(solution)/shard_map/ppermute | solution.py:134
  36.5 5.9 %collective-permute-start.5 = (bf16[3,8,576]{2,1,0:T(8,128)(2,1)S(1)}, bf16[3,8,576]{2,1,0:T(8,128)(2,1)S(1)}, u32[]{:S(2)}, u32[]{:S(2)}) collective-permute-start(bf16[3,8,576]{2,1,0:T(8,128)(2,1)S(1)} %get-tuple-element.33), channel_id=1, source_target_pairs={{0,12},{4,8},{8,4},{12,0},{1,13},{5,9},{9,5},{13,1},{2,14},{6,10},... | collective-permute-start | bytes 82952 | tf_op jit(solution)/shard_map/ppermute | solution.py:134
  39.3 21.8 %copy-start.2 = (bf16[288,576]{1,0:T(8,128)(2,1)S(1)}, bf16[288,576]{1,0:T(8,128)(2,1)}, u32[]{:S(2)}) copy-start(bf16[288,576]{1,0:T(8,128)(2,1)} %own.1) | copy-start | bytes 995332
  42.8 4.4 %collective-permute-start.6 = (bf16[16,576]{1,0:T(8,128)(2,1)S(1)}, bf16[16,576]{1,0:T(8,128)(2,1)S(1)}, u32[]{:S(2)}, u32[]{:S(2)}) collective-permute-start(bf16[16,576]{1,0:T(8,128)(2,1)S(1)} %shard_map.76.refs_0_.refs_4_), channel_id=1, source_target_pairs={{0,4},{4,0},{8,12},{12,8},{1,5},{5,1},{9,13},{13,9},{2,6},{6,2},{1... | collective-permute-start | bytes 55304 | tf_op jit(solution)/shard_map/ppermute | solution.py:134
  42.8 4.7 %collective-permute-start.7 = (bf16[16,576]{1,0:T(8,128)(2,1)S(1)}, bf16[16,576]{1,0:T(8,128)(2,1)S(1)}, u32[]{:S(2)}, u32[]{:S(2)}) collective-permute-start(bf16[16,576]{1,0:T(8,128)(2,1)S(1)} %shard_map.76.refs_0_.refs_4_), channel_id=1, source_target_pairs={{0,8},{4,12},{8,0},{12,4},{1,9},{5,13},{9,1},{13,5},{2,10},{6,14},... | collective-permute-start | bytes 55304 | tf_op jit(solution)/shard_map/ppermute | solution.py:134
  45.6 5.6 %collective-permute-start.8 = (bf16[16,576]{1,0:T(8,128)(2,1)S(1)}, bf16[16,576]{1,0:T(8,128)(2,1)S(1)}, u32[]{:S(2)}, u32[]{:S(2)}) collective-permute-start(bf16[16,576]{1,0:T(8,128)(2,1)S(1)} %shard_map.76.refs_0_.refs_4_), channel_id=1, source_target_pairs={{0,12},{4,8},{8,4},{12,0},{1,13},{5,9},{9,5},{13,1},{2,14},{6,10},... | collective-permute-start | bytes 55304 | tf_op jit(solution)/shard_map/ppermute | solution.py:134
  51.5 4.7 %collective-permute-start.10 = (bf16[32,288]{1,0:T(8,128)(2,1)S(1)}, bf16[32,288]{1,0:T(8,128)(2,1)S(1)}, u32[]{:S(2)}, u32[]{:S(2)}) collective-permute-start(bf16[32,288]{1,0:T(8,128)(2,1)S(1)} %get-tuple-element.37), channel_id=1, source_target_pairs={{0,2},{2,0},{1,3},{3,1},{4,6},{6,4},{5,7},{7,5},{8,10},{10,8},{9,1... | collective-permute-start | bytes 55304 | tf_op jit(solution)/shard_map/ppermute | solution.py:405
  53.1 3.1 %collective-permute-start.11 = (bf16[16,288]{1,0:T(8,128)(2,1)S(1)}, bf16[16,288]{1,0:T(8,128)(2,1)S(1)}, u32[]{:S(2)}, u32[]{:S(2)}) collective-permute-start(bf16[16,288]{1,0:T(8,128)(2,1)S(1)} %get-tuple-element.38), channel_id=1, source_target_pairs={{0,3},{1,2},{2,1},{3,0},{4,7},{5,6},{6,5},{7,4},{8,11},{9,10},{10,... | collective-permute-start | bytes 27656 | tf_op jit(solution)/shard_map/ppermute | solution.py:406
  53.1 3.1 %collective-permute-start.9 = (bf16[16,288]{1,0:T(8,128)(2,1)S(1)}, bf16[16,288]{1,0:T(8,128)(2,1)S(1)}, u32[]{:S(2)}, u32[]{:S(2)}) collective-permute-start(bf16[16,288]{1,0:T(8,128)(2,1)S(1)} %get-tuple-element.36.refs_0_), channel_id=1, source_target_pairs={{0,1},{1,0},{2,3},{3,2},{4,5},{5,4},{6,7},{7,6},{8,9},{9,8},{10,11... | collective-permute-start | bytes 27656 | tf_op jit(solution)/shard_map/ppermute | solution.py:404
  56.6 4.6 %collective-permute-start.12 = (bf16[8,2048]{1,0:T(8,128)(2,1)S(1)}, bf16[8,2048]{1,0:T(8,128)(2,1)S(1)}, u32[]{:S(2)}, u32[]{:S(2)}) collective-permute-start(bf16[8,2048]{1,0:T(8,128)(2,1)S(1)} %get-tuple-element.42), channel_id=1, source_target_pairs={{0,4},{4,0},{8,12},{12,8},{1,5},{5,1},{9,13},{13,9},{2,6},{6,2},{1... | collective-permute-start | bytes 98312 | tf_op jit(solution)/shard_map/ppermute | solution.py:134
  56.7 4.9 %collective-permute-start.13 = (bf16[8,2048]{1,0:T(8,128)(2,1)S(1)}, bf16[8,2048]{1,0:T(8,128)(2,1)S(1)}, u32[]{:S(2)}, u32[]{:S(2)}) collective-permute-start(bf16[8,2048]{1,0:T(8,128)(2,1)S(1)} %get-tuple-element.43), channel_id=1, source_target_pairs={{0,8},{4,12},{8,0},{12,4},{1,9},{5,13},{9,1},{13,5},{2,10},{6,14},... | collective-permute-start | bytes 98312 | tf_op jit(solution)/shard_map/ppermute | solution.py:134
  58.8 5.7 %collective-permute-start.14 = (bf16[8,2048]{1,0:T(8,128)(2,1)S(1)}, bf16[8,2048]{1,0:T(8,128)(2,1)S(1)}, u32[]{:S(2)}, u32[]{:S(2)}) collective-permute-start(bf16[8,2048]{1,0:T(8,128)(2,1)S(1)} %get-tuple-element.44), channel_id=1, source_target_pairs={{0,12},{4,8},{8,4},{12,0},{1,13},{5,9},{9,5},{13,1},{2,14},{6,10},... | collective-permute-start | bytes 98312 | tf_op jit(solution)/shard_map/ppermute | solution.py:134
  65.6 1.2 %collective-permute-start.21 = (bf16[8,1152]{1,0:T(8,128)(2,1)S(1)}, bf16[8,1152]{1,0:T(8,128)(2,1)S(1)}, u32[]{:S(2)}, u32[]{:S(2)}) collective-permute-start(bf16[8,1152]{1,0:T(8,128)(2,1)S(1)} %get-tuple-element.45.own), channel_id=1, source_target_pairs={{0,1},{1,0},{2,3},{3,2},{4,5},{5,4},{6,7},{7,6},{8,9},{9,8},{10,11... | collective-permute-start | bytes 55304 | tf_op jit(solution)/shard_map/ppermute | solution.py:428

commit v4 on v3

--- a/solution.py
+++ b/solution.py
@@ -109,16 +109,17 @@
 NT = (((1,), (1,)), ((), ()))
 
 
-def run(body, outs, *args, scratch=()):
+def run(body, outs, *args, scratch=(), sems=0):
     vmem = pl.BlockSpec(memory_space=pltpu.VMEM)
     single = not isinstance(outs, list)
     shapes = [jax.ShapeDtypeStruct(*o) for o in ([outs] if single else outs)]
     found = pl.pallas_call(
         body,
         out_shape=shapes,
-        in_specs=[vmem] * len(args),
+        in_specs=[pl.BlockSpec(memory_space=pltpu.HBM) if sems else vmem] * len(args),
         out_specs=[vmem] * len(shapes),
-        scratch_shapes=[pltpu.VMEM(*s) for s in scratch],
+        scratch_shapes=[pltpu.VMEM(*s) for s in scratch]
+        + [pltpu.SemaphoreType.DMA((sems,))] * (sems > 0),
         compiler_params=pltpu.CompilerParams(vmem_limit_bytes=16 << 20),
     )(*args)
     return found[0] if single else found
@@ -130,10 +131,11 @@
 
 def exchange(messages):
     count = len(messages)
-    return [messages[0]] + [
-        lax.ppermute(messages[k], "frame", [(i, i ^ k) for i in range(count)])
-        for k in range(1, count)
-    ]
+    found = [messages[0]]
+    for k in range(1, count):
+        pairs = [(i, i ^ k) for i in range(count)]
+        found.append(lax.ppermute(messages[k], "frame", pairs))
+    return found
 
 
 def pick_rows(value, source):
@@ -142,9 +144,17 @@
     return jnp.dot(chosen, value.astype(BF16), preferred_element_type=F32)
 
 
-def split_body(count, video_ref, gain_ref, *refs):
-    outs, held = refs[:count], refs[count]
+def split_body(count, video_hbm, gain_hbm, *refs):
+    outs, (held, video_ref, gain_ref, sems) = refs[:count], refs[count:]
     f = lax.axis_index("frame")
+    copies = [
+        pltpu.make_async_copy(video_hbm, video_ref, sems.at[0]),
+        pltpu.make_async_copy(gain_hbm, gain_ref, sems.at[1]),
+    ]
+    for copy in copies:
+        copy.start()
+    for copy in copies:
+        copy.wait()
     rows = video_ref.shape[0] * video_ref.shape[1]
     share = held.shape[2]
     x = jnp.concatenate([video_ref[i].astype(F32) for i in range(video_ref.shape[0])], axis=0)
@@ -157,6 +167,20 @@
         held[s, rows:] = lanes(x, s * share, share)
     for k in range(count):
         outs[k][...] = held[f ^ k].astype(BF16)
+
+
+def load_body(weight_ref, rows_ref, held_ref, piece_ref, sems):
+    quarter = 2 * lax.axis_index("patch") + lax.axis_index("groups")
+    size = piece_ref.shape[0]
+    place = pl.multiple_of(quarter * size, size)
+    copies = [
+        pltpu.make_async_copy(rows_ref.at[pl.ds(place, size), :], piece_ref, sems.at[0]),
+        pltpu.make_async_copy(weight_ref, held_ref, sems.at[1]),
+    ]
+    for copy in copies:
+        copy.start()
+    for copy in copies:
+        copy.wait()
 
 
 def project_body(count, *refs):
@@ -316,17 +340,16 @@
     attended = attend_rows(*qkv).astype(BF16)
     for k in range(count):
         held[f ^ k] = lanes(messages[k], KINDS * columns, share)
-    partial_ref[...] = lax.dot_general(
-        attended, weight_ref[...], NT, preferred_element_type=F32
-    ).astype(BF16)
+    partial = lax.dot_general(attended, weight_ref[...], NT, preferred_element_type=F32)
+    partial_ref[...] = partial.astype(BF16)
     after_ref[...] = jnp.concatenate([held[s] for s in range(count)], axis=1).astype(BF16)
 
 
-def assemble_body(count, own, near, side, far, last, out_ref):
+def assemble_body(order, own, near, side, far, last, out_ref):
     f, p, g = lax.axis_index("frame"), lax.axis_index("patch"), lax.axis_index("groups")
     share, quarter = own.shape[0], own.shape[0] // 4
     out_ref[pl.ds(pl.multiple_of(f * share, share), share), :] = own[...]
-    for k in range(1, count):
+    for at, k in enumerate(order):
         for piece, q in (
             (near, 2 * p + g),
             (side, 2 * (1 - p) + g),
@@ -334,7 +357,7 @@
             (last, 2 * (1 - p) + 1 - g),
         ):
             place = pl.multiple_of((f ^ k) * share + q * quarter, quarter)
-            out_ref[pl.ds(place, quarter), :] = piece[(k - 1) * quarter : k * quarter]
+            out_ref[pl.ds(place, quarter), :] = piece[at * quarter : (at + 1) * quarter]
 
 
 def finish_body(own, other, after, out_ref):
@@ -357,9 +380,17 @@
         [((2 * rows, share), BF16)] * count,
         video,
         gain_time,
-        scratch=[((count, 2 * rows, share), F32)],
+        scratch=[((count, 2 * rows, share), F32), (video.shape, BF16), ((width,), F32)],
+        sems=2,
     )
     normed = exchange(normed)
+    qkv_time, piece = run(
+        load_body,
+        [(qkv_time.shape, BF16), ((share // 4, columns), BF16)],
+        qkv_time,
+        out_space,
+        sems=2,
+    )
     partial_time = run(
         body(project_body, count),
         [((KINDS, rows, columns), BF16)] * count,
@@ -368,13 +399,19 @@
         scratch=[((plane, share), F32), ((KINDS, plane, columns), F32)],
     )
     partial_time = exchange(partial_time)
-    quarter = 2 * lax.axis_index("patch") + lax.axis_index("groups")
-    piece = lax.dynamic_slice_in_dim(out_space, quarter * (share // 4), share // 4)
-    near = jnp.concatenate(exchange([piece] * count)[1:], axis=0)
+    near, order = piece, [0]
+    for stage in range(count.bit_length() - 1):
+        hop = count >> (stage + 1)
+        pairs = [(i, i ^ hop) for i in range(count)]
+        near = jnp.concatenate([near, lax.ppermute(near, "frame", pairs)], axis=0)
+        order += [k ^ hop for k in order]
+    near = near[share // 4 :]
     side = lax.ppermute(near, "patch", swap)
-    far, last = (lax.ppermute(v, "groups", swap) for v in (near, side))
+    far = []
+    for value in (near, side):
+        far.append(lax.ppermute(value, "groups", swap))
     whole_space = run(
-        body(assemble_body, count), ((width, columns), BF16), out_space, near, side, far, last
+        body(assemble_body, order[1:]), ((width, columns), BF16), out_space, near, side, *far
     )
     fixed, gain_own, raw_own, raw_other = run(
         body(prepare_body, count),

time: 67.7 us -> 69.5 us (1.027)
  waiting for transfers between devices: 29 us -> 31.5 us
  local copies, waits for them, and re-layouts: 3.71 us -> 2.3 us
    ppermute x17 -> x16, waiting for transfers between devices: 21.9 us -> 24.1 us  [the longest x12 14.6 us: exchange(): found.append(lax.ppermute(messages[k], 'frame', pairs))]
    dynamic_slice x1 -> x0, local copies, waits for them, and re-layouts: 0.99 us -> none  [moving_tokens(): lax.dynamic_slice_in_dim(out_space, quarter * (share // 4), share // 4)]
    unnamed x16 -> x17, local copies, waits for them, and re-layouts: 2.71 us -> 2.27 us
    ppermute x17 -> x16, starting transfers between devices: 26.8 us -> 27.2 us  [the longest x12 19.2 us: exchange(): found.append(lax.ppermute(messages[k], 'frame', pairs))]
    pallas_call x9 -> x10, Pallas kernels: 3.98 us -> 4.28 us  [run(): pl.pallas_call(body, out_shape=shapes, in_specs=[pl.BlockSpec(memory_spac...]
  transfers between devices with their start and end apart: 22 -> 21, of which waited for: 13 -> 13; matrix products, arithmetic and copies ran while one was open for 0% -> 0% of each run, Pallas kernels for 3% -> 3%
where the time goes in v4:
time: 69.5 us; the launch traced here: 69.3 us
  waiting for transfers between devices  31.5 us (45%)
  starting transfers between devices  31 us (45%)
  Pallas kernels  4.28 us (6%)
  local copies, waits for them, and re-layouts  2.3 us (3%)
    ppermute x12, starting transfers between devices, exchange(): found.append(lax.ppermute(messages[k], 'frame', pairs))  19.2 us
    ppermute x12, waiting for transfers between devices, exchange(): found.append(lax.ppermute(messages[k], 'frame', pairs))  14.6 us
    ppermute x2, waiting for transfers between devices, moving_tokens(): near = jnp.concatenate([near, lax.ppermute(near, 'frame', pairs)], axis=0)  9.44 us
    ppermute x2, starting transfers between devices, moving_tokens(): near = jnp.concatenate([near, lax.ppermute(near, 'frame', pairs)], axis=0)  4.92 us
    pallas_call x10, Pallas kernels, run(): pl.pallas_call(body, out_shape=shapes, in_specs=[pl.BlockSpec(memory_spac...  4.28 us
    ppermute x1, waiting for transfers between devices, moving_tokens(): side = lax.ppermute(near, 'patch', swap)  3.76 us
    ppermute x2, starting transfers between devices, moving_tokens(): far.append(lax.ppermute(value, 'groups', swap))  3.04 us
    ppermute x1, waiting for transfers between devices, moving_tokens(): lax.ppermute(cross_only, ('patch', 'head'), [(i, 3 - i) for i in range(4)])  2.47 us
  transfers between devices with their start and end apart: 21, of which 13 were waited for; matrix products, arithmetic and copies ran while one was open for 0% of the time, Pallas kernels for 3%

profile of v4, /device:TPU:0, one launch (start us, length us, event | category | flops | bytes accessed | tf_op | source)
XLA Modules:
  0.0 69.3 jit_solution(3157884155980763948)
XLA Ops:
  0.0 0.0 copy-start.1
  0.0 1.0 %copy-done.1 = bf16[288,576]{1,0:T(8,128)(2,1)S(1)} copy-done((bf16[288,576]{1,0:T(8,128)(2,1)S(1)}, bf16[288,576]{1,0:T(8,128)(2,1)}, u32[]{:S(2)}) %copy-start.1) | copy-done | bytes 331800
  1.0 1.2 %copy-done.3 = bf16[288,3,576]{2,0,1:T(8,128)(2,1)S(1)} copy-done((bf16[288,3,576]{2,0,1:T(8,128)(2,1)S(1)}, bf16[288,3,576]{2,0,1:T(8,128)(2,1)}, u32[]{:S(2)}) %copy-start.3) | copy-done | bytes 995352
  2.2 0.3 shard_map.74
  2.5 0.0 copy-start
  2.5 0.0 copy-start.6
  2.5 4.1 %collective-permute-start.15 = (bf16[72,576]{1,0:T(8,128)(2,1)S(1)}, bf16[72,576]{1,0:T(8,128)(2,1)S(1)}, u32[]{:S(2)}, u32[]{:S(2)}) collective-permute-start(bf16[72,576]{1,0:T(8,128)(2,1)S(1)} %get-tuple-element.48), channel_id=1, source_target_pairs={{0,8},{4,12},{8,0},{12,4},{1,9},{5,13},{9,1},{13,5},{2,10},{6,14},... | collective-permute-start | bytes 248840 | tf_op jit(solution)/shard_map/ppermute | solution.py:406
  6.7 4.6 %collective-permute-done.15 = bf16[72,576]{1,0:T(8,128)(2,1)S(1)} collective-permute-done((bf16[72,576]{1,0:T(8,128)(2,1)S(1)}, bf16[72,576]{1,0:T(8,128)(2,1)S(1)}, u32[]{:S(2)}, u32[]{:S(2)}) %collective-permute-start.15) | collective-permute-done | bytes 82976 | tf_op jit(solution)/shard_map/ppermute | solution.py:406
  11.3 0.8 %collective-permute-start.16 = (bf16[144,576]{1,0:T(8,128)(2,1)S(1)}, bf16[144,576]{1,0:T(8,128)(2,1)S(1)}, u32[]{:S(2)}, u32[]{:S(2)}) collective-permute-start(bf16[144,576]{1,0:T(8,128)(2,1)S(1)} %pad_maximum_fusion), channel_id=1, source_target_pairs={{0,4},{4,0},{8,12},{12,8},{1,5},{5,1},{9,13},{13,9},{2,6},{6,2},{1... | collective-permute-start | bytes 497672 | tf_op jit(solution)/shard_map/ppermute | solution.py:406
  12.1 4.8 %collective-permute-done.16 = bf16[144,576]{1,0:T(8,128)(2,1)S(1)} collective-permute-done((bf16[144,576]{1,0:T(8,128)(2,1)S(1)}, bf16[144,576]{1,0:T(8,128)(2,1)S(1)}, u32[]{:S(2)}, u32[]{:S(2)}) %collective-permute-start.16) | collective-permute-done | bytes 165920 | tf_op jit(solution)/shard_map/ppermute | solution.py:406
  17.0 1.6 %collective-permute-start.17 = (bf16[216,576]{1,0:T(8,128)(2,1)S(1)}, bf16[216,576]{1,0:T(8,128)(2,1)S(1)}, u32[]{:S(2)}, u32[]{:S(2)}) collective-permute-start(bf16[216,576]{1,0:T(8,128)(2,1)S(1)} %constant_dynamic-update-slice_fusion.near), channel_id=1, source_target_pairs={{0,2},{2,0},{1,3},{3,1},{4,6},{6,4},{5,7},{7,5},{8,10},{10,8},{9,1... | collective-permute-start | bytes 746504 | tf_op jit(solution)/shard_map/ppermute | solution.py:409
  18.6 1.5 %collective-permute-start.18 = (bf16[216,576]{1,0:T(8,128)(2,1)S(1)}, bf16[216,576]{1,0:T(8,128)(2,1)S(1)}, u32[]{:S(2)}, u32[]{:S(2)}) collective-permute-start(bf16[216,576]{1,0:T(8,128)(2,1)S(1)} %constant_dynamic-update-slice_fusion.near), channel_id=1, source_target_pairs={{0,16},{16,0},{1,17},{17,1},{2,18},{18,2},{3,19},{19,3},{4,20},{20... | collective-permute-start | bytes 746504 | tf_op jit(solution)/shard_map/ppermute | solution.py:412
  20.1 3.8 %collective-permute-done.17.side = bf16[216,576]{1,0:T(8,128)(2,1)S(1)} collective-permute-done((bf16[216,576]{1,0:T(8,128)(2,1)S(1)}, bf16[216,576]{1,0:T(8,128)(2,1)S(1)}, u32[]{:S(2)}, u32[]{:S(2)}) %collective-permute-start.17) | collective-permute-done | bytes 248864 | tf_op jit(solution)/shard_map/ppermute | solution.py:409
  23.9 1.5 %collective-permute-start.19 = (bf16[216,576]{1,0:T(8,128)(2,1)S(1)}, bf16[216,576]{1,0:T(8,128)(2,1)S(1)}, u32[]{:S(2)}, u32[]{:S(2)}) collective-permute-start(bf16[216,576]{1,0:T(8,128)(2,1)S(1)} %collective-permute-done.17.side), channel_id=1, source_target_pairs={{0,16},{16,0},{1,17},{17,1},{2,18},{18,2},{3,19},{19,3},{4,20},{20... | collective-permute-start | bytes 746504 | tf_op jit(solution)/shard_map/ppermute | solution.py:412
  25.4 0.0 copy-done.5
  25.4 0.0 copy-done.7
  25.4 0.3 shard_map.73
  25.7 2.5 %collective-permute-start = (bf16[16,288]{1,0:T(8,128)(2,1)S(1)}, bf16[16,288]{1,0:T(8,128)(2,1)S(1)}, u32[]{:S(2)}, u32[]{:S(2)}) collective-permute-start(bf16[16,288]{1,0:T(8,128)(2,1)S(1)} %get-tuple-element.29), channel_id=1, source_target_pairs={{0,4},{4,0},{8,12},{12,8},{1,5},{5,1},{9,13},{13,9},{2,6},{6,2},{1... | collective-permute-start | bytes 27656 | tf_op jit(solution)/shard_map/ppermute | solution.py:137
  28.3 3.4 %collective-permute-start.1 = (bf16[16,288]{1,0:T(8,128)(2,1)S(1)}, bf16[16,288]{1,0:T(8,128)(2,1)S(1)}, u32[]{:S(2)}, u32[]{:S(2)}) collective-permute-start(bf16[16,288]{1,0:T(8,128)(2,1)S(1)} %get-tuple-element.30), channel_id=1, source_target_pairs={{0,8},{4,12},{8,0},{12,4},{1,9},{5,13},{9,1},{13,5},{2,10},{6,14},... | collective-permute-start | bytes 27656 | tf_op jit(solution)/shard_map/ppermute | solution.py:137
  31.6 0.0 collective-permute-start.2
  31.6 0.0 collective-permute-done.refs_1_
  31.6 1.7 %collective-permute-done.1.refs_2_ = bf16[16,288]{1,0:T(8,128)(2,1)S(1)} collective-permute-done((bf16[16,288]{1,0:T(8,128)(2,1)S(1)}, bf16[16,288]{1,0:T(8,128)(2,1)S(1)}, u32[]{:S(2)}, u32[]{:S(2)}) %collective-permute-start.1) | collective-permute-done | bytes 9248 | tf_op jit(solution)/shard_map/ppermute | solution.py:137
  33.3 3.8 %collective-permute-done.2.refs_3_ = bf16[16,288]{1,0:T(8,128)(2,1)S(1)} collective-permute-done((bf16[16,288]{1,0:T(8,128)(2,1)S(1)}, bf16[16,288]{1,0:T(8,128)(2,1)S(1)}, u32[]{:S(2)}, u32[]{:S(2)}) %collective-permute-start.2) | collective-permute-done | bytes 9248 | tf_op jit(solution)/shard_map/ppermute | solution.py:137
  37.1 0.4 shard_map.75
  37.6 0.1 collective-permute-start.3
  37.7 0.8 %collective-permute-start.4 = (bf16[3,8,576]{2,1,0:T(8,128)(2,1)S(1)}, bf16[3,8,576]{2,1,0:T(8,128)(2,1)S(1)}, u32[]{:S(2)}, u32[]{:S(2)}) collective-permute-start(bf16[3,8,576]{2,1,0:T(8,128)(2,1)S(1)} %get-tuple-element.35), channel_id=1, source_target_pairs={{0,8},{4,12},{8,0},{12,4},{1,9},{5,13},{9,1},{13,5},{2,10},{6,14},... | collective-permute-start | bytes 82952 | tf_op jit(solution)/shard_map/ppermute | solution.py:137
  38.4 3.6 %collective-permute-start.5 = (bf16[3,8,576]{2,1,0:T(8,128)(2,1)S(1)}, bf16[3,8,576]{2,1,0:T(8,128)(2,1)S(1)}, u32[]{:S(2)}, u32[]{:S(2)}) collective-permute-start(bf16[3,8,576]{2,1,0:T(8,128)(2,1)S(1)} %get-tuple-element.36), channel_id=1, source_target_pairs={{0,12},{4,8},{8,4},{12,0},{1,13},{5,9},{9,5},{13,1},{2,14},{6,10},... | collective-permute-start | bytes 82952 | tf_op jit(solution)/shard_map/ppermute | solution.py:137
  42.0 0.0 copy-done
  42.0 0.0 copy-done.6
  42.0 0.3 shard_map.76
  42.4 0.0 copy-start.2
  42.4 0.0 collective-permute-done.3.refs_1_
  42.4 0.1 collective-permute-done.4.refs_2_
  42.5 2.1 %collective-permute-done.5.refs_3_ = bf16[3,8,576]{2,1,0:T(8,128)(2,1)S(1)} collective-permute-done((bf16[3,8,576]{2,1,0:T(8,128)(2,1)S(1)}, bf16[3,8,576]{2,1,0:T(8,128)(2,1)S(1)}, u32[]{:S(2)}, u32[]{:S(2)}) %collective-permute-start.5) | collective-permute-done | bytes 27680 | tf_op jit(solution)/shard_map/ppermute | solution.py:137
  44.6 0.4 shard_map.77.refs_0_.refs_4_
  45.0 3.4 %collective-permute-start.8 = (bf16[16,576]{1,0:T(8,128)(2,1)S(1)}, bf16[16,576]{1,0:T(8,128)(2,1)S(1)}, u32[]{:S(2)}, u32[]{:S(2)}) collective-permute-start(bf16[16,576]{1,0:T(8,128)(2,1)S(1)} %shard_map.77.refs_0_.refs_4_), channel_id=1, source_target_pairs={{0,12},{4,8},{8,4},{12,0},{1,13},{5,9},{9,5},{13,1},{2,14},{6,10},... | collective-permute-start | bytes 55304 | tf_op jit(solution)/shard_map/ppermute | solution.py:137
  48.4 0.0 collective-permute-start.7
  48.4 1.0 %collective-permute-start.6 = (bf16[16,576]{1,0:T(8,128)(2,1)S(1)}, bf16[16,576]{1,0:T(8,128)(2,1)S(1)}, u32[]{:S(2)}, u32[]{:S(2)}) collective-permute-start(bf16[16,576]{1,0:T(8,128)(2,1)S(1)} %shard_map.77.refs_0_.refs_4_), channel_id=1, source_target_pairs={{0,4},{4,0},{8,12},{12,8},{1,5},{5,1},{9,13},{13,9},{2,6},{6,2},{1... | collective-permute-start | bytes 55304 | tf_op jit(solution)/shard_map/ppermute | solution.py:137
  49.4 1.2 %collective-permute-done.8.refs_3_.refs_7_ = bf16[16,576]{1,0:T(8,128)(2,1)S(1)} collective-permute-done((bf16[16,576]{1,0:T(8,128)(2,1)S(1)}, bf16[16,576]{1,0:T(8,128)(2,1)S(1)}, u32[]{:S(2)}, u32[]{:S(2)}) %collective-permute-start.8) | collective-permute-done | bytes 18464 | tf_op jit(solution)/shard_map/ppermute | solution.py:137
  50.6 2.5 %collective-permute-done.7.refs_2_.refs_6_ = bf16[16,576]{1,0:T(8,128)(2,1)S(1)} collective-permute-done((bf16[16,576]{1,0:T(8,128)(2,1)S(1)}, bf16[16,576]{1,0:T(8,128)(2,1)S(1)}, u32[]{:S(2)}, u32[]{:S(2)}) %collective-permute-start.7) | collective-permute-done | bytes 18464 | tf_op jit(solution)/shard_map/ppermute | solution.py:137
  53.0 0.0 collective-permute-done.6.refs_1_.refs_5_
  53.0 0.0 copy-done.4
  53.0 0.3 shard_map.78
  53.4 1.6 %collective-permute-start.10 = (bf16[32,288]{1,0:T(8,128)(2,1)S(1)}, bf16[32,288]{1,0:T(8,128)(2,1)S(1)}, u32[]{:S(2)}, u32[]{:S(2)}) collective-permute-start(bf16[32,288]{1,0:T(8,128)(2,1)S(1)} %get-tuple-element.40), channel_id=1, source_target_pairs={{0,2},{2,0},{1,3},{3,1},{4,6},{6,4},{5,7},{7,5},{8,10},{10,8},{9,1... | collective-permute-start | bytes 55304 | tf_op jit(solution)/shard_map/ppermute | solution.py:442
  54.9 0.0 collective-permute-start.11
  54.9 0.6 collective-permute-start.9
  55.6 2.5 %collective-permute-done.11.refs_3_ = bf16[16,288]{1,0:T(8,128)(2,1)S(1)} collective-permute-done((bf16[16,288]{1,0:T(8,128)(2,1)S(1)}, bf16[16,288]{1,0:T(8,128)(2,1)S(1)}, u32[]{:S(2)}, u32[]{:S(2)}) %collective-permute-start.11) | collective-permute-done | bytes 9248 | tf_op jit(solution)/shard_map/ppermute | solution.py:443
  58.0 0.0 collective-permute-done.9.refs_1_
  58.0 0.0 collective-permute-done.10.refs_2_
  58.0 0.4 shard_map.79
  58.5 0.2 collective-permute-start.12
  58.7 2.0 %collective-permute-start.13 = (bf16[8,2048]{1,0:T(8,128)(2,1)S(1)}, bf16[8,2048]{1,0:T(8,128)(2,1)S(1)}, u32[]{:S(2)}, u32[]{:S(2)}) collective-permute-start(bf16[8,2048]{1,0:T(8,128)(2,1)S(1)} %get-tuple-element.46), channel_id=1, source_target_pairs={{0,8},{4,12},{8,0},{12,4},{1,9},{5,13},{9,1},{13,5},{2,10},{6,14},... | collective-permute-start | bytes 98312 | tf_op jit(solution)/shard_map/ppermute | solution.py:137
  60.6 2.3 %collective-permute-start.14 = (bf16[8,2048]{1,0:T(8,128)(2,1)S(1)}, bf16[8,2048]{1,0:T(8,128)(2,1)S(1)}, u32[]{:S(2)}, u32[]{:S(2)}) collective-permute-start(bf16[8,2048]{1,0:T(8,128)(2,1)S(1)} %get-tuple-element.47), channel_id=1, source_target_pairs={{0,12},{4,8},{8,4},{12,0},{1,13},{5,9},{9,5},{13,1},{2,14},{6,10},... | collective-permute-start | bytes 98312 | tf_op jit(solution)/shard_map/ppermute | solution.py:137
  62.9 0.0 collective-permute-done.18.far
  62.9 0.0 collective-permute-done.19.last
  62.9 0.0 copy-done.2
  62.9 0.1 shard_map.80.refs_8_
  63.1 0.0 collective-permute-done.12.refs_1_
  63.1 0.5 collective-permute-done.13.refs_2_
  63.6 2.8 %collective-permute-done.14.refs_3_ = bf16[8,2048]{1,0:T(8,128)(2,1)S(1)} collective-permute-done((bf16[8,2048]{1,0:T(8,128)(2,1)S(1)}, bf16[8,2048]{1,0:T(8,128)(2,1)S(1)}, u32[]{:S(2)}, u32[]{:S(2)}) %collective-permute-start.14) | collective-permute-done | bytes 32800 | tf_op jit(solution)/shard_map/ppermute | solution.py:137
  66.4 1.1 %shard_map.81 = (bf16[8,1152]{1,0:T(8,128)(2,1)S(1)}, bf16[8,1152]{1,0:T(8,128)(2,1)S(1)}) custom-call(bf16[8,2048]{1,0:T(8,128)(2,1)S(1)} %get-tuple-element.44.refs_0_, bf16[8,2048]{1,0:T(8,128)(2,1)S(1)} %collective-permute-done.12.refs_1_, bf16[8,2048]{1,0:T(8,128)(2,1)S(1)} %collective-permute-done.13.refs_2_, ...), custom_call_target="tpu_custom_call" | custom-call | tf_op jit(solution)/shard_map/pallas_call | solution.py:116
  67.5 0.0 collective-permute-start.20
  67.5 1.2 %collective-permute-done.20.other = bf16[8,1152]{1,0:T(8,128)(2,1)S(1)} collective-permute-done((bf16[8,1152]{1,0:T(8,128)(2,1)S(1)}, bf16[8,1152]{1,0:T(8,128)(2,1)S(1)}, u32[]{:S(2)}, u32[]{:S(2)}) %collective-permute-start.20) | collective-permute-done | bytes 18464 | tf_op jit(solution)/shard_map/ppermute | solution.py:465
  68.7 0.6 shard_map.82
  (7 shorter events, 0.1 us)
Async XLA Ops:
  0.0 1.0 %copy-start.1 = (bf16[288,576]{1,0:T(8,128)(2,1)S(1)}, bf16[288,576]{1,0:T(8,128)(2,1)}, u32[]{:S(2)}) copy-start(bf16[288,576]{1,0:T(8,128)(2,1)} %own.1) | copy-start | bytes 995332
  1.0 1.2 %copy-start.3 = (bf16[288,3,576]{2,0,1:T(8,128)(2,1)S(1)}, bf16[288,3,576]{2,0,1:T(8,128)(2,1)}, u32[]{:S(2)}) copy-start(bf16[288,3,576]{2,0,1:T(8,128)(2,1)} %param.9) | copy-start | bytes 2985988
  2.2 23.2 %copy-start.5 = (bf16[2,4,1152]{2,1,0:T(4,128)(2,1)S(1)}, bf16[2,4,1152]{2,1,0:T(4,128)(2,1)}, u32[]{:S(2)}) copy-start(bf16[2,4,1152]{2,1,0:T(4,128)(2,1)} %video_hbm.1) | copy-start | bytes 55300
  2.2 23.2 %copy-start.7 = (f32[1152]{0:T(1024)S(1)}, f32[1152]{0:T(1024)}, u32[]{:S(2)}) copy-start(f32[1152]{0:T(1024)} %gain_hbm.1) | copy-start | bytes 13828
  2.5 39.5 %copy-start = (bf16[288,3,576]{2,0,1:T(8,128)(2,1)S(1)}, bf16[288,3,576]{2,0,1:T(8,128)(2,1)}, u32[]{:S(2)}) copy-start(bf16[288,3,576]{2,0,1:T(8,128)(2,1)} %param.12) | copy-start | bytes 2985988
  2.5 39.5 %copy-start.6 = (f32[1152]{0:T(1024)S(1)}, f32[1152]{0:T(1024)}, u32[]{:S(2)}) copy-start(f32[1152]{0:T(1024)} %refs_4_.2) | copy-start | bytes 13828
  2.5 8.8 %collective-permute-start.15 = (bf16[72,576]{1,0:T(8,128)(2,1)S(1)}, bf16[72,576]{1,0:T(8,128)(2,1)S(1)}, u32[]{:S(2)}, u32[]{:S(2)}) collective-permute-start(bf16[72,576]{1,0:T(8,128)(2,1)S(1)} %get-tuple-element.48), channel_id=1, source_target_pairs={{0,8},{4,12},{8,0},{12,4},{1,9},{5,13},{9,1},{13,5},{2,10},{6,14},... | collective-permute-start | bytes 248840 | tf_op jit(solution)/shard_map/ppermute | solution.py:406
  11.3 5.6 %collective-permute-start.16 = (bf16[144,576]{1,0:T(8,128)(2,1)S(1)}, bf16[144,576]{1,0:T(8,128)(2,1)S(1)}, u32[]{:S(2)}, u32[]{:S(2)}) collective-permute-start(bf16[144,576]{1,0:T(8,128)(2,1)S(1)} %pad_maximum_fusion), channel_id=1, source_target_pairs={{0,4},{4,0},{8,12},{12,8},{1,5},{5,1},{9,13},{13,9},{2,6},{6,2},{1... | collective-permute-start | bytes 497672 | tf_op jit(solution)/shard_map/ppermute | solution.py:406
  17.0 6.9 %collective-permute-start.17 = (bf16[216,576]{1,0:T(8,128)(2,1)S(1)}, bf16[216,576]{1,0:T(8,128)(2,1)S(1)}, u32[]{:S(2)}, u32[]{:S(2)}) collective-permute-start(bf16[216,576]{1,0:T(8,128)(2,1)S(1)} %constant_dynamic-update-slice_fusion.near), channel_id=1, source_target_pairs={{0,2},{2,0},{1,3},{3,1},{4,6},{6,4},{5,7},{7,5},{8,10},{10,8},{9,1... | collective-permute-start | bytes 746504 | tf_op jit(solution)/shard_map/ppermute | solution.py:409
  18.6 44.3 %collective-permute-start.18 = (bf16[216,576]{1,0:T(8,128)(2,1)S(1)}, bf16[216,576]{1,0:T(8,128)(2,1)S(1)}, u32[]{:S(2)}, u32[]{:S(2)}) collective-permute-start(bf16[216,576]{1,0:T(8,128)(2,1)S(1)} %constant_dynamic-update-slice_fusion.near), channel_id=1, source_target_pairs={{0,16},{16,0},{1,17},{17,1},{2,18},{18,2},{3,19},{19,3},{4,20},{20... | collective-permute-start | bytes 746504 | tf_op jit(solution)/shard_map/ppermute | solution.py:412
  23.9 39.1 %collective-permute-start.19 = (bf16[216,576]{1,0:T(8,128)(2,1)S(1)}, bf16[216,576]{1,0:T(8,128)(2,1)S(1)}, u32[]{:S(2)}, u32[]{:S(2)}) collective-permute-start(bf16[216,576]{1,0:T(8,128)(2,1)S(1)} %collective-permute-done.17.side), channel_id=1, source_target_pairs={{0,16},{16,0},{1,17},{17,1},{2,18},{18,2},{3,19},{19,3},{4,20},{20... | collective-permute-start | bytes 746504 | tf_op jit(solution)/shard_map/ppermute | solution.py:412
  25.7 5.9 %collective-permute-start = (bf16[16,288]{1,0:T(8,128)(2,1)S(1)}, bf16[16,288]{1,0:T(8,128)(2,1)S(1)}, u32[]{:S(2)}, u32[]{:S(2)}) collective-permute-start(bf16[16,288]{1,0:T(8,128)(2,1)S(1)} %get-tuple-element.29), channel_id=1, source_target_pairs={{0,4},{4,0},{8,12},{12,8},{1,5},{5,1},{9,13},{13,9},{2,6},{6,2},{1... | collective-permute-start | bytes 27656 | tf_op jit(solution)/shard_map/ppermute | solution.py:137
  28.3 5.1 %collective-permute-start.1 = (bf16[16,288]{1,0:T(8,128)(2,1)S(1)}, bf16[16,288]{1,0:T(8,128)(2,1)S(1)}, u32[]{:S(2)}, u32[]{:S(2)}) collective-permute-start(bf16[16,288]{1,0:T(8,128)(2,1)S(1)} %get-tuple-element.30), channel_id=1, source_target_pairs={{0,8},{4,12},{8,0},{12,4},{1,9},{5,13},{9,1},{13,5},{2,10},{6,14},... | collective-permute-start | bytes 27656 | tf_op jit(solution)/shard_map/ppermute | solution.py:137
  31.6 5.5 %collective-permute-start.2 = (bf16[16,288]{1,0:T(8,128)(2,1)S(1)}, bf16[16,288]{1,0:T(8,128)(2,1)S(1)}, u32[]{:S(2)}, u32[]{:S(2)}) collective-permute-start(bf16[16,288]{1,0:T(8,128)(2,1)S(1)} %get-tuple-element.31), channel_id=1, source_target_pairs={{0,12},{4,8},{8,4},{12,0},{1,13},{5,9},{9,5},{13,1},{2,14},{6,10},... | collective-permute-start | bytes 27656 | tf_op jit(solution)/shard_map/ppermute | solution.py:137
  37.1 15.9 %copy-start.4 = (bf16[288,576]{1,0:T(8,128)(2,1)S(1)}, bf16[288,576]{1,0:T(8,128)(2,1)}, u32[]{:S(2)}) copy-start(bf16[288,576]{1,0:T(8,128)(2,1)} %refs_4_.3) | copy-start | bytes 995332
  37.6 4.8 %collective-permute-start.3 = (bf16[3,8,576]{2,1,0:T(8,128)(2,1)S(1)}, bf16[3,8,576]{2,1,0:T(8,128)(2,1)S(1)}, u32[]{:S(2)}, u32[]{:S(2)}) collective-permute-start(bf16[3,8,576]{2,1,0:T(8,128)(2,1)S(1)} %get-tuple-element.34), channel_id=1, source_target_pairs={{0,4},{4,0},{8,12},{12,8},{1,5},{5,1},{9,13},{13,9},{2,6},{6,2},{1... | collective-permute-start | bytes 82952 | tf_op jit(solution)/shard_map/ppermute | solution.py:137
  37.7 4.9 %collective-permute-start.4 = (bf16[3,8,576]{2,1,0:T(8,128)(2,1)S(1)}, bf16[3,8,576]{2,1,0:T(8,128)(2,1)S(1)}, u32[]{:S(2)}, u32[]{:S(2)}) collective-permute-start(bf16[3,8,576]{2,1,0:T(8,128)(2,1)S(1)} %get-tuple-element.35), channel_id=1, source_target_pairs={{0,8},{4,12},{8,0},{12,4},{1,9},{5,13},{9,1},{13,5},{2,10},{6,14},... | collective-permute-start | bytes 82952 | tf_op jit(solution)/shard_map/ppermute | solution.py:137
  38.4 6.2 %collective-permute-start.5 = (bf16[3,8,576]{2,1,0:T(8,128)(2,1)S(1)}, bf16[3,8,576]{2,1,0:T(8,128)(2,1)S(1)}, u32[]{:S(2)}, u32[]{:S(2)}) collective-permute-start(bf16[3,8,576]{2,1,0:T(8,128)(2,1)S(1)} %get-tuple-element.36), channel_id=1, source_target_pairs={{0,12},{4,8},{8,4},{12,0},{1,13},{5,9},{9,5},{13,1},{2,14},{6,10},... | collective-permute-start | bytes 82952 | tf_op jit(solution)/shard_map/ppermute | solution.py:137
  42.4 20.6 %copy-start.2 = (bf16[288,576]{1,0:T(8,128)(2,1)S(1)}, bf16[288,576]{1,0:T(8,128)(2,1)}, u32[]{:S(2)}) copy-start(bf16[288,576]{1,0:T(8,128)(2,1)} %own.1) | copy-start | bytes 995332
  45.0 5.6 %collective-permute-start.8 = (bf16[16,576]{1,0:T(8,128)(2,1)S(1)}, bf16[16,576]{1,0:T(8,128)(2,1)S(1)}, u32[]{:S(2)}, u32[]{:S(2)}) collective-permute-start(bf16[16,576]{1,0:T(8,128)(2,1)S(1)} %shard_map.77.refs_0_.refs_4_), channel_id=1, source_target_pairs={{0,12},{4,8},{8,4},{12,0},{1,13},{5,9},{9,5},{13,1},{2,14},{6,10},... | collective-permute-start | bytes 55304 | tf_op jit(solution)/shard_map/ppermute | solution.py:137
  48.4 4.7 %collective-permute-start.7 = (bf16[16,576]{1,0:T(8,128)(2,1)S(1)}, bf16[16,576]{1,0:T(8,128)(2,1)S(1)}, u32[]{:S(2)}, u32[]{:S(2)}) collective-permute-start(bf16[16,576]{1,0:T(8,128)(2,1)S(1)} %shard_map.77.refs_0_.refs_4_), channel_id=1, source_target_pairs={{0,8},{4,12},{8,0},{12,4},{1,9},{5,13},{9,1},{13,5},{2,10},{6,14},... | collective-permute-start | bytes 55304 | tf_op jit(solution)/shard_map/ppermute | solution.py:137
  48.4 4.7 %collective-permute-start.6 = (bf16[16,576]{1,0:T(8,128)(2,1)S(1)}, bf16[16,576]{1,0:T(8,128)(2,1)S(1)}, u32[]{:S(2)}, u32[]{:S(2)}) collective-permute-start(bf16[16,576]{1,0:T(8,128)(2,1)S(1)} %shard_map.77.refs_0_.refs_4_), channel_id=1, source_target_pairs={{0,4},{4,0},{8,12},{12,8},{1,5},{5,1},{9,13},{13,9},{2,6},{6,2},{1... | collective-permute-start | bytes 55304 | tf_op jit(solution)/shard_map/ppermute | solution.py:137
  53.4 4.7 %collective-permute-start.10 = (bf16[32,288]{1,0:T(8,128)(2,1)S(1)}, bf16[32,288]{1,0:T(8,128)(2,1)S(1)}, u32[]{:S(2)}, u32[]{:S(2)}) collective-permute-start(bf16[32,288]{1,0:T(8,128)(2,1)S(1)} %get-tuple-element.40), channel_id=1, source_target_pairs={{0,2},{2,0},{1,3},{3,1},{4,6},{6,4},{5,7},{7,5},{8,10},{10,8},{9,1... | collective-permute-start | bytes 55304 | tf_op jit(solution)/shard_map/ppermute | solution.py:442
  54.9 3.1 %collective-permute-start.11 = (bf16[16,288]{1,0:T(8,128)(2,1)S(1)}, bf16[16,288]{1,0:T(8,128)(2,1)S(1)}, u32[]{:S(2)}, u32[]{:S(2)}) collective-permute-start(bf16[16,288]{1,0:T(8,128)(2,1)S(1)} %get-tuple-element.41), channel_id=1, source_target_pairs={{0,3},{1,2},{2,1},{3,0},{4,7},{5,6},{6,5},{7,4},{8,11},{9,10},{10,... | collective-permute-start | bytes 27656 | tf_op jit(solution)/shard_map/ppermute | solution.py:443
  54.9 3.1 %collective-permute-start.9 = (bf16[16,288]{1,0:T(8,128)(2,1)S(1)}, bf16[16,288]{1,0:T(8,128)(2,1)S(1)}, u32[]{:S(2)}, u32[]{:S(2)}) collective-permute-start(bf16[16,288]{1,0:T(8,128)(2,1)S(1)} %get-tuple-element.39.refs_0_), channel_id=1, source_target_pairs={{0,1},{1,0},{2,3},{3,2},{4,5},{5,4},{6,7},{7,6},{8,9},{9,8},{10,11... | collective-permute-start | bytes 27656 | tf_op jit(solution)/shard_map/ppermute | solution.py:441
  58.5 4.6 %collective-permute-start.12 = (bf16[8,2048]{1,0:T(8,128)(2,1)S(1)}, bf16[8,2048]{1,0:T(8,128)(2,1)S(1)}, u32[]{:S(2)}, u32[]{:S(2)}) collective-permute-start(bf16[8,2048]{1,0:T(8,128)(2,1)S(1)} %get-tuple-element.45), channel_id=1, source_target_pairs={{0,4},{4,0},{8,12},{12,8},{1,5},{5,1},{9,13},{13,9},{2,6},{6,2},{1... | collective-permute-start | bytes 98312 | tf_op jit(solution)/shard_map/ppermute | solution.py:137
  58.7 4.9 %collective-permute-start.13 = (bf16[8,2048]{1,0:T(8,128)(2,1)S(1)}, bf16[8,2048]{1,0:T(8,128)(2,1)S(1)}, u32[]{:S(2)}, u32[]{:S(2)}) collective-permute-start(bf16[8,2048]{1,0:T(8,128)(2,1)S(1)} %get-tuple-element.46), channel_id=1, source_target_pairs={{0,8},{4,12},{8,0},{12,4},{1,9},{5,13},{9,1},{13,5},{2,10},{6,14},... | collective-permute-start | bytes 98312 | tf_op jit(solution)/shard_map/ppermute | solution.py:137
  60.6 5.7 %collective-permute-start.14 = (bf16[8,2048]{1,0:T(8,128)(2,1)S(1)}, bf16[8,2048]{1,0:T(8,128)(2,1)S(1)}, u32[]{:S(2)}, u32[]{:S(2)}) collective-permute-start(bf16[8,2048]{1,0:T(8,128)(2,1)S(1)} %get-tuple-element.47), channel_id=1, source_target_pairs={{0,12},{4,8},{8,4},{12,0},{1,13},{5,9},{9,5},{13,1},{2,14},{6,10},... | collective-permute-start | bytes 98312 | tf_op jit(solution)/shard_map/ppermute | solution.py:137
  67.5 1.2 %collective-permute-start.20 = (bf16[8,1152]{1,0:T(8,128)(2,1)S(1)}, bf16[8,1152]{1,0:T(8,128)(2,1)S(1)}, u32[]{:S(2)}, u32[]{:S(2)}) collective-permute-start(bf16[8,1152]{1,0:T(8,128)(2,1)S(1)} %get-tuple-element.49.own), channel_id=1, source_target_pairs={{0,1},{1,0},{2,3},{3,2},{4,5},{5,4},{6,7},{7,6},{8,9},{9,8},{10,11... | collective-permute-start | bytes 55304 | tf_op jit(solution)/shard_map/ppermute | solution.py:465

commit v5 on v4

--- a/solution.py
+++ b/solution.py
@@ -144,83 +144,89 @@
     return jnp.dot(chosen, value.astype(BF16), preferred_element_type=F32)
 
 
-def split_body(count, video_hbm, gain_hbm, *refs):
-    outs, (held, video_ref, gain_ref, sems) = refs[:count], refs[count:]
+def in_three(value):
+    high = value.astype(BF16).astype(F32)
+    middle = (value - high).astype(BF16).astype(F32)
+    return high, middle, value - high - middle
+
+
+def tail_of(items, rows, size):
+    lane = lax.broadcasted_iota(jnp.int32, (rows, size), 1)
+    tail = jnp.zeros((rows, size), F32)
+    for at, item in enumerate(items):
+        tail = jnp.where(lane == at, item, tail)
+    return tail
+
+
+def from_three(tail, at):
+    lane = lax.broadcasted_iota(jnp.int32, tail.shape, 1)
+    return jnp.sum(jnp.where((lane >= at) & (lane < at + 3), tail, 0.0), axis=-1, keepdims=True)
+
+
+def rows_of(block_ref):
+    return jnp.concatenate([block_ref[i].astype(F32) for i in range(block_ref.shape[0])], axis=0)
+
+
+def load_body(weight_ref, held_ref, sems):
+    copy = pltpu.make_async_copy(weight_ref, held_ref, sems.at[0])
+    copy.start()
+    copy.wait()
+
+
+def slices_of(gain_ref, gains):
+    for s in range(gains.shape[0]):
+        row = lanes(gain_ref[...].reshape(1, -1), s * gains.shape[2], gains.shape[2])
+        gains[s] = jnp.broadcast_to(row, gains.shape[1:])
+    return gains[lax.axis_index("frame")]
+
+
+def project_body(count, *refs):
+    parts, gain_ref, weight_ref, outs = refs[:count], *refs[count : count + 2], refs[count + 2 : -2]
+    tokens, total = refs[-2:]
     f = lax.axis_index("frame")
-    copies = [
-        pltpu.make_async_copy(video_hbm, video_ref, sems.at[0]),
-        pltpu.make_async_copy(gain_hbm, gain_ref, sems.at[1]),
-    ]
-    for copy in copies:
-        copy.start()
-    for copy in copies:
-        copy.wait()
-    rows = video_ref.shape[0] * video_ref.shape[1]
-    share = held.shape[2]
-    x = jnp.concatenate([video_ref[i].astype(F32) for i in range(video_ref.shape[0])], axis=0)
-    mean = jnp.mean(x, axis=-1, keepdims=True)
-    centred = x - mean
-    spread = jnp.mean(centred * centred, axis=-1, keepdims=True)
-    y = centred * lax.rsqrt(spread + 1e-06) * gain_ref[...].reshape(1, -1)
-    for s in range(count):
-        held[s, 0:rows] = lanes(y, s * share, share)
-        held[s, rows:] = lanes(x, s * share, share)
-    for k in range(count):
-        outs[k][...] = held[f ^ k].astype(BF16)
-
-
-def load_body(weight_ref, rows_ref, held_ref, piece_ref, sems):
-    quarter = 2 * lax.axis_index("patch") + lax.axis_index("groups")
-    size = piece_ref.shape[0]
-    place = pl.multiple_of(quarter * size, size)
-    copies = [
-        pltpu.make_async_copy(rows_ref.at[pl.ds(place, size), :], piece_ref, sems.at[0]),
-        pltpu.make_async_copy(weight_ref, held_ref, sems.at[1]),
-    ]
-    for copy in copies:
-        copy.start()
-    for copy in copies:
-        copy.wait()
-
-
-def project_body(count, *refs):
-    parts, weight_ref, outs = refs[:count], refs[count], refs[count + 1 : 2 * count + 1]
-    tokens, total = refs[2 * count + 1 :]
-    f = lax.axis_index("frame")
-    rows = tokens.shape[0] // count
+    share = tokens.shape[2]
+    plane = tokens.shape[1]
+    rows = plane // count
+    gain = gain_ref[...].reshape(1, -1)
     for k in range(count):
         place = pl.multiple_of((f ^ k) * rows, rows)
-        tokens[pl.ds(place, rows), :] = parts[k][0:rows].astype(F32)
-    row = lax.broadcasted_iota(jnp.int32, (tokens.shape[0], 1), 0)
+        x = rows_of(parts[k])
+        centred = x - jnp.mean(x, axis=-1, keepdims=True)
+        spread = jnp.mean(centred * centred, axis=-1, keepdims=True)
+        y = centred * lax.rsqrt(spread + 1e-06) * gain
+        for s in range(count):
+            tokens[s, pl.ds(place, rows), :] = lanes(y, s * share, share)
+    row = lax.broadcasted_iota(jnp.int32, (plane, 1), 0)
     source = lax.rem(row, rows) * count + lax.div(row, rows)
-    x = pick_rows(tokens[...], source).astype(BF16)
-    for t in range(KINDS):
-        total[t] = jnp.dot(x, weight_ref[t], preferred_element_type=F32)
+    x = pick_rows(tokens[f], source).astype(BF16)
+    found = [jnp.dot(x, weight_ref[t], preferred_element_type=F32) for t in range(KINDS)]
+    total[...] = jnp.concatenate(found, axis=1)
     for k in range(count):
         place = pl.multiple_of((f ^ k) * rows, rows)
-        for t in range(KINDS):
-            outs[k][t] = total.at[t][pl.ds(place, rows), :].astype(BF16)
+        outs[k][...] = total[pl.ds(place, rows), :].astype(BF16)
 
 
 def prepare_body(count, *refs):
     parts, gain_ref, weight_ref = refs[:count], refs[count], refs[count + 1]
     fixed_ref, gain_own, raw_own, raw_other, gains, raw = refs[count + 2 :]
     f, p = lax.axis_index("frame"), lax.axis_index("patch")
-    share = gains.shape[2]
-    for s in range(count):
-        gains[s] = jnp.broadcast_to(lanes(gain_ref[...].reshape(1, -1), s * share, share), gains.shape[1:])
-    g = gains[f]
+    g = slices_of(gain_ref, gains)
     gain_own[...] = g
     g = g.astype(BF16)
     rows = [jnp.dot(g, weight_ref[t], preferred_element_type=F32) for t in range(KINDS)]
     row = lax.broadcasted_iota(jnp.int32, rows[0].shape, 0)
     fixed_ref[...] = jnp.where(row == 0, rows[0], jnp.where(row == 1, rows[1], rows[2]))
-    whole = parts[0].shape[0] // 2
-    places = whole // 2
-    for k in range(count):
-        raw[f ^ k] = parts[k][whole:].astype(F32)
+    share = gains.shape[2]
+    places = parts[0].shape[1]
+    rows = 2 * places
+    for k in range(count):
+        place = pl.multiple_of((f ^ k) * rows, rows)
+        x = rows_of(parts[k])
+        for s in range(count):
+            raw[s, pl.ds(place, rows), :] = lanes(x, s * share, share)
+    whole = raw[f]
     even, odd = (
-        jnp.concatenate([raw[s][at : at + places] for s in range(count)], axis=0)
+        jnp.concatenate([whole[r + at : r + at + places] for r in range(0, count * rows, rows)], axis=0)
         for at in (0, places)
     )
     raw_own[...] = jnp.where(p == 0, even, odd).astype(BF16)
@@ -247,13 +253,9 @@
 
 def attend_time_body(count, *refs):
     parts, fixed_ref, out_ref = refs[:count], refs[count], refs[count + 1]
-    qkv = []
-    for t in range(KINDS):
-        total = parts[0][t].astype(F32)
-        for k in range(1, count):
-            total = total + parts[k][t].astype(F32)
-        qkv.append(total.astype(BF16).astype(F32))
-    attended = attend_rows(*qkv)
+    total = sum(part[...].astype(F32) for part in parts).astype(BF16).astype(F32)
+    columns = out_ref.shape[1]
+    attended = attend_rows(*(lanes(total, t * columns, columns) for t in range(KINDS)))
     out_ref[...] = jnp.concatenate([attended, fixed_ref[...]], axis=0).astype(BF16)
 
 
@@ -276,12 +278,6 @@
     other_ref[0:half] = total[half:].astype(BF16)
     alone_ref[...] = total[half:].astype(BF16)
     other_ref[half:] = raw_other[...]
-
-
-def in_three(value):
-    high = value.astype(BF16).astype(F32)
-    middle = (value - high).astype(BF16).astype(F32)
-    return high, middle, value - high - middle
 
 
 def project_space_body(count, *refs):
@@ -303,10 +299,7 @@
     y = (centred * gain_ref[0:1]).astype(BF16)
     found = [jnp.dot(y, weight_ref[t], preferred_element_type=F32) for t in range(KINDS)]
     spare = total.shape[1] - KINDS * weight_ref.shape[2] - x.shape[1]
-    lane = lax.broadcasted_iota(jnp.int32, (x.shape[0], spare), 1)
-    tail = jnp.zeros(lane.shape, F32)
-    for at, item in enumerate((*in_three(mean), *in_three(square))):
-        tail = jnp.where(lane == at, item, tail)
+    tail = tail_of((*in_three(mean), *in_three(square)), x.shape[0], spare)
     total[...] = jnp.concatenate([*found, x, tail], axis=1)
     rows = total.shape[0] // count
     for k in range(count):
@@ -322,11 +315,8 @@
     share = weight_ref.shape[0] // count
     messages = [part[...].astype(F32) for part in parts]
     tails = [lanes(m, KINDS * columns + share, m.shape[1] - KINDS * columns - share) for m in messages]
-    lane = lax.broadcasted_iota(jnp.int32, tails[0].shape, 1)
-    means = [jnp.sum(jnp.where(lane < 3, t, 0.0), axis=-1, keepdims=True) for t in tails]
-    squares = [
-        jnp.sum(jnp.where((lane >= 3) & (lane < 6), t, 0.0), axis=-1, keepdims=True) for t in tails
-    ]
+    means = [from_three(t, 0) for t in tails]
+    squares = [from_three(t, 3) for t in tails]
     mean = sum(means) / count
     square = sum(squares) + share * sum((m - mean) * (m - mean) for m in means)
     scale = lax.rsqrt(square / (share * count) + 1e-06)
@@ -375,28 +365,17 @@
     body = functools.partial
     swap = [(0, 1), (1, 0)]
 
-    normed = run(
-        body(split_body, count),
-        [((2 * rows, share), BF16)] * count,
-        video,
-        gain_time,
-        scratch=[((count, 2 * rows, share), F32), (video.shape, BF16), ((width,), F32)],
-        sems=2,
-    )
-    normed = exchange(normed)
-    qkv_time, piece = run(
-        load_body,
-        [(qkv_time.shape, BF16), ((share // 4, columns), BF16)],
-        qkv_time,
-        out_space,
-        sems=2,
-    )
+    tokens = exchange([video] * count)
+    quarter = 2 * lax.axis_index("patch") + lax.axis_index("groups")
+    piece = lax.dynamic_slice_in_dim(out_space, quarter * (share // 4), share // 4)
+    qkv_time = run(load_body, (qkv_time.shape, BF16), qkv_time, sems=1)
     partial_time = run(
         body(project_body, count),
-        [((KINDS, rows, columns), BF16)] * count,
-        *normed,
+        [((rows, KINDS * columns), BF16)] * count,
+        *tokens,
+        gain_time,
         qkv_time,
-        scratch=[((plane, share), F32), ((KINDS, plane, columns), F32)],
+        scratch=[((count, plane, share), F32), ((plane, KINDS * columns), F32)],
     )
     partial_time = exchange(partial_time)
     near, order = piece, [0]
@@ -421,10 +400,10 @@
             ((plane // 2, share), BF16),
             ((plane // 2, share), BF16),
         ],
-        *normed,
+        *tokens,
         gain_space,
         qkv_space,
-        scratch=[((count, 8, share), F32), ((count, rows, share), F32)],
+        scratch=[((count, 8, share), F32), ((count, plane, share), F32)],
     )
     attended = run(
         body(attend_time_body, count), ((rows + 8, columns), BF16), *partial_time, fixed

time: 69.5 us -> 68.5 us (0.986)
  local copies, waits for them, and re-layouts: 2.3 us -> 1.05 us
    unnamed x17 -> x15, local copies, waits for them, and re-layouts: 2.27 us -> 0.04 us
    dynamic_slice x0 -> x1, local copies, waits for them, and re-layouts: none -> 0.99 us  [moving_tokens(): lax.dynamic_slice_in_dim(out_space, quarter * (share // 4), share // 4)]
    pallas_call x10 -> x9, Pallas kernels: 4.28 us -> 4.24 us  [run(): pl.pallas_call(body, out_shape=shapes, in_specs=[pl.BlockSpec(memory_spac...]
  transfers between devices with their start and end apart: 21 -> 21, of which waited for: 13 -> 14; matrix products, arithmetic and copies ran while one was open for 0% -> 0% of each run, Pallas kernels for 3% -> 4%
where the time goes in v5:
time: 68.5 us; the launch traced here: 68.4 us
  waiting for transfers between devices  32 us (47%)
  starting transfers between devices  30.9 us (45%)
  Pallas kernels  4.24 us (6%)
  local copies, waits for them, and re-layouts  1.05 us (2%)
    ppermute x12, starting transfers between devices, exchange(): found.append(lax.ppermute(messages[k], 'frame', pairs))  19.2 us
    ppermute x12, waiting for transfers between devices, exchange(): found.append(lax.ppermute(messages[k], 'frame', pairs))  15.1 us
    ppermute x2, waiting for transfers between devices, moving_tokens(): near = jnp.concatenate([near, lax.ppermute(near, 'frame', pairs)], axis=0)  9.44 us
    ppermute x2, starting transfers between devices, moving_tokens(): near = jnp.concatenate([near, lax.ppermute(near, 'frame', pairs)], axis=0)  4.91 us
    pallas_call x9, Pallas kernels, run(): pl.pallas_call(body, out_shape=shapes, in_specs=[pl.BlockSpec(memory_spac...  4.24 us
    ppermute x1, waiting for transfers between devices, moving_tokens(): side = lax.ppermute(near, 'patch', swap)  3.76 us
    ppermute x2, starting transfers between devices, moving_tokens(): far.append(lax.ppermute(value, 'groups', swap))  3.04 us
    ppermute x1, waiting for transfers between devices, moving_tokens(): lax.ppermute(cross_only, ('patch', 'head'), [(i, 3 - i) for i in range(4)])  1.94 us
  transfers between devices with their start and end apart: 21, of which 14 were waited for; matrix products, arithmetic and copies ran while one was open for 0% of the time, Pallas kernels for 4%

profile of v5, /device:TPU:0, one launch (start us, length us, event | category | flops | bytes accessed | tf_op | source)
XLA Modules:
  0.0 68.4 jit_solution(14298689050293282370)
XLA Ops:
  0.0 0.0 copy-start.4
  0.0 0.0 copy-start.1
  0.0 1.0 %constant_dynamic-slice_fusion = bf16[72,576]{1,0:T(8,128)(2,1)S(1)} fusion(bf16[288,576]{1,0:T(8,128)(2,1)} %own.1, s32[]{:T(128)S(6)} %select_n.3), kind=kLoop, calls=%fused_computation.3 | loop fusion | bytes 165892 | tf_op jit(solution)/shard_map/dynamic_slice | solution.py:370
  1.0 4.1 %collective-permute-start.15 = (bf16[72,576]{1,0:T(8,128)(2,1)S(1)}, bf16[72,576]{1,0:T(8,128)(2,1)S(1)}, u32[]{:S(2)}, u32[]{:S(2)}) collective-permute-start(bf16[72,576]{1,0:T(8,128)(2,1)S(1)} %constant_dynamic-slice_fusion), channel_id=1, source_target_pairs={{0,8},{4,12},{8,0},{12,4},{1,9},{5,13},{9,1},{13,5},{2,10},{6,14},... | collective-permute-start | bytes 248840 | tf_op jit(solution)/shard_map/ppermute | solution.py:385
  5.1 4.6 %collective-permute-done.15 = bf16[72,576]{1,0:T(8,128)(2,1)S(1)} collective-permute-done((bf16[72,576]{1,0:T(8,128)(2,1)S(1)}, bf16[72,576]{1,0:T(8,128)(2,1)S(1)}, u32[]{:S(2)}, u32[]{:S(2)}) %collective-permute-start.15) | collective-permute-done | bytes 82976 | tf_op jit(solution)/shard_map/ppermute | solution.py:385
  9.8 0.8 %collective-permute-start.16 = (bf16[144,576]{1,0:T(8,128)(2,1)S(1)}, bf16[144,576]{1,0:T(8,128)(2,1)S(1)}, u32[]{:S(2)}, u32[]{:S(2)}) collective-permute-start(bf16[144,576]{1,0:T(8,128)(2,1)S(1)} %pad_maximum_fusion), channel_id=1, source_target_pairs={{0,4},{4,0},{8,12},{12,8},{1,5},{5,1},{9,13},{13,9},{2,6},{6,2},{1... | collective-permute-start | bytes 497672 | tf_op jit(solution)/shard_map/ppermute | solution.py:385
  10.6 4.8 %collective-permute-done.16 = bf16[144,576]{1,0:T(8,128)(2,1)S(1)} collective-permute-done((bf16[144,576]{1,0:T(8,128)(2,1)S(1)}, bf16[144,576]{1,0:T(8,128)(2,1)S(1)}, u32[]{:S(2)}, u32[]{:S(2)}) %collective-permute-start.16) | collective-permute-done | bytes 165920 | tf_op jit(solution)/shard_map/ppermute | solution.py:385
  15.4 1.6 %collective-permute-start.17 = (bf16[216,576]{1,0:T(8,128)(2,1)S(1)}, bf16[216,576]{1,0:T(8,128)(2,1)S(1)}, u32[]{:S(2)}, u32[]{:S(2)}) collective-permute-start(bf16[216,576]{1,0:T(8,128)(2,1)S(1)} %constant_dynamic-update-slice_fusion.near), channel_id=1, source_target_pairs={{0,2},{2,0},{1,3},{3,1},{4,6},{6,4},{5,7},{7,5},{8,10},{10,8},{9,1... | collective-permute-start | bytes 746504 | tf_op jit(solution)/shard_map/ppermute | solution.py:388
  17.0 1.5 %collective-permute-start.18 = (bf16[216,576]{1,0:T(8,128)(2,1)S(1)}, bf16[216,576]{1,0:T(8,128)(2,1)S(1)}, u32[]{:S(2)}, u32[]{:S(2)}) collective-permute-start(bf16[216,576]{1,0:T(8,128)(2,1)S(1)} %constant_dynamic-update-slice_fusion.near), channel_id=1, source_target_pairs={{0,16},{16,0},{1,17},{17,1},{2,18},{18,2},{3,19},{19,3},{4,20},{20... | collective-permute-start | bytes 746504 | tf_op jit(solution)/shard_map/ppermute | solution.py:391
  18.6 3.8 %collective-permute-done.17.side = bf16[216,576]{1,0:T(8,128)(2,1)S(1)} collective-permute-done((bf16[216,576]{1,0:T(8,128)(2,1)S(1)}, bf16[216,576]{1,0:T(8,128)(2,1)S(1)}, u32[]{:S(2)}, u32[]{:S(2)}) %collective-permute-start.17) | collective-permute-done | bytes 248864 | tf_op jit(solution)/shard_map/ppermute | solution.py:388
  22.3 1.5 %collective-permute-start.19 = (bf16[216,576]{1,0:T(8,128)(2,1)S(1)}, bf16[216,576]{1,0:T(8,128)(2,1)S(1)}, u32[]{:S(2)}, u32[]{:S(2)}) collective-permute-start(bf16[216,576]{1,0:T(8,128)(2,1)S(1)} %collective-permute-done.17.side), channel_id=1, source_target_pairs={{0,16},{16,0},{1,17},{17,1},{2,18},{18,2},{3,19},{19,3},{4,20},{20... | collective-permute-start | bytes 746504 | tf_op jit(solution)/shard_map/ppermute | solution.py:391
  23.8 0.0 copy-done.4
  23.8 2.5 %collective-permute-start = (bf16[2,4,1152]{2,1,0:T(4,128)(2,1)S(1)}, bf16[2,4,1152]{2,1,0:T(4,128)(2,1)S(1)}, u32[]{:S(2)}, u32[]{:S(2)}) collective-permute-start(bf16[2,4,1152]{2,1,0:T(4,128)(2,1)S(1)} %copy-done.4), channel_id=1, source_target_pairs={{0,4},{4,0},{8,12},{12,8},{1,5},{5,1},{9,13},{13,9},{2,6},{6,2},{1... | collective-permute-start | bytes 55304 | tf_op jit(solution)/shard_map/ppermute | solution.py:137
  26.3 3.4 %collective-permute-start.1 = (bf16[2,4,1152]{2,1,0:T(4,128)(2,1)S(1)}, bf16[2,4,1152]{2,1,0:T(4,128)(2,1)S(1)}, u32[]{:S(2)}, u32[]{:S(2)}) collective-permute-start(bf16[2,4,1152]{2,1,0:T(4,128)(2,1)S(1)} %copy-done.4), channel_id=1, source_target_pairs={{0,8},{4,12},{8,0},{12,4},{1,9},{5,13},{9,1},{13,5},{2,10},{6,14},... | collective-permute-start | bytes 55304 | tf_op jit(solution)/shard_map/ppermute | solution.py:137
  29.7 0.0 collective-permute-start.2
  29.7 0.0 copy-done.1
  29.7 0.0 copy-start.5
  29.7 0.2 shard_map.73.refs_5_
  29.9 0.0 copy-start
  29.9 0.0 copy-start.3
  29.9 0.0 collective-permute-done.refs_1_
  29.9 1.5 %collective-permute-done.1.refs_2_ = bf16[2,4,1152]{2,1,0:T(4,128)(2,1)S(1)} collective-permute-done((bf16[2,4,1152]{2,1,0:T(4,128)(2,1)S(1)}, bf16[2,4,1152]{2,1,0:T(4,128)(2,1)S(1)}, u32[]{:S(2)}, u32[]{:S(2)}) %collective-permute-start.1) | collective-permute-done | bytes 18464 | tf_op jit(solution)/shard_map/ppermute | solution.py:137
  31.4 3.9 %collective-permute-done.2.refs_3_ = bf16[2,4,1152]{2,1,0:T(4,128)(2,1)S(1)} collective-permute-done((bf16[2,4,1152]{2,1,0:T(4,128)(2,1)S(1)}, bf16[2,4,1152]{2,1,0:T(4,128)(2,1)S(1)}, u32[]{:S(2)}, u32[]{:S(2)}) %collective-permute-start.2) | collective-permute-done | bytes 18464 | tf_op jit(solution)/shard_map/ppermute | solution.py:137
  35.4 0.0 copy-done.5
  35.4 0.7 %shard_map.74 = (bf16[8,1728]{1,0:T(8,128)(2,1)S(1)}, bf16[8,1728]{1,0:T(8,128)(2,1)S(1)}, bf16[8,1728]{1,0:T(8,128)(2,1)S(1)}, bf16[8,1728]{1,0:T(8,128)(2,1)S(1)}) custom-call(bf16[2,4,1152]{2,1,0:T(4,128)(2,1)S(1)} %copy-done.4, bf16[2,4,1152]{2,1,0:T(4,128)(2,1)S(1)} %collective-permute-done.refs_1_, ...), custom_call_target="tpu_custom_call" | custom-call | tf_op jit(solution)/shard_map/pallas_call | solution.py:116
  36.1 0.1 collective-permute-start.3
  36.2 0.7 collective-permute-start.4
  36.8 3.7 %collective-permute-start.5 = (bf16[8,1728]{1,0:T(8,128)(2,1)S(1)}, bf16[8,1728]{1,0:T(8,128)(2,1)S(1)}, u32[]{:S(2)}, u32[]{:S(2)}) collective-permute-start(bf16[8,1728]{1,0:T(8,128)(2,1)S(1)} %get-tuple-element.25), channel_id=1, source_target_pairs={{0,12},{4,8},{8,4},{12,0},{1,13},{5,9},{9,5},{13,1},{2,14},{6,10},... | collective-permute-start | bytes 82952 | tf_op jit(solution)/shard_map/ppermute | solution.py:137
  40.6 0.0 copy-done.6
  40.6 0.0 copy-done
  40.6 0.3 shard_map.75
  40.9 0.0 collective-permute-done.3.refs_1_
  40.9 0.2 collective-permute-done.4.refs_2_
  41.1 2.1 %collective-permute-done.5.refs_3_ = bf16[8,1728]{1,0:T(8,128)(2,1)S(1)} collective-permute-done((bf16[8,1728]{1,0:T(8,128)(2,1)S(1)}, bf16[8,1728]{1,0:T(8,128)(2,1)S(1)}, u32[]{:S(2)}, u32[]{:S(2)}) %collective-permute-start.5) | collective-permute-done | bytes 27680 | tf_op jit(solution)/shard_map/ppermute | solution.py:137
  43.3 0.4 shard_map.76.refs_0_.refs_4_
  43.7 0.1 collective-permute-start.6
  43.7 3.8 %collective-permute-start.7 = (bf16[16,576]{1,0:T(8,128)(2,1)S(1)}, bf16[16,576]{1,0:T(8,128)(2,1)S(1)}, u32[]{:S(2)}, u32[]{:S(2)}) collective-permute-start(bf16[16,576]{1,0:T(8,128)(2,1)S(1)} %shard_map.76.refs_0_.refs_4_), channel_id=1, source_target_pairs={{0,8},{4,12},{8,0},{12,4},{1,9},{5,13},{9,1},{13,5},{2,10},{6,14},... | collective-permute-start | bytes 55304 | tf_op jit(solution)/shard_map/ppermute | solution.py:137
  47.5 0.5 collective-permute-start.8
  48.1 0.0 collective-permute-done.6.refs_1_.refs_5_
  48.1 1.2 %collective-permute-done.7.refs_2_.refs_6_ = bf16[16,576]{1,0:T(8,128)(2,1)S(1)} collective-permute-done((bf16[16,576]{1,0:T(8,128)(2,1)S(1)}, bf16[16,576]{1,0:T(8,128)(2,1)S(1)}, u32[]{:S(2)}, u32[]{:S(2)}) %collective-permute-start.7) | collective-permute-done | bytes 18464 | tf_op jit(solution)/shard_map/ppermute | solution.py:137
  49.3 3.8 %collective-permute-done.8.refs_3_.refs_7_ = bf16[16,576]{1,0:T(8,128)(2,1)S(1)} collective-permute-done((bf16[16,576]{1,0:T(8,128)(2,1)S(1)}, bf16[16,576]{1,0:T(8,128)(2,1)S(1)}, u32[]{:S(2)}, u32[]{:S(2)}) %collective-permute-start.8) | collective-permute-done | bytes 18464 | tf_op jit(solution)/shard_map/ppermute | solution.py:137
  53.1 0.0 copy-done.3
  53.1 0.3 shard_map.77
  53.4 1.6 %collective-permute-start.10 = (bf16[32,288]{1,0:T(8,128)(2,1)S(1)}, bf16[32,288]{1,0:T(8,128)(2,1)S(1)}, u32[]{:S(2)}, u32[]{:S(2)}) collective-permute-start(bf16[32,288]{1,0:T(8,128)(2,1)S(1)} %get-tuple-element.29), channel_id=1, source_target_pairs={{0,2},{2,0},{1,3},{3,1},{4,6},{6,4},{5,7},{7,5},{8,10},{10,8},{9,1... | collective-permute-start | bytes 55304 | tf_op jit(solution)/shard_map/ppermute | solution.py:421
  55.0 0.0 collective-permute-start.9
  55.0 0.6 collective-permute-start.11
  55.6 0.5 collective-permute-done.9.refs_1_
  56.2 1.9 %collective-permute-done.11.refs_3_ = bf16[16,288]{1,0:T(8,128)(2,1)S(1)} collective-permute-done((bf16[16,288]{1,0:T(8,128)(2,1)S(1)}, bf16[16,288]{1,0:T(8,128)(2,1)S(1)}, u32[]{:S(2)}, u32[]{:S(2)}) %collective-permute-start.11) | collective-permute-done | bytes 9248 | tf_op jit(solution)/shard_map/ppermute | solution.py:422
  58.1 0.0 collective-permute-done.10.refs_2_
  58.1 0.4 shard_map.78
  58.6 0.1 collective-permute-start.12
  58.6 1.1 %collective-permute-start.13 = (bf16[8,2048]{1,0:T(8,128)(2,1)S(1)}, bf16[8,2048]{1,0:T(8,128)(2,1)S(1)}, u32[]{:S(2)}, u32[]{:S(2)}) collective-permute-start(bf16[8,2048]{1,0:T(8,128)(2,1)S(1)} %get-tuple-element.35), channel_id=1, source_target_pairs={{0,8},{4,12},{8,0},{12,4},{1,9},{5,13},{9,1},{13,5},{2,10},{6,14},... | collective-permute-start | bytes 98312 | tf_op jit(solution)/shard_map/ppermute | solution.py:137
  59.7 3.3 %collective-permute-start.14 = (bf16[8,2048]{1,0:T(8,128)(2,1)S(1)}, bf16[8,2048]{1,0:T(8,128)(2,1)S(1)}, u32[]{:S(2)}, u32[]{:S(2)}) collective-permute-start(bf16[8,2048]{1,0:T(8,128)(2,1)S(1)} %get-tuple-element.36), channel_id=1, source_target_pairs={{0,12},{4,8},{8,4},{12,0},{1,13},{5,9},{9,5},{13,1},{2,14},{6,10},... | collective-permute-start | bytes 98312 | tf_op jit(solution)/shard_map/ppermute | solution.py:137
  63.0 0.0 collective-permute-done.18.far
  63.0 0.0 collective-permute-done.19.last
  63.0 0.0 copy-done.2
  63.0 0.1 shard_map.79.refs_8_
  63.2 0.0 collective-permute-done.12.refs_1_
  63.2 0.6 collective-permute-done.13.refs_2_
  63.7 1.7 %collective-permute-done.14.refs_3_ = bf16[8,2048]{1,0:T(8,128)(2,1)S(1)} collective-permute-done((bf16[8,2048]{1,0:T(8,128)(2,1)S(1)}, bf16[8,2048]{1,0:T(8,128)(2,1)S(1)}, u32[]{:S(2)}, u32[]{:S(2)}) %collective-permute-start.14) | collective-permute-done | bytes 32800 | tf_op jit(solution)/shard_map/ppermute | solution.py:137
  65.4 1.1 %shard_map.80 = (bf16[8,1152]{1,0:T(8,128)(2,1)S(1)}, bf16[8,1152]{1,0:T(8,128)(2,1)S(1)}) custom-call(bf16[8,2048]{1,0:T(8,128)(2,1)S(1)} %get-tuple-element.33.refs_0_, bf16[8,2048]{1,0:T(8,128)(2,1)S(1)} %collective-permute-done.12.refs_1_, bf16[8,2048]{1,0:T(8,128)(2,1)S(1)} %collective-permute-done.13.refs_2_, ...), custom_call_target="tpu_custom_call" | custom-call | tf_op jit(solution)/shard_map/pallas_call | solution.py:116
  66.6 0.0 collective-permute-start.20
  66.6 1.2 %collective-permute-done.20.other = bf16[8,1152]{1,0:T(8,128)(2,1)S(1)} collective-permute-done((bf16[8,1152]{1,0:T(8,128)(2,1)S(1)}, bf16[8,1152]{1,0:T(8,128)(2,1)S(1)}, u32[]{:S(2)}, u32[]{:S(2)}) %collective-permute-start.20) | collective-permute-done | bytes 18464 | tf_op jit(solution)/shard_map/ppermute | solution.py:444
  67.8 0.6 shard_map.81
  (5 shorter events, 0.1 us)
Async XLA Ops:
  0.0 23.8 %copy-start.4 = (bf16[2,4,1152]{2,1,0:T(4,128)(2,1)S(1)}, bf16[2,4,1152]{2,1,0:T(4,128)(2,1)}, u32[]{:S(2)}) copy-start(bf16[2,4,1152]{2,1,0:T(4,128)(2,1)} %refs_0_.3) | copy-start | bytes 55300
  0.0 29.7 %copy-start.1 = (bf16[288,3,576]{2,0,1:T(8,128)(2,1)S(1)}, bf16[288,3,576]{2,0,1:T(8,128)(2,1)}, u32[]{:S(2)}) copy-start(bf16[288,3,576]{2,0,1:T(8,128)(2,1)} %param.9) | copy-start | bytes 2985988
  1.0 8.8 %collective-permute-start.15 = (bf16[72,576]{1,0:T(8,128)(2,1)S(1)}, bf16[72,576]{1,0:T(8,128)(2,1)S(1)}, u32[]{:S(2)}, u32[]{:S(2)}) collective-permute-start(bf16[72,576]{1,0:T(8,128)(2,1)S(1)} %constant_dynamic-slice_fusion), channel_id=1, source_target_pairs={{0,8},{4,12},{8,0},{12,4},{1,9},{5,13},{9,1},{13,5},{2,10},{6,14},... | collective-permute-start | bytes 248840 | tf_op jit(solution)/shard_map/ppermute | solution.py:385
  9.8 5.6 %collective-permute-start.16 = (bf16[144,576]{1,0:T(8,128)(2,1)S(1)}, bf16[144,576]{1,0:T(8,128)(2,1)S(1)}, u32[]{:S(2)}, u32[]{:S(2)}) collective-permute-start(bf16[144,576]{1,0:T(8,128)(2,1)S(1)} %pad_maximum_fusion), channel_id=1, source_target_pairs={{0,4},{4,0},{8,12},{12,8},{1,5},{5,1},{9,13},{13,9},{2,6},{6,2},{1... | collective-permute-start | bytes 497672 | tf_op jit(solution)/shard_map/ppermute | solution.py:385
  15.4 6.9 %collective-permute-start.17 = (bf16[216,576]{1,0:T(8,128)(2,1)S(1)}, bf16[216,576]{1,0:T(8,128)(2,1)S(1)}, u32[]{:S(2)}, u32[]{:S(2)}) collective-permute-start(bf16[216,576]{1,0:T(8,128)(2,1)S(1)} %constant_dynamic-update-slice_fusion.near), channel_id=1, source_target_pairs={{0,2},{2,0},{1,3},{3,1},{4,6},{6,4},{5,7},{7,5},{8,10},{10,8},{9,1... | collective-permute-start | bytes 746504 | tf_op jit(solution)/shard_map/ppermute | solution.py:388
  17.0 46.0 %collective-permute-start.18 = (bf16[216,576]{1,0:T(8,128)(2,1)S(1)}, bf16[216,576]{1,0:T(8,128)(2,1)S(1)}, u32[]{:S(2)}, u32[]{:S(2)}) collective-permute-start(bf16[216,576]{1,0:T(8,128)(2,1)S(1)} %constant_dynamic-update-slice_fusion.near), channel_id=1, source_target_pairs={{0,16},{16,0},{1,17},{17,1},{2,18},{18,2},{3,19},{19,3},{4,20},{20... | collective-permute-start | bytes 746504 | tf_op jit(solution)/shard_map/ppermute | solution.py:391
  22.3 40.7 %collective-permute-start.19 = (bf16[216,576]{1,0:T(8,128)(2,1)S(1)}, bf16[216,576]{1,0:T(8,128)(2,1)S(1)}, u32[]{:S(2)}, u32[]{:S(2)}) collective-permute-start(bf16[216,576]{1,0:T(8,128)(2,1)S(1)} %collective-permute-done.17.side), channel_id=1, source_target_pairs={{0,16},{16,0},{1,17},{17,1},{2,18},{18,2},{3,19},{19,3},{4,20},{20... | collective-permute-start | bytes 746504 | tf_op jit(solution)/shard_map/ppermute | solution.py:391
  23.8 6.1 %collective-permute-start = (bf16[2,4,1152]{2,1,0:T(4,128)(2,1)S(1)}, bf16[2,4,1152]{2,1,0:T(4,128)(2,1)S(1)}, u32[]{:S(2)}, u32[]{:S(2)}) collective-permute-start(bf16[2,4,1152]{2,1,0:T(4,128)(2,1)S(1)} %copy-done.4), channel_id=1, source_target_pairs={{0,4},{4,0},{8,12},{12,8},{1,5},{5,1},{9,13},{13,9},{2,6},{6,2},{1... | collective-permute-start | bytes 55304 | tf_op jit(solution)/shard_map/ppermute | solution.py:137
  26.3 5.1 %collective-permute-start.1 = (bf16[2,4,1152]{2,1,0:T(4,128)(2,1)S(1)}, bf16[2,4,1152]{2,1,0:T(4,128)(2,1)S(1)}, u32[]{:S(2)}, u32[]{:S(2)}) collective-permute-start(bf16[2,4,1152]{2,1,0:T(4,128)(2,1)S(1)} %copy-done.4), channel_id=1, source_target_pairs={{0,8},{4,12},{8,0},{12,4},{1,9},{5,13},{9,1},{13,5},{2,10},{6,14},... | collective-permute-start | bytes 55304 | tf_op jit(solution)/shard_map/ppermute | solution.py:137
  29.7 5.7 %collective-permute-start.2 = (bf16[2,4,1152]{2,1,0:T(4,128)(2,1)S(1)}, bf16[2,4,1152]{2,1,0:T(4,128)(2,1)S(1)}, u32[]{:S(2)}, u32[]{:S(2)}) collective-permute-start(bf16[2,4,1152]{2,1,0:T(4,128)(2,1)S(1)} %copy-done.4), channel_id=1, source_target_pairs={{0,12},{4,8},{8,4},{12,0},{1,13},{5,9},{9,5},{13,1},{2,14},{6,10},... | collective-permute-start | bytes 55304 | tf_op jit(solution)/shard_map/ppermute | solution.py:137
  29.7 5.7 %copy-start.5 = (f32[1152]{0:T(1024)S(1)}, f32[1152]{0:T(1024)}, u32[]{:S(2)}) copy-start(f32[1152]{0:T(1024)} %refs_4_.3) | copy-start | bytes 13828
  29.7 10.8 %copy-start.6 = (f32[1152]{0:T(1024)S(1)}, f32[1152]{0:T(1024)}, u32[]{:S(2)}) copy-start(f32[1152]{0:T(1024)} %refs_4_.4) | copy-start | bytes 13828
  29.9 10.7 %copy-start = (bf16[288,3,576]{2,0,1:T(8,128)(2,1)S(1)}, bf16[288,3,576]{2,0,1:T(8,128)(2,1)}, u32[]{:S(2)}) copy-start(bf16[288,3,576]{2,0,1:T(8,128)(2,1)} %param.12) | copy-start | bytes 2985988
  29.9 23.2 %copy-start.3 = (bf16[288,576]{1,0:T(8,128)(2,1)S(1)}, bf16[288,576]{1,0:T(8,128)(2,1)}, u32[]{:S(2)}) copy-start(bf16[288,576]{1,0:T(8,128)(2,1)} %refs_4_.5) | copy-start | bytes 995332
  36.1 4.8 %collective-permute-start.3 = (bf16[8,1728]{1,0:T(8,128)(2,1)S(1)}, bf16[8,1728]{1,0:T(8,128)(2,1)S(1)}, u32[]{:S(2)}, u32[]{:S(2)}) collective-permute-start(bf16[8,1728]{1,0:T(8,128)(2,1)S(1)} %get-tuple-element.23), channel_id=1, source_target_pairs={{0,4},{4,0},{8,12},{12,8},{1,5},{5,1},{9,13},{13,9},{2,6},{6,2},{1... | collective-permute-start | bytes 82952 | tf_op jit(solution)/shard_map/ppermute | solution.py:137
  36.2 4.9 %collective-permute-start.4 = (bf16[8,1728]{1,0:T(8,128)(2,1)S(1)}, bf16[8,1728]{1,0:T(8,128)(2,1)S(1)}, u32[]{:S(2)}, u32[]{:S(2)}) collective-permute-start(bf16[8,1728]{1,0:T(8,128)(2,1)S(1)} %get-tuple-element.24), channel_id=1, source_target_pairs={{0,8},{4,12},{8,0},{12,4},{1,9},{5,13},{9,1},{13,5},{2,10},{6,14},... | collective-permute-start | bytes 82952 | tf_op jit(solution)/shard_map/ppermute | solution.py:137
  36.8 6.4 %collective-permute-start.5 = (bf16[8,1728]{1,0:T(8,128)(2,1)S(1)}, bf16[8,1728]{1,0:T(8,128)(2,1)S(1)}, u32[]{:S(2)}, u32[]{:S(2)}) collective-permute-start(bf16[8,1728]{1,0:T(8,128)(2,1)S(1)} %get-tuple-element.25), channel_id=1, source_target_pairs={{0,12},{4,8},{8,4},{12,0},{1,13},{5,9},{9,5},{13,1},{2,14},{6,10},... | collective-permute-start | bytes 82952 | tf_op jit(solution)/shard_map/ppermute | solution.py:137
  40.9 22.1 %copy-start.2 = (bf16[288,576]{1,0:T(8,128)(2,1)S(1)}, bf16[288,576]{1,0:T(8,128)(2,1)}, u32[]{:S(2)}) copy-start(bf16[288,576]{1,0:T(8,128)(2,1)} %own.1) | copy-start | bytes 995332
  43.7 4.4 %collective-permute-start.6 = (bf16[16,576]{1,0:T(8,128)(2,1)S(1)}, bf16[16,576]{1,0:T(8,128)(2,1)S(1)}, u32[]{:S(2)}, u32[]{:S(2)}) collective-permute-start(bf16[16,576]{1,0:T(8,128)(2,1)S(1)} %shard_map.76.refs_0_.refs_4_), channel_id=1, source_target_pairs={{0,4},{4,0},{8,12},{12,8},{1,5},{5,1},{9,13},{13,9},{2,6},{6,2},{1... | collective-permute-start | bytes 55304 | tf_op jit(solution)/shard_map/ppermute | solution.py:137
  43.7 5.6 %collective-permute-start.7 = (bf16[16,576]{1,0:T(8,128)(2,1)S(1)}, bf16[16,576]{1,0:T(8,128)(2,1)S(1)}, u32[]{:S(2)}, u32[]{:S(2)}) collective-permute-start(bf16[16,576]{1,0:T(8,128)(2,1)S(1)} %shard_map.76.refs_0_.refs_4_), channel_id=1, source_target_pairs={{0,8},{4,12},{8,0},{12,4},{1,9},{5,13},{9,1},{13,5},{2,10},{6,14},... | collective-permute-start | bytes 55304 | tf_op jit(solution)/shard_map/ppermute | solution.py:137
  47.5 5.6 %collective-permute-start.8 = (bf16[16,576]{1,0:T(8,128)(2,1)S(1)}, bf16[16,576]{1,0:T(8,128)(2,1)S(1)}, u32[]{:S(2)}, u32[]{:S(2)}) collective-permute-start(bf16[16,576]{1,0:T(8,128)(2,1)S(1)} %shard_map.76.refs_0_.refs_4_), channel_id=1, source_target_pairs={{0,12},{4,8},{8,4},{12,0},{1,13},{5,9},{9,5},{13,1},{2,14},{6,10},... | collective-permute-start | bytes 55304 | tf_op jit(solution)/shard_map/ppermute | solution.py:137
  53.4 4.7 %collective-permute-start.10 = (bf16[32,288]{1,0:T(8,128)(2,1)S(1)}, bf16[32,288]{1,0:T(8,128)(2,1)S(1)}, u32[]{:S(2)}, u32[]{:S(2)}) collective-permute-start(bf16[32,288]{1,0:T(8,128)(2,1)S(1)} %get-tuple-element.29), channel_id=1, source_target_pairs={{0,2},{2,0},{1,3},{3,1},{4,6},{6,4},{5,7},{7,5},{8,10},{10,8},{9,1... | collective-permute-start | bytes 55304 | tf_op jit(solution)/shard_map/ppermute | solution.py:421
  55.0 1.2 %collective-permute-start.9 = (bf16[16,288]{1,0:T(8,128)(2,1)S(1)}, bf16[16,288]{1,0:T(8,128)(2,1)S(1)}, u32[]{:S(2)}, u32[]{:S(2)}) collective-permute-start(bf16[16,288]{1,0:T(8,128)(2,1)S(1)} %get-tuple-element.28.refs_0_), channel_id=1, source_target_pairs={{0,1},{1,0},{2,3},{3,2},{4,5},{5,4},{6,7},{7,6},{8,9},{9,8},{10,11... | collective-permute-start | bytes 27656 | tf_op jit(solution)/shard_map/ppermute | solution.py:420
  55.0 3.1 %collective-permute-start.11 = (bf16[16,288]{1,0:T(8,128)(2,1)S(1)}, bf16[16,288]{1,0:T(8,128)(2,1)S(1)}, u32[]{:S(2)}, u32[]{:S(2)}) collective-permute-start(bf16[16,288]{1,0:T(8,128)(2,1)S(1)} %get-tuple-element.30), channel_id=1, source_target_pairs={{0,3},{1,2},{2,1},{3,0},{4,7},{5,6},{6,5},{7,4},{8,11},{9,10},{10,... | collective-permute-start | bytes 27656 | tf_op jit(solution)/shard_map/ppermute | solution.py:422
  58.6 4.6 %collective-permute-start.12 = (bf16[8,2048]{1,0:T(8,128)(2,1)S(1)}, bf16[8,2048]{1,0:T(8,128)(2,1)S(1)}, u32[]{:S(2)}, u32[]{:S(2)}) collective-permute-start(bf16[8,2048]{1,0:T(8,128)(2,1)S(1)} %get-tuple-element.34), channel_id=1, source_target_pairs={{0,4},{4,0},{8,12},{12,8},{1,5},{5,1},{9,13},{13,9},{2,6},{6,2},{1... | collective-permute-start | bytes 98312 | tf_op jit(solution)/shard_map/ppermute | solution.py:137
  58.6 5.1 %collective-permute-start.13 = (bf16[8,2048]{1,0:T(8,128)(2,1)S(1)}, bf16[8,2048]{1,0:T(8,128)(2,1)S(1)}, u32[]{:S(2)}, u32[]{:S(2)}) collective-permute-start(bf16[8,2048]{1,0:T(8,128)(2,1)S(1)} %get-tuple-element.35), channel_id=1, source_target_pairs={{0,8},{4,12},{8,0},{12,4},{1,9},{5,13},{9,1},{13,5},{2,10},{6,14},... | collective-permute-start | bytes 98312 | tf_op jit(solution)/shard_map/ppermute | solution.py:137
  59.7 5.7 %collective-permute-start.14 = (bf16[8,2048]{1,0:T(8,128)(2,1)S(1)}, bf16[8,2048]{1,0:T(8,128)(2,1)S(1)}, u32[]{:S(2)}, u32[]{:S(2)}) collective-permute-start(bf16[8,2048]{1,0:T(8,128)(2,1)S(1)} %get-tuple-element.36), channel_id=1, source_target_pairs={{0,12},{4,8},{8,4},{12,0},{1,13},{5,9},{9,5},{13,1},{2,14},{6,10},... | collective-permute-start | bytes 98312 | tf_op jit(solution)/shard_map/ppermute | solution.py:137
  66.6 1.2 %collective-permute-start.20 = (bf16[8,1152]{1,0:T(8,128)(2,1)S(1)}, bf16[8,1152]{1,0:T(8,128)(2,1)S(1)}, u32[]{:S(2)}, u32[]{:S(2)}) collective-permute-start(bf16[8,1152]{1,0:T(8,128)(2,1)S(1)} %get-tuple-element.37.own), channel_id=1, source_target_pairs={{0,1},{1,0},{2,3},{3,2},{4,5},{5,4},{6,7},{7,6},{8,9},{9,8},{10,11... | collective-permute-start | bytes 55304 | tf_op jit(solution)/shard_map/ppermute | solution.py:444

commit v6 on v5

--- a/solution.py
+++ b/solution.py
@@ -378,14 +378,16 @@
         scratch=[((count, plane, share), F32), ((plane, KINDS * columns), F32)],
     )
     partial_time = exchange(partial_time)
-    near, order = piece, [0]
+    near, order, sides = piece, [0], []
     for stage in range(count.bit_length() - 1):
         hop = count >> (stage + 1)
         pairs = [(i, i ^ hop) for i in range(count)]
-        near = jnp.concatenate([near, lax.ppermute(near, "frame", pairs)], axis=0)
+        arrived = lax.ppermute(near, "frame", pairs)
+        near = jnp.concatenate([near, arrived], axis=0)
+        sides.append(lax.ppermute(arrived, "patch", swap))
         order += [k ^ hop for k in order]
     near = near[share // 4 :]
-    side = lax.ppermute(near, "patch", swap)
+    side = jnp.concatenate(sides, axis=0)
     far = []
     for value in (near, side):
         far.append(lax.ppermute(value, "groups", swap))

time: 68.5 us -> 66.6 us (0.972)
  waiting for transfers between devices: 32 us -> 29.1 us
  starting transfers between devices: 30.9 us -> 31.8 us
    ppermute x3 -> x4, waiting for transfers between devices: 13.2 us -> 10.3 us  [the longest x2 7.95 us: moving_tokens(): arrived = lax.ppermute(near, 'frame', pairs)]
    ppermute x3 -> x4, starting transfers between devices: 6.54 us -> 7.97 us  [the longest x2 4.91 us: moving_tokens(): arrived = lax.ppermute(near, 'frame', pairs)]
    ppermute x12, starting transfers between devices: 19.2 us -> 18.4 us  [exchange(): found.append(lax.ppermute(messages[k], 'frame', pairs))]
  transfers between devices with their start and end apart: 21 -> 22, of which waited for: 14 -> 14; matrix products, arithmetic and copies ran while one was open for 0% -> 0% of each run, Pallas kernels for 4% -> 4%
where the time goes in v6:
time: 66.6 us; the launch traced here: 66.4 us
  starting transfers between devices  31.8 us (48%)
  waiting for transfers between devices  29.1 us (44%)
  Pallas kernels  4.24 us (6%)
  local copies, waits for them, and re-layouts  1.09 us (2%)
    ppermute x12, starting transfers between devices, exchange(): found.append(lax.ppermute(messages[k], 'frame', pairs))  18.4 us
    ppermute x12, waiting for transfers between devices, exchange(): found.append(lax.ppermute(messages[k], 'frame', pairs))  15.1 us
    ppermute x2, waiting for transfers between devices, moving_tokens(): arrived = lax.ppermute(near, 'frame', pairs)  7.95 us
    ppermute x2, starting transfers between devices, moving_tokens(): arrived = lax.ppermute(near, 'frame', pairs)  4.91 us
    pallas_call x9, Pallas kernels, run(): pl.pallas_call(body, out_shape=shapes, in_specs=[pl.BlockSpec(memory_spac...  4.24 us
    ppermute x2, starting transfers between devices, moving_tokens(): far.append(lax.ppermute(value, 'groups', swap))  3.24 us
    ppermute x2, starting transfers between devices, moving_tokens(): sides.append(lax.ppermute(arrived, 'patch', swap))  3.06 us
    ppermute x2, waiting for transfers between devices, moving_tokens(): sides.append(lax.ppermute(arrived, 'patch', swap))  2.34 us
  transfers between devices with their start and end apart: 22, of which 14 were waited for; matrix products, arithmetic and copies ran while one was open for 0% of the time, Pallas kernels for 4%

profile of v6, /device:TPU:0, one launch (start us, length us, event | category | flops | bytes accessed | tf_op | source)
XLA Modules:
  0.0 66.4 jit_solution(17047625592858644904)
XLA Ops:
  0.0 0.0 copy-start.4
  0.0 1.0 %constant_dynamic-slice_fusion = bf16[72,576]{1,0:T(8,128)(2,1)S(1)} fusion(bf16[288,576]{1,0:T(8,128)(2,1)} %own.1, s32[]{:T(128)S(6)} %select_n.3), kind=kLoop, calls=%fused_computation.5 | loop fusion | bytes 165892 | tf_op jit(solution)/shard_map/dynamic_slice | solution.py:370
  1.0 4.1 %collective-permute-start.15 = (bf16[72,576]{1,0:T(8,128)(2,1)S(1)}, bf16[72,576]{1,0:T(8,128)(2,1)S(1)}, u32[]{:S(2)}, u32[]{:S(2)}) collective-permute-start(bf16[72,576]{1,0:T(8,128)(2,1)S(1)} %constant_dynamic-slice_fusion), channel_id=1, source_target_pairs={{0,8},{4,12},{8,0},{12,4},{1,9},{5,13},{9,1},{13,5},{2,10},{6,14},... | collective-permute-start | bytes 248840 | tf_op jit(solution)/shard_map/ppermute | solution.py:385
  5.1 4.6 %collective-permute-done.15 = bf16[72,576]{1,0:T(8,128)(2,1)S(1)} collective-permute-done((bf16[72,576]{1,0:T(8,128)(2,1)S(1)}, bf16[72,576]{1,0:T(8,128)(2,1)S(1)}, u32[]{:S(2)}, u32[]{:S(2)}) %collective-permute-start.15) | collective-permute-done | bytes 82976 | tf_op jit(solution)/shard_map/ppermute | solution.py:385
  9.8 0.8 %collective-permute-start.16 = (bf16[144,576]{1,0:T(8,128)(2,1)S(1)}, bf16[144,576]{1,0:T(8,128)(2,1)S(1)}, u32[]{:S(2)}, u32[]{:S(2)}) collective-permute-start(bf16[144,576]{1,0:T(8,128)(2,1)S(1)} %pad_maximum_fusion), channel_id=1, source_target_pairs={{0,4},{4,0},{8,12},{12,8},{1,5},{5,1},{9,13},{13,9},{2,6},{6,2},{1... | collective-permute-start | bytes 497672 | tf_op jit(solution)/shard_map/ppermute | solution.py:385
  10.6 1.5 %collective-permute-start.17 = (bf16[72,576]{1,0:T(8,128)(2,1)S(1)}, bf16[72,576]{1,0:T(8,128)(2,1)S(1)}, u32[]{:S(2)}, u32[]{:S(2)}) collective-permute-start(bf16[72,576]{1,0:T(8,128)(2,1)S(1)} %collective-permute-done.15), channel_id=1, source_target_pairs={{0,2},{2,0},{1,3},{3,1},{4,6},{6,4},{5,7},{7,5},{8,10},{10,8},{9,1... | collective-permute-start | bytes 248840 | tf_op jit(solution)/shard_map/ppermute | solution.py:387
  12.1 3.3 %collective-permute-done.16 = bf16[144,576]{1,0:T(8,128)(2,1)S(1)} collective-permute-done((bf16[144,576]{1,0:T(8,128)(2,1)S(1)}, bf16[144,576]{1,0:T(8,128)(2,1)S(1)}, u32[]{:S(2)}, u32[]{:S(2)}) %collective-permute-start.16) | collective-permute-done | bytes 165920 | tf_op jit(solution)/shard_map/ppermute | solution.py:385
  15.4 1.6 %collective-permute-start.18 = (bf16[144,576]{1,0:T(8,128)(2,1)S(1)}, bf16[144,576]{1,0:T(8,128)(2,1)S(1)}, u32[]{:S(2)}, u32[]{:S(2)}) collective-permute-start(bf16[144,576]{1,0:T(8,128)(2,1)S(1)} %collective-permute-done.16), channel_id=1, source_target_pairs={{0,2},{2,0},{1,3},{3,1},{4,6},{6,4},{5,7},{7,5},{8,10},{10,8},{9,1... | collective-permute-start | bytes 497672 | tf_op jit(solution)/shard_map/ppermute | solution.py:387
  17.0 0.0 collective-permute-done.17
  17.0 1.6 %collective-permute-start.19 = (bf16[216,576]{1,0:T(8,128)(2,1)S(1)}, bf16[216,576]{1,0:T(8,128)(2,1)S(1)}, u32[]{:S(2)}, u32[]{:S(2)}) collective-permute-start(bf16[216,576]{1,0:T(8,128)(2,1)S(1)} %constant_dynamic-update-slice_fusion.near), channel_id=1, source_target_pairs={{0,16},{16,0},{1,17},{17,1},{2,18},{18,2},{3,19},{19,3},{4,20},{20... | collective-permute-start | bytes 746504 | tf_op jit(solution)/shard_map/ppermute | solution.py:393
  18.6 2.3 %collective-permute-done.18 = bf16[144,576]{1,0:T(8,128)(2,1)S(1)} collective-permute-done((bf16[144,576]{1,0:T(8,128)(2,1)S(1)}, bf16[144,576]{1,0:T(8,128)(2,1)S(1)}, u32[]{:S(2)}, u32[]{:S(2)}) %collective-permute-start.18) | collective-permute-done | bytes 165920 | tf_op jit(solution)/shard_map/ppermute | solution.py:387
  21.0 1.7 %collective-permute-start.20 = (bf16[216,576]{1,0:T(8,128)(2,1)S(1)}, bf16[216,576]{1,0:T(8,128)(2,1)S(1)}, u32[]{:S(2)}, u32[]{:S(2)}) collective-permute-start(bf16[216,576]{1,0:T(8,128)(2,1)S(1)} %constant_dynamic-update-slice_fusion.2.side), channel_id=1, source_target_pairs={{0,16},{16,0},{1,17},{17,1},{2,18},{18,2},{3,19},{19,3},{4,20},{20... | collective-permute-start | bytes 746504 | tf_op jit(solution)/shard_map/ppermute | solution.py:393
  22.6 0.0 copy-done.4
  22.6 1.7 %collective-permute-start = (bf16[2,4,1152]{2,1,0:T(4,128)(2,1)S(1)}, bf16[2,4,1152]{2,1,0:T(4,128)(2,1)S(1)}, u32[]{:S(2)}, u32[]{:S(2)}) collective-permute-start(bf16[2,4,1152]{2,1,0:T(4,128)(2,1)S(1)} %copy-done.4), channel_id=1, source_target_pairs={{0,4},{4,0},{8,12},{12,8},{1,5},{5,1},{9,13},{13,9},{2,6},{6,2},{1... | collective-permute-start | bytes 55304 | tf_op jit(solution)/shard_map/ppermute | solution.py:137
  24.4 3.4 %collective-permute-start.1 = (bf16[2,4,1152]{2,1,0:T(4,128)(2,1)S(1)}, bf16[2,4,1152]{2,1,0:T(4,128)(2,1)S(1)}, u32[]{:S(2)}, u32[]{:S(2)}) collective-permute-start(bf16[2,4,1152]{2,1,0:T(4,128)(2,1)S(1)} %copy-done.4), channel_id=1, source_target_pairs={{0,8},{4,12},{8,0},{12,4},{1,9},{5,13},{9,1},{13,5},{2,10},{6,14},... | collective-permute-start | bytes 55304 | tf_op jit(solution)/shard_map/ppermute | solution.py:137
  27.7 0.0 collective-permute-start.2
  27.7 0.0 copy-done.1
  27.7 0.2 shard_map.73.refs_5_
  27.9 0.0 copy-start
  27.9 0.0 copy-start.3
  27.9 0.0 collective-permute-done.refs_1_
  27.9 1.5 %collective-permute-done.1.refs_2_ = bf16[2,4,1152]{2,1,0:T(4,128)(2,1)S(1)} collective-permute-done((bf16[2,4,1152]{2,1,0:T(4,128)(2,1)S(1)}, bf16[2,4,1152]{2,1,0:T(4,128)(2,1)S(1)}, u32[]{:S(2)}, u32[]{:S(2)}) %collective-permute-start.1) | collective-permute-done | bytes 18464 | tf_op jit(solution)/shard_map/ppermute | solution.py:137
  29.5 3.9 %collective-permute-done.2.refs_3_ = bf16[2,4,1152]{2,1,0:T(4,128)(2,1)S(1)} collective-permute-done((bf16[2,4,1152]{2,1,0:T(4,128)(2,1)S(1)}, bf16[2,4,1152]{2,1,0:T(4,128)(2,1)S(1)}, u32[]{:S(2)}, u32[]{:S(2)}) %collective-permute-start.2) | collective-permute-done | bytes 18464 | tf_op jit(solution)/shard_map/ppermute | solution.py:137
  33.4 0.0 copy-done.5
  33.4 0.7 %shard_map.74 = (bf16[8,1728]{1,0:T(8,128)(2,1)S(1)}, bf16[8,1728]{1,0:T(8,128)(2,1)S(1)}, bf16[8,1728]{1,0:T(8,128)(2,1)S(1)}, bf16[8,1728]{1,0:T(8,128)(2,1)S(1)}) custom-call(bf16[2,4,1152]{2,1,0:T(4,128)(2,1)S(1)} %copy-done.4, bf16[2,4,1152]{2,1,0:T(4,128)(2,1)S(1)} %collective-permute-done.refs_1_, ...), custom_call_target="tpu_custom_call" | custom-call | tf_op jit(solution)/shard_map/pallas_call | solution.py:116
  34.1 0.1 collective-permute-start.3
  34.2 0.7 collective-permute-start.4
  34.9 3.7 %collective-permute-start.5 = (bf16[8,1728]{1,0:T(8,128)(2,1)S(1)}, bf16[8,1728]{1,0:T(8,128)(2,1)S(1)}, u32[]{:S(2)}, u32[]{:S(2)}) collective-permute-start(bf16[8,1728]{1,0:T(8,128)(2,1)S(1)} %get-tuple-element.25), channel_id=1, source_target_pairs={{0,12},{4,8},{8,4},{12,0},{1,13},{5,9},{9,5},{13,1},{2,14},{6,10},... | collective-permute-start | bytes 82952 | tf_op jit(solution)/shard_map/ppermute | solution.py:137
  38.6 0.0 copy-done.6
  38.6 0.0 copy-done
  38.6 0.3 shard_map.75
  38.9 0.0 collective-permute-done.3.refs_1_
  38.9 0.2 collective-permute-done.4.refs_2_
  39.2 2.1 %collective-permute-done.5.refs_3_ = bf16[8,1728]{1,0:T(8,128)(2,1)S(1)} collective-permute-done((bf16[8,1728]{1,0:T(8,128)(2,1)S(1)}, bf16[8,1728]{1,0:T(8,128)(2,1)S(1)}, u32[]{:S(2)}, u32[]{:S(2)}) %collective-permute-start.5) | collective-permute-done | bytes 27680 | tf_op jit(solution)/shard_map/ppermute | solution.py:137
  41.3 0.4 shard_map.76.refs_0_.refs_4_
  41.7 0.1 collective-permute-start.6
  41.8 3.8 %collective-permute-start.7 = (bf16[16,576]{1,0:T(8,128)(2,1)S(1)}, bf16[16,576]{1,0:T(8,128)(2,1)S(1)}, u32[]{:S(2)}, u32[]{:S(2)}) collective-permute-start(bf16[16,576]{1,0:T(8,128)(2,1)S(1)} %shard_map.76.refs_0_.refs_4_), channel_id=1, source_target_pairs={{0,8},{4,12},{8,0},{12,4},{1,9},{5,13},{9,1},{13,5},{2,10},{6,14},... | collective-permute-start | bytes 55304 | tf_op jit(solution)/shard_map/ppermute | solution.py:137
  45.6 0.6 collective-permute-start.8
  46.1 0.0 collective-permute-done.6.refs_1_.refs_5_
  46.1 1.2 %collective-permute-done.7.refs_2_.refs_6_ = bf16[16,576]{1,0:T(8,128)(2,1)S(1)} collective-permute-done((bf16[16,576]{1,0:T(8,128)(2,1)S(1)}, bf16[16,576]{1,0:T(8,128)(2,1)S(1)}, u32[]{:S(2)}, u32[]{:S(2)}) %collective-permute-start.7) | collective-permute-done | bytes 18464 | tf_op jit(solution)/shard_map/ppermute | solution.py:137
  47.3 3.8 %collective-permute-done.8.refs_3_.refs_7_ = bf16[16,576]{1,0:T(8,128)(2,1)S(1)} collective-permute-done((bf16[16,576]{1,0:T(8,128)(2,1)S(1)}, bf16[16,576]{1,0:T(8,128)(2,1)S(1)}, u32[]{:S(2)}, u32[]{:S(2)}) %collective-permute-start.8) | collective-permute-done | bytes 18464 | tf_op jit(solution)/shard_map/ppermute | solution.py:137
  51.1 0.0 copy-done.3
  51.1 0.3 shard_map.77
  51.4 1.6 %collective-permute-start.10 = (bf16[32,288]{1,0:T(8,128)(2,1)S(1)}, bf16[32,288]{1,0:T(8,128)(2,1)S(1)}, u32[]{:S(2)}, u32[]{:S(2)}) collective-permute-start(bf16[32,288]{1,0:T(8,128)(2,1)S(1)} %get-tuple-element.29), channel_id=1, source_target_pairs={{0,2},{2,0},{1,3},{3,1},{4,6},{6,4},{5,7},{7,5},{8,10},{10,8},{9,1... | collective-permute-start | bytes 55304 | tf_op jit(solution)/shard_map/ppermute | solution.py:423
  53.0 0.0 collective-permute-start.9
  53.0 0.6 collective-permute-start.11
  53.7 0.5 collective-permute-done.9.refs_1_
  54.2 1.9 %collective-permute-done.11.refs_3_ = bf16[16,288]{1,0:T(8,128)(2,1)S(1)} collective-permute-done((bf16[16,288]{1,0:T(8,128)(2,1)S(1)}, bf16[16,288]{1,0:T(8,128)(2,1)S(1)}, u32[]{:S(2)}, u32[]{:S(2)}) %collective-permute-start.11) | collective-permute-done | bytes 9248 | tf_op jit(solution)/shard_map/ppermute | solution.py:424
  56.1 0.0 collective-permute-done.10.refs_2_
  56.1 0.4 shard_map.78
  56.6 0.1 collective-permute-start.12
  56.6 1.1 %collective-permute-start.13 = (bf16[8,2048]{1,0:T(8,128)(2,1)S(1)}, bf16[8,2048]{1,0:T(8,128)(2,1)S(1)}, u32[]{:S(2)}, u32[]{:S(2)}) collective-permute-start(bf16[8,2048]{1,0:T(8,128)(2,1)S(1)} %get-tuple-element.35), channel_id=1, source_target_pairs={{0,8},{4,12},{8,0},{12,4},{1,9},{5,13},{9,1},{13,5},{2,10},{6,14},... | collective-permute-start | bytes 98312 | tf_op jit(solution)/shard_map/ppermute | solution.py:137
  57.8 3.3 %collective-permute-start.14 = (bf16[8,2048]{1,0:T(8,128)(2,1)S(1)}, bf16[8,2048]{1,0:T(8,128)(2,1)S(1)}, u32[]{:S(2)}, u32[]{:S(2)}) collective-permute-start(bf16[8,2048]{1,0:T(8,128)(2,1)S(1)} %get-tuple-element.36), channel_id=1, source_target_pairs={{0,12},{4,8},{8,4},{12,0},{1,13},{5,9},{9,5},{13,1},{2,14},{6,10},... | collective-permute-start | bytes 98312 | tf_op jit(solution)/shard_map/ppermute | solution.py:137
  61.0 0.0 collective-permute-done.19.far
  61.0 0.0 collective-permute-done.20.last
  61.0 0.0 copy-done.2
  61.0 0.1 shard_map.79.refs_8_
  61.2 0.0 collective-permute-done.12.refs_1_
  61.2 0.6 collective-permute-done.13.refs_2_
  61.8 1.7 %collective-permute-done.14.refs_3_ = bf16[8,2048]{1,0:T(8,128)(2,1)S(1)} collective-permute-done((bf16[8,2048]{1,0:T(8,128)(2,1)S(1)}, bf16[8,2048]{1,0:T(8,128)(2,1)S(1)}, u32[]{:S(2)}, u32[]{:S(2)}) %collective-permute-start.14) | collective-permute-done | bytes 32800 | tf_op jit(solution)/shard_map/ppermute | solution.py:137
  63.5 1.1 %shard_map.80 = (bf16[8,1152]{1,0:T(8,128)(2,1)S(1)}, bf16[8,1152]{1,0:T(8,128)(2,1)S(1)}) custom-call(bf16[8,2048]{1,0:T(8,128)(2,1)S(1)} %get-tuple-element.33.refs_0_, bf16[8,2048]{1,0:T(8,128)(2,1)S(1)} %collective-permute-done.12.refs_1_, bf16[8,2048]{1,0:T(8,128)(2,1)S(1)} %collective-permute-done.13.refs_2_, ...), custom_call_target="tpu_custom_call" | custom-call | tf_op jit(solution)/shard_map/pallas_call | solution.py:116
  64.6 0.0 collective-permute-start.21
  64.6 1.2 %collective-permute-done.21.other = bf16[8,1152]{1,0:T(8,128)(2,1)S(1)} collective-permute-done((bf16[8,1152]{1,0:T(8,128)(2,1)S(1)}, bf16[8,1152]{1,0:T(8,128)(2,1)S(1)}, u32[]{:S(2)}, u32[]{:S(2)}) %collective-permute-start.21) | collective-permute-done | bytes 18464 | tf_op jit(solution)/shard_map/ppermute | solution.py:446
  65.8 0.6 shard_map.81
  (9 shorter events, 0.1 us)
Async XLA Ops:
  0.0 22.6 %copy-start.4 = (bf16[2,4,1152]{2,1,0:T(4,128)(2,1)S(1)}, bf16[2,4,1152]{2,1,0:T(4,128)(2,1)}, u32[]{:S(2)}) copy-start(bf16[2,4,1152]{2,1,0:T(4,128)(2,1)} %refs_0_.3) | copy-start | bytes 55300
  0.0 27.7 %copy-start.1 = (bf16[288,3,576]{2,0,1:T(8,128)(2,1)S(1)}, bf16[288,3,576]{2,0,1:T(8,128)(2,1)}, u32[]{:S(2)}) copy-start(bf16[288,3,576]{2,0,1:T(8,128)(2,1)} %param.9) | copy-start | bytes 2985988
  1.0 8.8 %collective-permute-start.15 = (bf16[72,576]{1,0:T(8,128)(2,1)S(1)}, bf16[72,576]{1,0:T(8,128)(2,1)S(1)}, u32[]{:S(2)}, u32[]{:S(2)}) collective-permute-start(bf16[72,576]{1,0:T(8,128)(2,1)S(1)} %constant_dynamic-slice_fusion), channel_id=1, source_target_pairs={{0,8},{4,12},{8,0},{12,4},{1,9},{5,13},{9,1},{13,5},{2,10},{6,14},... | collective-permute-start | bytes 248840 | tf_op jit(solution)/shard_map/ppermute | solution.py:385
  9.8 5.6 %collective-permute-start.16 = (bf16[144,576]{1,0:T(8,128)(2,1)S(1)}, bf16[144,576]{1,0:T(8,128)(2,1)S(1)}, u32[]{:S(2)}, u32[]{:S(2)}) collective-permute-start(bf16[144,576]{1,0:T(8,128)(2,1)S(1)} %pad_maximum_fusion), channel_id=1, source_target_pairs={{0,4},{4,0},{8,12},{12,8},{1,5},{5,1},{9,13},{13,9},{2,6},{6,2},{1... | collective-permute-start | bytes 497672 | tf_op jit(solution)/shard_map/ppermute | solution.py:385
  10.6 6.4 %collective-permute-start.17 = (bf16[72,576]{1,0:T(8,128)(2,1)S(1)}, bf16[72,576]{1,0:T(8,128)(2,1)S(1)}, u32[]{:S(2)}, u32[]{:S(2)}) collective-permute-start(bf16[72,576]{1,0:T(8,128)(2,1)S(1)} %collective-permute-done.15), channel_id=1, source_target_pairs={{0,2},{2,0},{1,3},{3,1},{4,6},{6,4},{5,7},{7,5},{8,10},{10,8},{9,1... | collective-permute-start | bytes 248840 | tf_op jit(solution)/shard_map/ppermute | solution.py:387
  15.4 5.5 %collective-permute-start.18 = (bf16[144,576]{1,0:T(8,128)(2,1)S(1)}, bf16[144,576]{1,0:T(8,128)(2,1)S(1)}, u32[]{:S(2)}, u32[]{:S(2)}) collective-permute-start(bf16[144,576]{1,0:T(8,128)(2,1)S(1)} %collective-permute-done.16), channel_id=1, source_target_pairs={{0,2},{2,0},{1,3},{3,1},{4,6},{6,4},{5,7},{7,5},{8,10},{10,8},{9,1... | collective-permute-start | bytes 497672 | tf_op jit(solution)/shard_map/ppermute | solution.py:387
  17.0 44.0 %collective-permute-start.19 = (bf16[216,576]{1,0:T(8,128)(2,1)S(1)}, bf16[216,576]{1,0:T(8,128)(2,1)S(1)}, u32[]{:S(2)}, u32[]{:S(2)}) collective-permute-start(bf16[216,576]{1,0:T(8,128)(2,1)S(1)} %constant_dynamic-update-slice_fusion.near), channel_id=1, source_target_pairs={{0,16},{16,0},{1,17},{17,1},{2,18},{18,2},{3,19},{19,3},{4,20},{20... | collective-permute-start | bytes 746504 | tf_op jit(solution)/shard_map/ppermute | solution.py:393
  21.0 40.1 %collective-permute-start.20 = (bf16[216,576]{1,0:T(8,128)(2,1)S(1)}, bf16[216,576]{1,0:T(8,128)(2,1)S(1)}, u32[]{:S(2)}, u32[]{:S(2)}) collective-permute-start(bf16[216,576]{1,0:T(8,128)(2,1)S(1)} %constant_dynamic-update-slice_fusion.2.side), channel_id=1, source_target_pairs={{0,16},{16,0},{1,17},{17,1},{2,18},{18,2},{3,19},{19,3},{4,20},{20... | collective-permute-start | bytes 746504 | tf_op jit(solution)/shard_map/ppermute | solution.py:393
  22.6 5.3 %collective-permute-start = (bf16[2,4,1152]{2,1,0:T(4,128)(2,1)S(1)}, bf16[2,4,1152]{2,1,0:T(4,128)(2,1)S(1)}, u32[]{:S(2)}, u32[]{:S(2)}) collective-permute-start(bf16[2,4,1152]{2,1,0:T(4,128)(2,1)S(1)} %copy-done.4), channel_id=1, source_target_pairs={{0,4},{4,0},{8,12},{12,8},{1,5},{5,1},{9,13},{13,9},{2,6},{6,2},{1... | collective-permute-start | bytes 55304 | tf_op jit(solution)/shard_map/ppermute | solution.py:137
  24.4 5.1 %collective-permute-start.1 = (bf16[2,4,1152]{2,1,0:T(4,128)(2,1)S(1)}, bf16[2,4,1152]{2,1,0:T(4,128)(2,1)S(1)}, u32[]{:S(2)}, u32[]{:S(2)}) collective-permute-start(bf16[2,4,1152]{2,1,0:T(4,128)(2,1)S(1)} %copy-done.4), channel_id=1, source_target_pairs={{0,8},{4,12},{8,0},{12,4},{1,9},{5,13},{9,1},{13,5},{2,10},{6,14},... | collective-permute-start | bytes 55304 | tf_op jit(solution)/shard_map/ppermute | solution.py:137
  27.7 5.7 %collective-permute-start.2 = (bf16[2,4,1152]{2,1,0:T(4,128)(2,1)S(1)}, bf16[2,4,1152]{2,1,0:T(4,128)(2,1)S(1)}, u32[]{:S(2)}, u32[]{:S(2)}) collective-permute-start(bf16[2,4,1152]{2,1,0:T(4,128)(2,1)S(1)} %copy-done.4), channel_id=1, source_target_pairs={{0,12},{4,8},{8,4},{12,0},{1,13},{5,9},{9,5},{13,1},{2,14},{6,10},... | collective-permute-start | bytes 55304 | tf_op jit(solution)/shard_map/ppermute | solution.py:137
  27.7 5.7 %copy-start.5 = (f32[1152]{0:T(1024)S(1)}, f32[1152]{0:T(1024)}, u32[]{:S(2)}) copy-start(f32[1152]{0:T(1024)} %refs_4_.3) | copy-start | bytes 13828
  27.7 10.8 %copy-start.6 = (f32[1152]{0:T(1024)S(1)}, f32[1152]{0:T(1024)}, u32[]{:S(2)}) copy-start(f32[1152]{0:T(1024)} %refs_4_.4) | copy-start | bytes 13828
  27.9 10.7 %copy-start = (bf16[288,3,576]{2,0,1:T(8,128)(2,1)S(1)}, bf16[288,3,576]{2,0,1:T(8,128)(2,1)}, u32[]{:S(2)}) copy-start(bf16[288,3,576]{2,0,1:T(8,128)(2,1)} %param.12) | copy-start | bytes 2985988
  27.9 23.2 %copy-start.3 = (bf16[288,576]{1,0:T(8,128)(2,1)S(1)}, bf16[288,576]{1,0:T(8,128)(2,1)}, u32[]{:S(2)}) copy-start(bf16[288,576]{1,0:T(8,128)(2,1)} %refs_4_.5) | copy-start | bytes 995332
  34.1 4.8 %collective-permute-start.3 = (bf16[8,1728]{1,0:T(8,128)(2,1)S(1)}, bf16[8,1728]{1,0:T(8,128)(2,1)S(1)}, u32[]{:S(2)}, u32[]{:S(2)}) collective-permute-start(bf16[8,1728]{1,0:T(8,128)(2,1)S(1)} %get-tuple-element.23), channel_id=1, source_target_pairs={{0,4},{4,0},{8,12},{12,8},{1,5},{5,1},{9,13},{13,9},{2,6},{6,2},{1... | collective-permute-start | bytes 82952 | tf_op jit(solution)/shard_map/ppermute | solution.py:137
  34.2 4.9 %collective-permute-start.4 = (bf16[8,1728]{1,0:T(8,128)(2,1)S(1)}, bf16[8,1728]{1,0:T(8,128)(2,1)S(1)}, u32[]{:S(2)}, u32[]{:S(2)}) collective-permute-start(bf16[8,1728]{1,0:T(8,128)(2,1)S(1)} %get-tuple-element.24), channel_id=1, source_target_pairs={{0,8},{4,12},{8,0},{12,4},{1,9},{5,13},{9,1},{13,5},{2,10},{6,14},... | collective-permute-start | bytes 82952 | tf_op jit(solution)/shard_map/ppermute | solution.py:137
  34.9 6.4 %collective-permute-start.5 = (bf16[8,1728]{1,0:T(8,128)(2,1)S(1)}, bf16[8,1728]{1,0:T(8,128)(2,1)S(1)}, u32[]{:S(2)}, u32[]{:S(2)}) collective-permute-start(bf16[8,1728]{1,0:T(8,128)(2,1)S(1)} %get-tuple-element.25), channel_id=1, source_target_pairs={{0,12},{4,8},{8,4},{12,0},{1,13},{5,9},{9,5},{13,1},{2,14},{6,10},... | collective-permute-start | bytes 82952 | tf_op jit(solution)/shard_map/ppermute | solution.py:137
  38.9 22.1 %copy-start.2 = (bf16[288,576]{1,0:T(8,128)(2,1)S(1)}, bf16[288,576]{1,0:T(8,128)(2,1)}, u32[]{:S(2)}) copy-start(bf16[288,576]{1,0:T(8,128)(2,1)} %own.1) | copy-start | bytes 995332
  41.7 4.4 %collective-permute-start.6 = (bf16[16,576]{1,0:T(8,128)(2,1)S(1)}, bf16[16,576]{1,0:T(8,128)(2,1)S(1)}, u32[]{:S(2)}, u32[]{:S(2)}) collective-permute-start(bf16[16,576]{1,0:T(8,128)(2,1)S(1)} %shard_map.76.refs_0_.refs_4_), channel_id=1, source_target_pairs={{0,4},{4,0},{8,12},{12,8},{1,5},{5,1},{9,13},{13,9},{2,6},{6,2},{1... | collective-permute-start | bytes 55304 | tf_op jit(solution)/shard_map/ppermute | solution.py:137
  41.8 5.6 %collective-permute-start.7 = (bf16[16,576]{1,0:T(8,128)(2,1)S(1)}, bf16[16,576]{1,0:T(8,128)(2,1)S(1)}, u32[]{:S(2)}, u32[]{:S(2)}) collective-permute-start(bf16[16,576]{1,0:T(8,128)(2,1)S(1)} %shard_map.76.refs_0_.refs_4_), channel_id=1, source_target_pairs={{0,8},{4,12},{8,0},{12,4},{1,9},{5,13},{9,1},{13,5},{2,10},{6,14},... | collective-permute-start | bytes 55304 | tf_op jit(solution)/shard_map/ppermute | solution.py:137
  45.6 5.6 %collective-permute-start.8 = (bf16[16,576]{1,0:T(8,128)(2,1)S(1)}, bf16[16,576]{1,0:T(8,128)(2,1)S(1)}, u32[]{:S(2)}, u32[]{:S(2)}) collective-permute-start(bf16[16,576]{1,0:T(8,128)(2,1)S(1)} %shard_map.76.refs_0_.refs_4_), channel_id=1, source_target_pairs={{0,12},{4,8},{8,4},{12,0},{1,13},{5,9},{9,5},{13,1},{2,14},{6,10},... | collective-permute-start | bytes 55304 | tf_op jit(solution)/shard_map/ppermute | solution.py:137
  51.4 4.7 %collective-permute-start.10 = (bf16[32,288]{1,0:T(8,128)(2,1)S(1)}, bf16[32,288]{1,0:T(8,128)(2,1)S(1)}, u32[]{:S(2)}, u32[]{:S(2)}) collective-permute-start(bf16[32,288]{1,0:T(8,128)(2,1)S(1)} %get-tuple-element.29), channel_id=1, source_target_pairs={{0,2},{2,0},{1,3},{3,1},{4,6},{6,4},{5,7},{7,5},{8,10},{10,8},{9,1... | collective-permute-start | bytes 55304 | tf_op jit(solution)/shard_map/ppermute | solution.py:423
  53.0 1.2 %collective-permute-start.9 = (bf16[16,288]{1,0:T(8,128)(2,1)S(1)}, bf16[16,288]{1,0:T(8,128)(2,1)S(1)}, u32[]{:S(2)}, u32[]{:S(2)}) collective-permute-start(bf16[16,288]{1,0:T(8,128)(2,1)S(1)} %get-tuple-element.28.refs_0_), channel_id=1, source_target_pairs={{0,1},{1,0},{2,3},{3,2},{4,5},{5,4},{6,7},{7,6},{8,9},{9,8},{10,11... | collective-permute-start | bytes 27656 | tf_op jit(solution)/shard_map/ppermute | solution.py:422
  53.0 3.1 %collective-permute-start.11 = (bf16[16,288]{1,0:T(8,128)(2,1)S(1)}, bf16[16,288]{1,0:T(8,128)(2,1)S(1)}, u32[]{:S(2)}, u32[]{:S(2)}) collective-permute-start(bf16[16,288]{1,0:T(8,128)(2,1)S(1)} %get-tuple-element.30), channel_id=1, source_target_pairs={{0,3},{1,2},{2,1},{3,0},{4,7},{5,6},{6,5},{7,4},{8,11},{9,10},{10,... | collective-permute-start | bytes 27656 | tf_op jit(solution)/shard_map/ppermute | solution.py:424
  56.6 4.6 %collective-permute-start.12 = (bf16[8,2048]{1,0:T(8,128)(2,1)S(1)}, bf16[8,2048]{1,0:T(8,128)(2,1)S(1)}, u32[]{:S(2)}, u32[]{:S(2)}) collective-permute-start(bf16[8,2048]{1,0:T(8,128)(2,1)S(1)} %get-tuple-element.34), channel_id=1, source_target_pairs={{0,4},{4,0},{8,12},{12,8},{1,5},{5,1},{9,13},{13,9},{2,6},{6,2},{1... | collective-permute-start | bytes 98312 | tf_op jit(solution)/shard_map/ppermute | solution.py:137
  56.6 5.1 %collective-permute-start.13 = (bf16[8,2048]{1,0:T(8,128)(2,1)S(1)}, bf16[8,2048]{1,0:T(8,128)(2,1)S(1)}, u32[]{:S(2)}, u32[]{:S(2)}) collective-permute-start(bf16[8,2048]{1,0:T(8,128)(2,1)S(1)} %get-tuple-element.35), channel_id=1, source_target_pairs={{0,8},{4,12},{8,0},{12,4},{1,9},{5,13},{9,1},{13,5},{2,10},{6,14},... | collective-permute-start | bytes 98312 | tf_op jit(solution)/shard_map/ppermute | solution.py:137
  57.8 5.7 %collective-permute-start.14 = (bf16[8,2048]{1,0:T(8,128)(2,1)S(1)}, bf16[8,2048]{1,0:T(8,128)(2,1)S(1)}, u32[]{:S(2)}, u32[]{:S(2)}) collective-permute-start(bf16[8,2048]{1,0:T(8,128)(2,1)S(1)} %get-tuple-element.36), channel_id=1, source_target_pairs={{0,12},{4,8},{8,4},{12,0},{1,13},{5,9},{9,5},{13,1},{2,14},{6,10},... | collective-permute-start | bytes 98312 | tf_op jit(solution)/shard_map/ppermute | solution.py:137
  64.6 1.2 %collective-permute-start.21 = (bf16[8,1152]{1,0:T(8,128)(2,1)S(1)}, bf16[8,1152]{1,0:T(8,128)(2,1)S(1)}, u32[]{:S(2)}, u32[]{:S(2)}) collective-permute-start(bf16[8,1152]{1,0:T(8,128)(2,1)S(1)} %get-tuple-element.37.own), channel_id=1, source_target_pairs={{0,1},{1,0},{2,3},{3,2},{4,5},{5,4},{6,7},{7,6},{8,9},{9,8},{10,11... | collective-permute-start | bytes 55304 | tf_op jit(solution)/shard_map/ppermute | solution.py:446
